TPU v7x, 32 devices: a whole 2x2x4 slice. The times are simulated.
32 devices in a mesh: fsdp: 4 (over z), ctx: 4 (over x, core), tp: 2 (over y).
Axes of the slice: x: 2, y: 2, z: 4, core: 2. Of those that a mesh axis runs over, the one named last changes fastest.
Arguments:
- tokens: bfloat16 [4, 1536, 2048], P('fsdp', 'ctx'), may hold values from -6 to 6
- seq_ids: int32 [4, 1536], P('fsdp'), may hold values from 0 to 2, never falling along the last dimension, each value on 1 to 768 neighbouring positions
- pic_starts: int32 [4, 3], P('fsdp'), may hold values from 0 to 1408, as said below
- pic_lengths: int32 [4, 3], P('fsdp'), may hold values from 128 to 256, as said below
- skip_mask: int32 [4, 1536], P('fsdp', 'ctx'), may hold values 0 or 1
- w_query: bfloat16 [2048, 2048], P('fsdp', 'tp'), may hold values from -0.125 to 0.125
- w_key: bfloat16 [2048, 512], P('fsdp', 'tp'), may hold values from -0.125 to 0.125
- w_value: bfloat16 [2048, 512], P('fsdp', 'tp'), may hold values from -0.125 to 0.125
- w_out: bfloat16 [2048, 2048], P('tp', 'fsdp'), may hold values from -1 to 1
- w_gate: bfloat16 [2048, 5632], P('fsdp', 'tp'), may hold values from -0.125 to 0.125
- w_up: bfloat16 [2048, 5632], P('fsdp', 'tp'), may hold values from -0.125 to 0.125
- w_down: bfloat16 [5632, 2048], P('tp', 'fsdp'), may hold values from -0.078125 to 0.078125
- gain_attn: bfloat16 [2048], P('fsdp'), may hold values from 0.25 to 1.75
- gain_ffn: bfloat16 [2048], P('fsdp'), may hold values from 0.25 to 1.75
- cotangent: bfloat16 [4, 1536, 2048], P('fsdp', 'ctx'), may hold values from -6 to 6
Outputs:
- output: bfloat16 [4, 1536, 2048], P('fsdp', 'ctx')
- input_grad: bfloat16 [4, 1536, 2048], P('fsdp', 'ctx')
- grad_query: float32 [2048, 2048], P('fsdp', 'tp')
- grad_key: float32 [2048, 512], P('fsdp', 'tp')
- grad_value: float32 [2048, 512], P('fsdp', 'tp')
- grad_out: float32 [2048, 2048], P('tp', 'fsdp')
- grad_gate: float32 [2048, 5632], P('fsdp', 'tp')
- grad_up: float32 [2048, 5632], P('fsdp', 'tp')
- grad_down: float32 [5632, 2048], P('tp', 'fsdp')
- grad_gain_attn: float32 [2048], P('fsdp')
- grad_gain_ffn: float32 [2048], P('fsdp')
Inputs may be any that keep to these rules, and one draw needn't show every extreme that they name: `pic_starts`: picture p of a row (counting from 0) lies inside positions p * 2 * 256 to (p + 1) * 2 * 256 - 1, so pictures never intersect; it may start anywhere in that range where it fits. `pic_lengths`: every row has a picture of exactly 256 positions and another of exactly 128.
All inputs are finite; a program needn't handle non-finite values. No bound on the sum of `skip_mask` on one device may be relied on, other than what follows from the above.
Results may differ from a plain program's by a relative error of at most 0.022.
Values may be sent and summed in bfloat16 or wider, within the bound.
No kernel may reach another device: no remote copies, remote signals or barrier semaphores. Data moves between devices by JAX's collectives and lax.ppermute only.
A program may use at most 256 MiB of HBM per device.

v0:
```python
import math

import jax
import jax.numpy as jnp
from jax import lax
from jax.sharding import PartitionSpec as P

HEAD = 128


norm_eps = 1e-05
rope_base = 10000.0


def rotate(values_in, positions, sign):
    half_width = values_in.shape[-1] // 2
    frequency = jnp.power(
        rope_base, -jnp.arange(half_width, dtype=jnp.float32) * 2.0 / values_in.shape[-1]
    )
    angles = positions.astype(jnp.float32)[:, None] * frequency[None, :]
    cosine = jnp.cos(angles)[:, None, :]
    sine_val = sign * jnp.sin(angles)[:, None, :]
    first_half = values_in[..., :half_width]
    second = values_in[..., half_width:]
    return jnp.concatenate(
        [first_half * cosine - second * sine_val, second * cosine + first_half * sine_val], axis=-1
    )


def picture_ids(starts, lengths, positions):
    inside = (positions[:, None] >= starts[None, :]) & (
        positions[:, None] < starts[None, :] + lengths[None, :]
    )
    numbers = jnp.arange(1, starts.shape[0] + 1, dtype=jnp.int32)
    return jnp.sum(jnp.where(inside, numbers[None, :], 0), axis=1)


def allowed_mask(query_pos, key_pos, query_doc, key_doc, query_pic, key_pic):
    same_doc = query_doc[:, None] == key_doc[None, :]
    causal = key_pos[None, :] <= query_pos[:, None]
    picture = (query_pic[:, None] == key_pic[None, :]) & (query_pic[:, None] > 0)
    return same_doc & (causal | picture)


def norm_back(d_normed, hat, inv_rms, gain):
    scaled = d_normed * gain
    return inv_rms * (scaled - hat * jnp.mean(scaled * hat, axis=-1, keepdims=True))


def body(
    tokens,
    seq_ids,
    pic_starts,
    pic_lengths,
    skip_mask,
    w_query,
    w_key,
    w_value,
    w_out,
    w_gate,
    w_up,
    w_down,
    gain_attn,
    gain_ffn,
    cotangent,
):
    tok_rows = tokens.shape[1]
    seq_len = seq_ids.shape[1]
    local_q = w_query.shape[1] // HEAD
    local_kv = w_key.shape[1] // HEAD
    group_size = local_q // local_kv
    query_scale = 1.0 / math.sqrt(HEAD)
    offset = lax.axis_index("ctx") * tok_rows
    positions = offset + jnp.arange(tok_rows, dtype=jnp.int32)
    all_pos = jnp.arange(seq_len, dtype=jnp.int32)
    pic_all = picture_ids(pic_starts[0], pic_lengths[0], all_pos)
    doc_all = seq_ids[0]
    query_doc = lax.dynamic_slice_in_dim(doc_all, offset, tok_rows)
    query_pic = lax.dynamic_slice_in_dim(pic_all, offset, tok_rows)
    allowed = allowed_mask(positions, all_pos, query_doc, doc_all, query_pic, pic_all)

    def attn_weights():
        return (
            lax.all_gather(w_query, "fsdp", axis=0, tiled=True),
            lax.all_gather(w_key, "fsdp", axis=0, tiled=True),
            lax.all_gather(w_value, "fsdp", axis=0, tiled=True),
            lax.all_gather(w_out, "fsdp", axis=1, tiled=True),
            lax.all_gather(gain_attn, "fsdp", axis=0, tiled=True),
        )

    def ffn_weights():
        return (
            lax.all_gather(w_gate, "fsdp", axis=0, tiled=True),
            lax.all_gather(w_up, "fsdp", axis=0, tiled=True),
            lax.all_gather(w_down, "fsdp", axis=1, tiled=True),
            lax.all_gather(gain_ffn, "fsdp", axis=0, tiled=True),
        )

    inputs_f = tokens[0].astype(jnp.float32)
    full_query, full_key, full_value, full_out, gain_one = attn_weights()
    inv_one = lax.rsqrt(jnp.mean(inputs_f * inputs_f, axis=-1, keepdims=True) + norm_eps)
    hat_one = inputs_f * inv_one
    normed_one = (hat_one * gain_one.astype(jnp.float32)).astype(jnp.bfloat16)
    query_pre = jnp.dot(normed_one, full_query, preferred_element_type=jnp.float32)
    key_pre = jnp.dot(normed_one, full_key, preferred_element_type=jnp.float32)
    value_pre = jnp.dot(normed_one, full_value, preferred_element_type=jnp.float32)
    queries = (
        rotate(query_pre.reshape(tok_rows, local_q, HEAD), positions, 1.0) * query_scale
    ).astype(jnp.bfloat16)
    keys_local = rotate(key_pre.reshape(tok_rows, local_kv, HEAD), positions, 1.0).astype(
        jnp.bfloat16
    )
    values_local = value_pre.astype(jnp.bfloat16)
    keys_all, values_all = (
        lax.all_gather(keys_local.reshape(tok_rows, local_kv * HEAD), "ctx", axis=0, tiled=True),
        lax.all_gather(values_local, "ctx", axis=0, tiled=True),
    )
    query_groups = queries.reshape(tok_rows, local_kv, group_size, HEAD)
    key_heads = keys_all.reshape(seq_len, local_kv, HEAD)
    value_heads = values_all.reshape(seq_len, local_kv, HEAD)
    head_outs = []
    log_totals = []
    for kv_index in range(local_kv):
        scores = jnp.einsum(
            "qgd,kd->gqk",
            query_groups[:, kv_index],
            key_heads[:, kv_index],
            preferred_element_type=jnp.float32,
        )
        masked = jnp.where(allowed[None], scores, -1e30)
        row_max = jnp.max(masked, axis=-1, keepdims=True)
        exp_scores = jnp.exp(masked - row_max)
        row_total = jnp.sum(exp_scores, axis=-1, keepdims=True)
        soft_b = (exp_scores / row_total).astype(jnp.bfloat16)
        head_outs.append(
            jnp.einsum(
                "gqk,kd->qgd", soft_b, value_heads[:, kv_index], preferred_element_type=jnp.float32
            )
        )
        log_totals.append(row_max + jnp.log(row_total))
    head_out = jnp.stack(head_outs, axis=1).reshape(tok_rows, local_q * HEAD).astype(jnp.bfloat16)
    attn = lax.psum(jnp.dot(head_out, full_out, preferred_element_type=jnp.float32), "tp")
    keep_f = skip_mask[0].astype(jnp.float32)[:, None]
    mid = inputs_f + keep_f * attn
    full_gate, full_up, full_down, gain_two = ffn_weights()
    inv_two = lax.rsqrt(jnp.mean(mid * mid, axis=-1, keepdims=True) + norm_eps)
    hat_two = mid * inv_two
    normed_two = (hat_two * gain_two.astype(jnp.float32)).astype(jnp.bfloat16)
    gate_act = jnp.dot(normed_two, full_gate, preferred_element_type=jnp.float32)
    up_act = jnp.dot(normed_two, full_up, preferred_element_type=jnp.float32)
    hidden_b = (jax.nn.silu(gate_act) * up_act).astype(jnp.bfloat16)
    ffn = lax.psum(
        jnp.dot(hidden_b, full_down, preferred_element_type=jnp.float32).astype(jnp.bfloat16), "tp"
    ).astype(jnp.float32)
    output = (mid + keep_f * ffn).astype(jnp.bfloat16)
    full_gate, full_up, full_down, gain_two = ffn_weights()
    d_out_f = cotangent[0].astype(jnp.float32)
    d_ffn = (keep_f * d_out_f).astype(jnp.bfloat16)
    grad_down = jnp.einsum("tf,td->fd", hidden_b, d_ffn, preferred_element_type=jnp.float32)
    d_hidden = jnp.einsum("td,fd->tf", d_ffn, full_down, preferred_element_type=jnp.float32)
    sigmoid_gate = jax.nn.sigmoid(gate_act)
    d_up = (d_hidden * (gate_act * sigmoid_gate)).astype(jnp.bfloat16)
    d_gate = (d_hidden * up_act * sigmoid_gate * (1.0 + gate_act * (1.0 - sigmoid_gate))).astype(
        jnp.bfloat16
    )
    grad_gate = jnp.einsum("td,tf->df", normed_two, d_gate, preferred_element_type=jnp.float32)
    grad_up = jnp.einsum("td,tf->df", normed_two, d_up, preferred_element_type=jnp.float32)
    d_norm_part = jnp.einsum(
        "tf,df->td", d_gate, full_gate, preferred_element_type=jnp.float32
    ) + jnp.einsum("tf,df->td", d_up, full_up, preferred_element_type=jnp.float32)
    d_norm_two = lax.psum(d_norm_part, "tp")
    grad_gain_two = jnp.sum(d_norm_two * hat_two, axis=0)
    d_mid = d_out_f + norm_back(d_norm_two, hat_two, inv_two, gain_two.astype(jnp.float32))
    full_query, full_key, full_value, full_out, gain_one = attn_weights()
    d_attn = (keep_f * d_mid).astype(jnp.bfloat16)
    grad_out = jnp.einsum("tc,td->cd", head_out, d_attn, preferred_element_type=jnp.float32)
    d_head = jnp.einsum("td,cd->tc", d_attn, full_out, preferred_element_type=jnp.float32).astype(
        jnp.bfloat16
    )
    d_head_groups = d_head.reshape(tok_rows, local_kv, group_size, HEAD)
    d_query_list = []
    d_key_list = []
    d_value_list = []
    for kv_index in range(local_kv):
        scores = jnp.einsum(
            "qgd,kd->gqk",
            query_groups[:, kv_index],
            key_heads[:, kv_index],
            preferred_element_type=jnp.float32,
        )
        soft_f = jnp.where(allowed[None], jnp.exp(scores - log_totals[kv_index]), 0.0)
        soft_b = soft_f.astype(jnp.bfloat16)
        d_soft = jnp.einsum(
            "qgd,kd->gqk",
            d_head_groups[:, kv_index],
            value_heads[:, kv_index],
            preferred_element_type=jnp.float32,
        )
        row_delta = jnp.sum(soft_f * d_soft, axis=-1, keepdims=True)
        d_scores = (soft_f * (d_soft - row_delta)).astype(jnp.bfloat16)
        d_query_list.append(
            jnp.einsum(
                "gqk,kd->qgd", d_scores, key_heads[:, kv_index], preferred_element_type=jnp.float32
            )
        )
        d_key_list.append(
            jnp.einsum(
                "gqk,qgd->kd",
                d_scores,
                query_groups[:, kv_index],
                preferred_element_type=jnp.float32,
            )
        )
        d_value_list.append(
            jnp.einsum(
                "gqk,qgd->kd",
                soft_b,
                d_head_groups[:, kv_index],
                preferred_element_type=jnp.float32,
            )
        )
    d_keys_all = jnp.stack(d_key_list, axis=1).reshape(seq_len, local_kv * HEAD)
    d_values_all = jnp.stack(d_value_list, axis=1).reshape(seq_len, local_kv * HEAD)
    d_keys, d_values = (
        lax.psum_scatter(
            d_keys_all.astype(jnp.bfloat16), "ctx", scatter_dimension=0, tiled=True
        ).astype(jnp.float32),
        lax.psum_scatter(
            d_values_all.astype(jnp.bfloat16), "ctx", scatter_dimension=0, tiled=True
        ).astype(jnp.float32),
    )
    d_queries = jnp.stack(d_query_list, axis=1).reshape(tok_rows, local_q, HEAD)
    d_query_pre = (
        (rotate(d_queries, positions, -1.0) * query_scale)
        .reshape(tok_rows, local_q * HEAD)
        .astype(jnp.bfloat16)
    )
    d_key_pre = (
        rotate(d_keys.reshape(tok_rows, local_kv, HEAD), positions, -1.0)
        .reshape(tok_rows, local_kv * HEAD)
        .astype(jnp.bfloat16)
    )
    d_value_pre = d_values.astype(jnp.bfloat16)
    grad_query = jnp.einsum(
        "td,tc->dc", normed_one, d_query_pre, preferred_element_type=jnp.float32
    )
    grad_key = jnp.einsum("td,tc->dc", normed_one, d_key_pre, preferred_element_type=jnp.float32)
    grad_value = jnp.einsum(
        "td,tc->dc", normed_one, d_value_pre, preferred_element_type=jnp.float32
    )
    d_norm_part_one = (
        jnp.einsum("tc,dc->td", d_query_pre, full_query, preferred_element_type=jnp.float32)
        + jnp.einsum("tc,dc->td", d_key_pre, full_key, preferred_element_type=jnp.float32)
        + jnp.einsum("tc,dc->td", d_value_pre, full_value, preferred_element_type=jnp.float32)
    )
    d_norm_one = lax.psum(d_norm_part_one.astype(jnp.bfloat16), "tp").astype(jnp.float32)
    grad_gain_one = jnp.sum(d_norm_one * hat_one, axis=0)
    input_grad = (
        d_mid + norm_back(d_norm_one, hat_one, inv_one, gain_one.astype(jnp.float32))
    ).astype(jnp.bfloat16)
    (
        shard_query,
        shard_key,
        shard_value,
        shard_out,
        shard_gain_one,
        shard_gate,
        shard_up,
        shard_down,
        shard_gain_two,
    ) = (
        lax.psum_scatter(
            grad_query.astype(jnp.bfloat16), "fsdp", scatter_dimension=0, tiled=True
        ).astype(jnp.float32),
        lax.psum_scatter(
            grad_key.astype(jnp.bfloat16), "fsdp", scatter_dimension=0, tiled=True
        ).astype(jnp.float32),
        lax.psum_scatter(
            grad_value.astype(jnp.bfloat16), "fsdp", scatter_dimension=0, tiled=True
        ).astype(jnp.float32),
        lax.psum_scatter(
            grad_out.astype(jnp.bfloat16), "fsdp", scatter_dimension=1, tiled=True
        ).astype(jnp.float32),
        lax.psum_scatter(
            grad_gain_one.astype(jnp.bfloat16), "fsdp", scatter_dimension=0, tiled=True
        ).astype(jnp.float32),
        lax.psum_scatter(
            grad_gate.astype(jnp.bfloat16), "fsdp", scatter_dimension=0, tiled=True
        ).astype(jnp.float32),
        lax.psum_scatter(
            grad_up.astype(jnp.bfloat16), "fsdp", scatter_dimension=0, tiled=True
        ).astype(jnp.float32),
        lax.psum_scatter(
            grad_down.astype(jnp.bfloat16), "fsdp", scatter_dimension=1, tiled=True
        ).astype(jnp.float32),
        lax.psum_scatter(
            grad_gain_two.astype(jnp.bfloat16), "fsdp", scatter_dimension=0, tiled=True
        ).astype(jnp.float32),
    )
    summed = (
        lax.psum(shard_query.astype(jnp.bfloat16), "ctx").astype(jnp.float32),
        lax.psum(shard_key.astype(jnp.bfloat16), "ctx").astype(jnp.float32),
        lax.psum(shard_value.astype(jnp.bfloat16), "ctx").astype(jnp.float32),
        lax.psum(shard_out.astype(jnp.bfloat16), "ctx").astype(jnp.float32),
        lax.psum(shard_gate.astype(jnp.bfloat16), "ctx").astype(jnp.float32),
        lax.psum(shard_up.astype(jnp.bfloat16), "ctx").astype(jnp.float32),
        lax.psum(shard_down.astype(jnp.bfloat16), "ctx").astype(jnp.float32),
        lax.psum(shard_gain_one.astype(jnp.bfloat16), "ctx").astype(jnp.float32),
        lax.psum(shard_gain_two.astype(jnp.bfloat16), "ctx").astype(jnp.float32),
    )
    return (
        output[None],
        input_grad[None],
        summed[0],
        summed[1],
        summed[2],
        summed[3],
        summed[4],
        summed[5],
        summed[6],
        summed[7],
        summed[8],
    )


def solution(mesh):
    placed = (
        P("fsdp", "ctx", None),
        P("fsdp", None),
        P("fsdp", None),
        P("fsdp", None),
        P("fsdp", "ctx"),
        P("fsdp", "tp"),
        P("fsdp", "tp"),
        P("fsdp", "tp"),
        P("tp", "fsdp"),
        P("fsdp", "tp"),
        P("fsdp", "tp"),
        P("tp", "fsdp"),
        P("fsdp"),
        P("fsdp"),
        P("fsdp", "ctx", None),
    )
    return jax.shard_map(
        body,
        mesh=mesh,
        in_specs=placed,
        out_specs=(
            P("fsdp", "ctx", None),
            P("fsdp", "ctx", None),
            P("fsdp", "tp"),
            P("fsdp", "tp"),
            P("fsdp", "tp"),
            P("tp", "fsdp"),
            P("fsdp", "tp"),
            P("fsdp", "tp"),
            P("tp", "fsdp"),
            P("fsdp"),
            P("fsdp"),
        ),
        check_vma=False,
    )
```

profile of v0, /device:TPU:0, one launch (start us, length us, event | category | flops | bytes accessed | tf_op | source)
XLA Modules:
  0.0 2267.7 jit_solution(3418881602823138451)
XLA Ops:
  12.6 13.7 all-gather
  28.8 11.5 all-gather.10.cloned.1.call-done
  42.2 8.6 all_gather.44
  51.9 17.4 all-gather.12.cloned.1.call-done
  69.3 2.3 copy.103
  71.6 2.0 fusion.73
  73.7 9.0 all_gather.46
  82.7 68.5 %all-gather.14.cloned.1.call-done = bf16[2048,1024]{1,0:T(8,128)(2,1)} async-done(((bf16[512,1024]{1,0:T(8,128)(2,1)}), bf16[2048,1024]{1,0:T(8,128)(2,1)}) %all-gather.14.cloned.1.call-update) | async-done | bytes 4194320 | tf_op jit(solution)/shard_map/all_gather | solution.py:84
  151.2 6.9 copy.105
  158.1 5.0 fusion.71
  166.6 2.4 fusion.69
  170.6 3.3 fusion.12
  175.7 2.7 fusion.79
  178.5 2.9 fusion.80
  181.5 50.5 %all-gather.16.cloned.1.call-done = bf16[1024,2048]{1,0:T(8,128)(2,1)} async-done(((bf16[1024,512]{1,0:T(8,128)(2,1)}), bf16[1024,2048]{1,0:T(8,128)(2,1)}) %all-gather.16.cloned.1.call-update) | async-done | bytes 4194320 | tf_op jit(solution)/shard_map/all_gather | solution.py:87
  231.9 5.7 fusion.102
  239.8 11.9 all-gather.1
  251.7 70.4 %all-reduce.11.cloned.1.call-done = f32[384,2048]{1,0:T(8,128)} async-done(((f32[384,2048]{1,0:T(8,128)}), f32[384,2048]{1,0:T(8,128)}) %all-reduce.11.cloned.1.call-update) | async-done | bytes 3145744 | tf_op jit(solution)/shard_map/psum | solution.py:142
  322.1 3.0 multiply_reduce_fusion.2
  326.6 198.1 %all-gather.20.cloned.1.call-done = bf16[2048,2816]{1,0:T(8,128)(2,1)} async-done(((bf16[512,2816]{1,0:T(8,128)(2,1)}), bf16[2048,2816]{1,0:T(8,128)(2,1)}) %all-gather.20.cloned.1.call-update) | async-done | bytes 11534352 | tf_op jit(solution)/shard_map/all_gather | solution.py:94
  524.7 11.4 fusion.104
  536.2 189.5 %all-gather.18.cloned.1.call-done = bf16[2048,2816]{1,0:T(8,128)(2,1)} async-done(((bf16[512,2816]{1,0:T(8,128)(2,1)}), bf16[2048,2816]{1,0:T(8,128)(2,1)}) %all-gather.18.cloned.1.call-update) | async-done | bytes 11534352 | tf_op jit(solution)/shard_map/all_gather | solution.py:93
  725.6 11.4 fusion.103
  737.1 189.5 %all-gather.22.cloned.1.call-done = bf16[2816,2048]{1,0:T(8,128)(2,1)} async-done(((bf16[2816,512]{1,0:T(8,128)(2,1)}), bf16[2816,2048]{1,0:T(8,128)(2,1)}) %all-gather.22.cloned.1.call-update) | async-done | bytes 11534352 | tf_op jit(solution)/shard_map/all_gather | solution.py:95
  926.6 12.7 multiply_convert_fusion
  939.3 9.1 fusion.105
  948.4 10.6 convolution_add_fusion
  959.1 84.1 %all-reduce.13.cloned.1.call-done = f32[384,2048]{1,0:T(8,128)} async-done(((f32[384,2048]{1,0:T(8,128)}), f32[384,2048]{1,0:T(8,128)}) %all-reduce.13.cloned.1.call-update) | async-done | bytes 3145744 | tf_op jit(solution)/shard_map/psum | solution.py:171
  1043.2 3.4 multiply_reduce_fusion
  1049.6 2.7 convolution_convert_fusion.8
  1052.3 3.0 reshape.370
  1056.8 6.1 fusion.87
  1062.9 5.7 fusion.62
  1071.6 2.3 copy.150
  1074.0 16.4 fusion.3
  1090.4 13.9 fusion.5
  1110.8 2.3 copy.148
  1113.2 3.3 convolution_convert_fusion.6
  1116.5 20.1 reduce-scatter.28.cloned.1.call-done
  1137.9 3.3 convolution_convert_fusion.7
  1141.2 6.6 convolution_convert_fusion.3
  1148.1 3.3 convolution_bitcast_fusion.3
  1151.4 3.2 convolution_bitcast_fusion.2
  1156.3 4.5 convolution_convert_fusion.4
  1160.9 11.0 convolution_convert_fusion.2
  1171.9 10.7 convolution_convert_fusion
  1183.0 10.8 convolution_convert_fusion.1
  1193.9 10.9 convolution_convert_fusion.5
  1209.9 63.6 %reduce-scatter.20.cloned.1.call-done = bf16[1024,512]{1,0:T(8,128)(2,1)} async-done(((bf16[1024,2048]{1,0:T(8,128)(2,1)}), bf16[1024,512]{1,0:T(8,128)(2,1)}) %reduce-scatter.20.cloned.1.call-update) | async-done | bytes 1048592 | tf_op jit(solution)/shard_map/reduce_scatter | solution.py:281
  1273.5 80.1 %reduce-scatter.14.cloned.1.call-done = bf16[512,1024]{1,0:T(8,128)(2,1)} async-done(((bf16[2048,1024]{1,0:T(8,128)(2,1)}), bf16[512,1024]{1,0:T(8,128)(2,1)}) %reduce-scatter.14.cloned.1.call-update) | async-done | bytes 1048592 | tf_op jit(solution)/shard_map/reduce_scatter | solution.py:272
  1353.6 197.7 %reduce-scatter.26.cloned.1.call-done = bf16[2816,512]{1,0:T(8,128)(2,1)} async-done(((bf16[2816,2048]{1,0:T(8,128)(2,1)}), bf16[2816,512]{1,0:T(8,128)(2,1)}) %reduce-scatter.26.cloned.1.call-update) | async-done | bytes 2883600 | tf_op jit(solution)/shard_map/reduce_scatter | solution.py:293
  1551.3 198.2 %reduce-scatter.24.cloned.1.call-done = bf16[512,2816]{1,0:T(8,128)(2,1)} async-done(((bf16[2048,2816]{1,0:T(8,128)(2,1)}), bf16[512,2816]{1,0:T(8,128)(2,1)}) %reduce-scatter.24.cloned.1.call-update) | async-done | bytes 2883600 | tf_op jit(solution)/shard_map/reduce_scatter | solution.py:290
  1749.5 198.2 %reduce-scatter.22.cloned.1.call-done = bf16[512,2816]{1,0:T(8,128)(2,1)} async-done(((bf16[2048,2816]{1,0:T(8,128)(2,1)}), bf16[512,2816]{1,0:T(8,128)(2,1)}) %reduce-scatter.22.cloned.1.call-update) | async-done | bytes 2883600 | tf_op jit(solution)/shard_map/reduce_scatter | solution.py:287
  1949.6 88.1 %all-reduce.17.cloned.1.call-done = (bf16[384,2048]{1,0:T(8,128)(2,1)}, bf16[384,2048]{1,0:T(8,128)(2,1)}) async-done(((bf16[384,2048]{1,0:T(8,128)(2,1)}, bf16[384,2048]{1,0:T(8,128)(2,1)}), (bf16[384,2048]{1,0:T(8,128)(2,1)}, bf16[384,2048]{1,0:T(8,128)(2,1)})) %all-reduce.17.cloned.1.call-update) | async-done | bytes 3145744 | tf_op jit(solution)/shard_map/psum | solution.py:152
  2037.7 3.0 fusion.38
  2040.7 11.9 all-reduce.4
  2052.7 6.4 all-reduce.2
  2060.3 3.1 fusion.67
  2064.3 2.2 fusion.68
  2066.5 176.5 %all-reduce.15.cloned.1.call-done = (bf16[512,1024]{1,0:T(8,128)(2,1)}, bf16[512,256]{1,0:T(8,128)(2,1)}, bf16[512,256]{1,0:T(8,128)(2,1)}, bf16[1024,512]{1,0:T...) async-done(((bf16[512,1024]{1,0:T(8,128)(2,1)}, bf16[512,256]{1,0:T(8,128)(2,1)}, bf16[512,256]{1,0:T(8,128)(2,1)}, ...) | async-done | bytes 11272208 | tf_op jit(solution)/shard_map/psum | solution.py:301
  2246.6 2.9 convert_element_type.282
  2251.2 2.9 convert_element_type.290
  2254.1 2.9 convert_element_type.292
  2257.0 3.4 convert_element_type.294
  (206 shorter events, 52.7 us)
Async XLA Ops:
  7.2 5.0 copy-start.4
  7.2 19.1 copy-start.44
  7.2 19.1 copy-start.45
  7.2 33.1 %all-gather.10.cloned.1.call-start = ((), (), s32[]{:S(2)}) async-start(), calls=%async_computation.9 | async-start | bytes 1310720 | tf_op jit(solution)/shard_map/all_gather | solution.py:86
  7.9 61.4 %all-gather.12.cloned.1.call-start = ((), (), s32[]{:S(2)}) async-start(), calls=%async_computation.10 | async-start | bytes 1310720 | tf_op jit(solution)/shard_map/all_gather | solution.py:85
  8.7 142.5 %all-gather.14.cloned.1.call-start = ((), (), s32[]{:S(2)}) async-start(), calls=%async_computation.11 | async-start | bytes 5242880 | tf_op jit(solution)/shard_map/all_gather | solution.py:84
  9.4 222.5 %all-gather.16.cloned.1.call-start = ((), (), s32[]{:S(2)}) async-start(), calls=%async_computation.12 | async-start | bytes 5242880 | tf_op jit(solution)/shard_map/all_gather | solution.py:87
  10.0 312.1 %all-reduce.11.cloned.1.call-start = ((), (), s32[]{:S(2)}) async-start(), calls=%async_computation.13 | async-start | bytes 6291456 | tf_op jit(solution)/shard_map/psum | solution.py:142
  12.6 145.5 %copy-start.39 = (f32[384]{0:T(512)}, f32[384]{0:T(512)S(1)}, u32[]{:S(2)}) copy-start(f32[384]{0:T(512)S(1)} %add_rsqrt_fusion.1) | copy-start | bytes 4612
  26.3 131.8 %copy-start.35 = (f32[4,1,512]{2,1,0:T(1,128)}, f32[4,1,512]{2,1,0:T(1,128)S(1)}, u32[]{:S(2)}) copy-start(f32[4,1,512]{2,1,0:T(1,128)S(1)} %convert_element_type.301) | copy-start | bytes 24580
  27.6 135.5 %copy-start.26 = (f32[384,64]{0,1:T(8,128)}, f32[384,64]{0,1:T(8,128)S(1)}, u32[]{:S(2)}) copy-start(f32[384,64]{0,1:T(8,128)S(1)} %get-tuple-element.53) | copy-start | bytes 294916
  28.8 149.6 %copy-start.7 = (pred[384,1536]{0,1:T(8,128)(4,1)}, pred[384,1536]{0,1:T(8,128)(4,1)S(1)}, u32[]{:S(2)}) copy-start(pred[384,1536]{0,1:T(8,128)(4,1)S(1)} %fusion.58) | copy-start | bytes 1769476
  165.0 4.0 copy-start.16
  170.6 5.1 copy-start
  173.9 4.5 copy-start.1
  173.9 1.8 copy-start.22
  181.5 56.2 %copy-start.19 = (bf16[384,2,4,128]{0,3,2,1:T(8,128)(2,1)}, bf16[384,2,4,128]{0,3,2,1:T(8,128)(2,1)S(1)}, u32[]{:S(2)}) copy-start(bf16[384,2,4,128]{0,3,2,1:T(8,128)(2,1)S(1)} %pad_maximum_fusion.1) | copy-start | bytes 2359300
  237.6 287.1 %all-gather.20.cloned.1.call-start = ((), (), s32[]{:S(2)}) async-start(), calls=%async_computation.15 | async-start | bytes 14417920 | tf_op jit(solution)/shard_map/all_gather | solution.py:94
  238.2 13.5 copy-start.42
  238.3 487.4 %all-gather.18.cloned.1.call-start = ((), (), s32[]{:S(2)}) async-start(), calls=%async_computation.14 | async-start | bytes 14417920 | tf_op jit(solution)/shard_map/all_gather | solution.py:93
  239.0 687.6 %all-gather.22.cloned.1.call-start = ((), (), s32[]{:S(2)}) async-start(), calls=%async_computation.16 | async-start | bytes 14417920 | tf_op jit(solution)/shard_map/all_gather | solution.py:95
  239.8 803.4 %all-reduce.13.cloned.1.call-start = ((), (), s32[]{:S(2)}) async-start(), calls=%async_computation.17 | async-start | bytes 6291456 | tf_op jit(solution)/shard_map/psum | solution.py:171
  251.7 795.8 %copy-start.37 = (f32[384]{0:T(512)}, f32[384]{0:T(512)S(1)}, u32[]{:S(2)}) copy-start(f32[384]{0:T(512)S(1)} %convert_reduce_fusion) | copy-start | bytes 4612
  939.3 9.1 copy-start.47
  939.3 9.1 copy-start.48
  959.1 154.1 %reduce-scatter.30.cloned.1.call-start = ((), (), s32[]{:S(2)}) async-start(), calls=%async_computation.26 | async-start | bytes 983040
  1043.2 3.4 copy-start.12
  1043.2 3.4 copy-start.28
  1046.6 3.0 copy-start.13
  1056.7 6.1 copy-start.8
  1056.7 11.9 slice-start
  1056.8 11.9 slice-start.1
  1062.9 5.8 slice-start.2
  1073.9 62.7 %reduce-scatter.28.cloned.1.call-start = ((), (), s32[]{:S(2)}) async-start(), calls=%async_computation.25 | async-start | bytes 983040
  1074.0 16.4 copy-start.9
  1090.4 14.0 copy-start.15
  1104.4 2.2 copy-start.3
  1104.4 3.7 copy-start.2
  1109.8 3.4 copy-start.36
  1109.8 3.4 copy-start.40
  1113.1 24.7 %copy-start.27 = (f32[384,64]{0,1:T(8,128)S(1)}, f32[384,64]{0,1:T(8,128)}, u32[]{:S(2)}) copy-start(f32[384,64]{0,1:T(8,128)} %copy-done.26) | copy-start | bytes 294916
  1113.1 24.7 %copy-start.31 = (f32[384,64]{0,1:T(8,128)S(1)}, f32[384,64]{0,1:T(8,128)}, u32[]{:S(2)}) copy-start(f32[384,64]{0,1:T(8,128)} %get-tuple-element.51) | copy-start | bytes 294916
  1113.1 96.8 %reduce-scatter.18.cloned.1.call-start = ((), (), s32[]{:S(2)}) async-start(), calls=%async_computation.20 | async-start | bytes 1310720 | tf_op jit(solution)/shard_map/reduce_scatter | solution.py:278
  1116.5 93.4 %reduce-scatter.16.cloned.1.call-start = ((), (), s32[]{:S(2)}) async-start(), calls=%async_computation.19 | async-start | bytes 1310720 | tf_op jit(solution)/shard_map/reduce_scatter | solution.py:275
  1137.7 3.5 copy-start.38
  1141.2 132.3 %reduce-scatter.20.cloned.1.call-start = ((), (), s32[]{:S(2)}) async-start(), calls=%async_computation.21 | async-start | bytes 5242880 | tf_op jit(solution)/shard_map/reduce_scatter | solution.py:281
  1147.8 205.8 %reduce-scatter.14.cloned.1.call-start = ((), (), s32[]{:S(2)}) async-start(), calls=%async_computation.18 | async-start | bytes 5242880 | tf_op jit(solution)/shard_map/reduce_scatter | solution.py:272
  1148.1 3.3 copy-start.17
  1160.8 390.4 %reduce-scatter.26.cloned.1.call-start = ((), (), s32[]{:S(2)}) async-start(), calls=%async_computation.24 | async-start | bytes 14417920 | tf_op jit(solution)/shard_map/reduce_scatter | solution.py:293
  1171.9 577.6 %reduce-scatter.24.cloned.1.call-start = ((), (), s32[]{:S(2)}) async-start(), calls=%async_computation.23 | async-start | bytes 14417920 | tf_op jit(solution)/shard_map/reduce_scatter | solution.py:290
  1182.7 765.0 %reduce-scatter.22.cloned.1.call-start = ((), (), s32[]{:S(2)}) async-start(), calls=%async_computation.22 | async-start | bytes 14417920 | tf_op jit(solution)/shard_map/reduce_scatter | solution.py:287
  1193.8 843.9 %all-reduce.17.cloned.1.call-start = ((), (), s32[]{:S(2)}) async-start(), calls=%async_computation.28 | async-start | bytes 6291456 | tf_op jit(solution)/shard_map/psum | solution.py:152
  1193.8 10.9 copy-start.20
  1193.8 10.9 copy-start.33
  1204.7 1.9 copy-start.21
  1209.8 1033.1 %all-reduce.15.cloned.1.call-start = ((), (), s32[]{:S(2)}) async-start(), calls=%async_computation.27 | async-start | bytes 22544384 | tf_op jit(solution)/shard_map/psum | solution.py:301
  1947.7 92.9 %copy-start.41 = (bf16[2048]{0:T(1024)(128)(2,1)S(1)}, bf16[2048]{0:T(1024)(128)(2,1)}, u32[]{:S(2)}) copy-start(bf16[2048]{0:T(1024)(128)(2,1)} %get-tuple-element.11) | copy-start | bytes 12292
  2060.3 3.1 copy-start.6
  2060.3 3.1 copy-start.11
  2060.3 4.0 copy-start.18
  2242.9 6.6 copy-start.30
  2246.6 4.6 copy-start.25
  2251.2 2.9 copy-start.24
  2254.1 2.9 copy-start.23
  (8 other events, 10.4 us)
Sparse Core Ops, SparseCore 0:
  9.6 30.6 all-gather.9
  41.9 27.3 all-gather.11
  70.9 80.2 all-gather.13
  152.6 79.2 all-gather.15
  237.8 84.3 all-reduce.10
  323.6 201.0 all-gather.19
  526.4 199.2 all-gather.17
  727.3 199.2 all-gather.21
  959.2 83.9 all-reduce.12
  1074.1 23.2 reduce-scatter.29
  1113.2 23.3 reduce-scatter.27
  1139.3 27.1 reduce-scatter.17
  1169.5 25.7 reduce-scatter.15
  1198.0 75.4 reduce-scatter.19
  1276.3 77.2 reduce-scatter.13
  1355.8 195.4 reduce-scatter.25
  1553.5 195.9 reduce-scatter.23
  1751.7 195.9 reduce-scatter.21
  1950.6 86.9 all-reduce.16
  2041.1 201.7 all-reduce.14
where the time goes:
time: 2270 us
  waiting for transfers between devices  1910 us (84%)
  matrix products  189 us (8%)
  blocking collectives  61.4 us (3%)
  other arithmetic  60.2 us (3%)
  local copies, waits for them, and re-layouts  33.3 us (1%)
    reduce_scatter x1, waiting for transfers between devices, body(): lax.psum_scatter(grad_gate.astype(jnp.bfloat16), 'fsdp', scatter_dimensio...  198 us
    reduce_scatter x1, waiting for transfers between devices, body(): lax.psum_scatter(grad_up.astype(jnp.bfloat16), 'fsdp', scatter_dimension=...  198 us
    all_gather x1, waiting for transfers between devices, ffn_weights(): lax.all_gather(w_up, 'fsdp', axis=0, tiled=True)  198 us
    reduce_scatter x1, waiting for transfers between devices, body(): lax.psum_scatter(grad_down.astype(jnp.bfloat16), 'fsdp', scatter_dimensio...  198 us
    all_gather x1, waiting for transfers between devices, ffn_weights(): lax.all_gather(w_gate, 'fsdp', axis=0, tiled=True)  189 us
    all_gather x1, waiting for transfers between devices, ffn_weights(): lax.all_gather(w_down, 'fsdp', axis=1, tiled=True)  189 us
    psum x1, waiting for transfers between devices, body(): lax.psum(shard_query.astype(jnp.bfloat16), 'ctx').astype(jnp.float32)  176 us
    psum x1, waiting for transfers between devices, body(): lax.psum(jnp.dot(hidden_b, full_down, preferred_element_type=jnp.float32)...  88.1 us
  transfers between devices with their start and end apart: 20, of which 17 were waited for; matrix products, arithmetic and copies ran while one was open for 8% of the time, Pallas kernels for 0%

commit v1 on v0

v1 whole, which is shorter than its diff:
```python
import math

import jax
import jax.numpy as jnp
from jax import lax
from jax.sharding import PartitionSpec as P

HEAD = 128
norm_eps = 1e-05
rope_base = 10000.0
F32 = jnp.float32
BF16 = jnp.bfloat16


def dot(a, b, ca, cb):
    return lax.dot_general(a, b, (((ca,), (cb,)), ((), ())), preferred_element_type=F32)


def rope_tables(positions):
    half_width = HEAD // 2
    frequency = jnp.power(rope_base, -jnp.arange(half_width, dtype=F32) * 2.0 / HEAD)
    angles = positions.astype(F32)[:, None] * frequency[None, :]
    return jnp.cos(angles), jnp.sin(angles)


def rotate(u, cosine, sine):
    half_width = HEAD // 2
    parts = []
    for head in range(u.shape[1] // HEAD):
        first = u[:, head * HEAD : head * HEAD + half_width]
        second = u[:, head * HEAD + half_width : (head + 1) * HEAD]
        parts += [first * cosine - second * sine, second * cosine + first * sine]
    return jnp.concatenate(parts, axis=1)


def picture_ids(starts, lengths, positions):
    inside = (positions[:, None] >= starts[None, :]) & (
        positions[:, None] < starts[None, :] + lengths[None, :]
    )
    numbers = jnp.arange(1, starts.shape[0] + 1, dtype=jnp.int32)
    return jnp.sum(jnp.where(inside, numbers[None, :], 0), axis=1)


def allowed_mask(query_pos, key_pos, query_doc, key_doc, query_pic, key_pic):
    same_doc = query_doc[:, None] == key_doc[None, :]
    causal = key_pos[None, :] <= query_pos[:, None]
    picture = (query_pic[:, None] == key_pic[None, :]) & (query_pic[:, None] > 0)
    return same_doc & (causal | picture)


def norm_back(d_normed, hat, inv_rms, gain):
    scaled = d_normed * gain
    return inv_rms * (scaled - hat * jnp.mean(scaled * hat, axis=-1, keepdims=True))


def far(v):
    return lax.ppermute(v, "ctx", [(i, i ^ 2) for i in range(4)])


def near(v):
    return lax.ppermute(v, "ctx", [(i, i ^ 1) for i in range(4)])


def side(v):
    return lax.ppermute(v, "tp", [(0, 1), (1, 0)])


def spread(v):
    n, w = v.shape
    left, right = v[:, : w // 2], v[:, w // 2 :]
    left_far = far(left)
    right_side = side(right)
    left_two = side(jnp.concatenate([left, left_far], axis=0))
    right_two = far(jnp.concatenate([right, right_side], axis=0))
    left_all = jnp.concatenate([left, left_two[:n], left_far, left_two[n:]], axis=0)
    right_all = jnp.concatenate([right, right_side, right_two], axis=0)
    mine = jnp.concatenate([left_all, right_all], axis=1)
    return jnp.concatenate([mine, near(mine)], axis=0)


def collect(p):
    n, w = p.shape[0] // 8, p.shape[1]
    both = p[: 4 * n].astype(F32) + near(p[4 * n :]).astype(F32)
    both = both.astype(BF16)
    left, right = both[:, : w // 2], both[:, w // 2 :].reshape(2, 2, n, w // 2)
    left_far = far(left[2 * n :])
    right_side = side(right[:, 1].reshape(2 * n, w // 2))
    left = (left[: 2 * n].astype(F32) + left_far.astype(F32)).astype(BF16)
    right = (right[:, 0].reshape(2 * n, w // 2).astype(F32) + right_side.astype(F32)).astype(BF16)
    left_side = side(left[n:])
    right_far = far(right[n:])
    return jnp.concatenate(
        [
            left[:n].astype(F32) + left_side.astype(F32),
            right[:n].astype(F32) + right_far.astype(F32),
        ],
        axis=1,
    )


def both_sides(v, t):
    other = side(v)
    return jnp.where(
        t == 0, jnp.concatenate([v, other], axis=0), jnp.concatenate([other, v], axis=0)
    )


def ctx_rows(v, c):
    n = v.shape[0]
    two = jnp.stack([v, far(v)])
    other = near(two)
    out = jnp.zeros((4, n, v.shape[1]), v.dtype)
    for bits, piece in ((0, two[0]), (2, two[1]), (1, other[0]), (3, other[1])):
        out = lax.dynamic_update_slice(out, piece[None], (c ^ bits, 0, 0))
    return out


def swap_halves(v):
    n = v.shape[0] // 2
    return jnp.concatenate([v[n:], v[:n]], axis=0)


def body(
    tokens,
    seq_ids,
    pic_starts,
    pic_lengths,
    skip_mask,
    w_query,
    w_key,
    w_value,
    w_out,
    w_gate,
    w_up,
    w_down,
    gain_attn,
    gain_ffn,
    cotangent,
):
    tok_rows = tokens.shape[1]
    width = tokens.shape[2]
    own = tok_rows // 2
    seq_len = seq_ids.shape[1]
    c = lax.axis_index("ctx")
    t = lax.axis_index("tp")
    core = c & 1
    q_cols = w_query.shape[1] // 4
    heads = q_cols // HEAD
    ff = w_gate.shape[1] // 4
    query_scale = 1.0 / math.sqrt(HEAD)

    wq_t = lax.dynamic_slice_in_dim(w_query, c * q_cols, q_cols, 1).T
    w_kv = jnp.where(core == 0, w_key, w_value)
    wkv_t = lax.dynamic_slice_in_dim(w_kv, (c >> 1) * HEAD, HEAD, 1).T
    gains = jnp.concatenate(
        [gain_attn[None], gain_ffn[None], jnp.zeros((14, gain_attn.shape[0]), BF16)], axis=0
    )
    first = lax.all_gather(
        jnp.concatenate([wq_t, wkv_t, gains], axis=0), "fsdp", axis=1, tiled=True
    )
    qkv_cols = q_cols + HEAD
    wqkv = first[:qkv_cols]
    gain_one = first[qkv_cols].astype(F32)
    gain_two = first[qkv_cols + 1].astype(F32)
    wo = lax.all_gather(
        lax.dynamic_slice_in_dim(w_out, c * q_cols, q_cols, 0), "fsdp", axis=1, tiled=True
    )
    wg_t = lax.dynamic_slice_in_dim(w_gate, c * ff, ff, 1).T
    wu_t = lax.dynamic_slice_in_dim(w_up, c * ff, ff, 1).T
    wgu = lax.all_gather(jnp.concatenate([wg_t, wu_t], axis=0), "fsdp", axis=1, tiled=True)
    wd = lax.all_gather(
        lax.dynamic_slice_in_dim(w_down, c * ff, ff, 0), "fsdp", axis=1, tiled=True
    )

    x_own_b = lax.dynamic_slice_in_dim(tokens[0], t * own, own, 0)
    x_own = x_own_b.astype(F32)
    keep_own = lax.dynamic_slice_in_dim(skip_mask[0], t * own, own, 0).astype(F32)[:, None]
    dy_own = lax.dynamic_slice_in_dim(cotangent[0], t * own, own, 0).astype(F32)
    d_ffn_own = (keep_own * dy_own).astype(BF16)

    pos_list = []
    for block in range(8):
        near_bit, far_bit, side_bit = block >> 2, (block >> 1) & 1, block & 1
        start = (c ^ (near_bit + 2 * far_bit)) * tok_rows + (t ^ side_bit) * own
        pos_list.append(start)
    positions = jnp.concatenate([s + jnp.arange(own, dtype=jnp.int32) for s in pos_list])
    docs = jnp.concatenate([lax.dynamic_slice_in_dim(seq_ids[0], s, own, 0) for s in pos_list])
    pics = picture_ids(pic_starts[0], pic_lengths[0], positions)
    allowed = allowed_mask(positions, positions, docs, docs, pics, pics)
    cosine, sine = rope_tables(positions)

    x_all = spread(x_own_b).astype(F32)
    inv_all = lax.rsqrt(jnp.mean(x_all * x_all, axis=-1, keepdims=True) + norm_eps)
    n1 = (x_all * inv_all * gain_one).astype(BF16)
    qkv_pre = dot(n1, wqkv, 1, 1)
    queries = (rotate(qkv_pre[:, :q_cols], cosine, sine) * query_scale).astype(BF16)
    kv_pre = qkv_pre[:, q_cols:]
    kv_own = jnp.where(core == 0, rotate(kv_pre, cosine, sine), kv_pre).astype(BF16)
    kv_other = swap_halves(near(kv_own))
    keys = jnp.where(core == 0, kv_own, kv_other)
    values = jnp.where(core == 0, kv_other, kv_own)
    q_heads = queries.reshape(seq_len, heads, HEAD)
    scores = jnp.einsum("qhd,kd->hqk", q_heads, keys, preferred_element_type=F32)
    masked = jnp.where(allowed[None], scores, -1e30)
    row_max = jnp.max(masked, axis=-1, keepdims=True)
    exp_scores = jnp.exp(masked - row_max)
    row_total = jnp.sum(exp_scores, axis=-1, keepdims=True)
    soft_b = (exp_scores / row_total).astype(BF16)
    log_total = row_max + jnp.log(row_total)
    head_out = (
        jnp.einsum("hqk,kd->qhd", soft_b, values, preferred_element_type=F32)
        .reshape(seq_len, q_cols)
        .astype(BF16)
    )
    attn = collect(dot(head_out, wo, 1, 0).astype(BF16))
    mid = x_own + keep_own * attn
    inv_two = lax.rsqrt(jnp.mean(mid * mid, axis=-1, keepdims=True) + norm_eps)
    hat_two = mid * inv_two
    n2 = spread((hat_two * gain_two).astype(BF16))

    d_ffn = spread(d_ffn_own)
    gu = dot(wgu, n2, 1, 1)
    gate, up = gu[:ff], gu[ff:]
    sig = jax.nn.sigmoid(gate)
    hidden = (gate * sig * up).astype(BF16)
    d_hidden = dot(wd, d_ffn, 1, 1)
    d_gate = (d_hidden * up * sig * (1.0 + gate * (1.0 - sig))).astype(BF16)
    d_up = (d_hidden * (gate * sig)).astype(BF16)
    d_gu = jnp.concatenate([d_gate, d_up], axis=0)
    d_n2 = collect(dot(d_gu, wgu, 0, 0).astype(BF16))
    grad_gu = dot(d_gu, n2, 1, 0).astype(BF16)
    grad_down = dot(hidden, d_ffn, 1, 0).astype(BF16)
    shard_gu = lax.psum_scatter(grad_gu, "fsdp", scatter_dimension=1, tiled=True)
    shard_down = lax.psum_scatter(grad_down, "fsdp", scatter_dimension=1, tiled=True)
    ffn = collect(dot(hidden, wd, 0, 0).astype(BF16))
    output = both_sides((mid + keep_own * ffn).astype(BF16), t)

    d_mid = dy_own + norm_back(d_n2, hat_two, inv_two, gain_two)
    d_attn = spread((keep_own * d_mid).astype(BF16))
    grad_out = dot(head_out, d_attn, 0, 0).astype(BF16)
    shard_out = lax.psum_scatter(grad_out, "fsdp", scatter_dimension=1, tiled=True)
    d_head = dot(d_attn, wo, 1, 1).astype(BF16).reshape(seq_len, heads, HEAD)
    scores = jnp.einsum("qhd,kd->hqk", q_heads, keys, preferred_element_type=F32)
    soft = jnp.where(allowed[None], jnp.exp(scores - log_total), 0.0)
    d_soft = jnp.einsum("qhd,kd->hqk", d_head, values, preferred_element_type=F32)
    delta = jnp.sum(soft * d_soft, axis=-1, keepdims=True)
    d_scores = (soft * (d_soft - delta)).astype(BF16)
    d_queries = jnp.einsum("hqk,kd->qhd", d_scores, keys, preferred_element_type=F32)
    d_keys = jnp.einsum("hqk,qhd->kd", d_scores, q_heads, preferred_element_type=F32)
    d_values = jnp.einsum("hqk,qhd->kd", soft.astype(BF16), d_head, preferred_element_type=F32)
    sent = swap_halves(near(jnp.where(core == 0, d_values, d_keys).astype(BF16)))
    d_kv = jnp.where(core == 0, d_keys, d_values) + sent.astype(F32)
    d_kv_pre = jnp.where(core == 0, rotate(d_kv, cosine, -sine), d_kv)
    d_query_pre = rotate(d_queries.reshape(seq_len, q_cols), cosine, -sine) * query_scale
    d_qkv = jnp.concatenate([d_query_pre.astype(BF16), d_kv_pre.astype(BF16)], axis=1)
    grad_qkv = dot(d_qkv, n1, 0, 0).astype(BF16)
    shard_qkv = lax.psum_scatter(grad_qkv, "fsdp", scatter_dimension=1, tiled=True)
    d_n1 = collect(dot(d_qkv, wqkv, 1, 0).astype(BF16))
    inv_one = lax.rsqrt(jnp.mean(x_own * x_own, axis=-1, keepdims=True) + norm_eps)
    hat_one = x_own * inv_one
    input_grad = both_sides(
        (d_mid + norm_back(d_n1, hat_one, inv_one, gain_one)).astype(BF16), t
    )

    gain_grads = lax.psum(
        jnp.stack([jnp.sum(d_n1 * hat_one, axis=0), jnp.sum(d_n2 * hat_two, axis=0)]),
        ("fsdp", "ctx", "tp"),
    )
    shard_width = gain_attn.shape[0]
    gain_grads = lax.dynamic_slice_in_dim(
        gain_grads, lax.axis_index("fsdp") * shard_width, shard_width, 1
    )

    all_gu = ctx_rows(shard_gu, c)
    all_down = ctx_rows(shard_down, c).reshape(4 * ff, -1)
    all_out = ctx_rows(shard_out, c).reshape(4 * q_cols, -1)
    all_qkv = ctx_rows(shard_qkv, c)
    grad_kv = all_qkv[:, q_cols:].reshape(2, 2, HEAD, -1)
    return (
        output[None],
        input_grad[None],
        all_qkv[:, :q_cols].reshape(4 * q_cols, -1).T.astype(F32),
        grad_kv[:, 0].reshape(2 * HEAD, -1).T.astype(F32),
        grad_kv[:, 1].reshape(2 * HEAD, -1).T.astype(F32),
        all_out.astype(F32),
        all_gu[:, :ff].reshape(4 * ff, -1).T.astype(F32),
        all_gu[:, ff:].reshape(4 * ff, -1).T.astype(F32),
        all_down.astype(F32),
        gain_grads[0],
        gain_grads[1],
    )


def solution(mesh):
    placed = (
        P("fsdp", "ctx", None),
        P("fsdp", None),
        P("fsdp", None),
        P("fsdp", None),
        P("fsdp", "ctx"),
        P("fsdp", "tp"),
        P("fsdp", "tp"),
        P("fsdp", "tp"),
        P("tp", "fsdp"),
        P("fsdp", "tp"),
        P("fsdp", "tp"),
        P("tp", "fsdp"),
        P("fsdp"),
        P("fsdp"),
        P("fsdp", "ctx", None),
    )
    return jax.shard_map(
        body,
        mesh=mesh,
        in_specs=placed,
        out_specs=(
            P("fsdp", "ctx", None),
            P("fsdp", "ctx", None),
            P("fsdp", "tp"),
            P("fsdp", "tp"),
            P("fsdp", "tp"),
            P("tp", "fsdp"),
            P("fsdp", "tp"),
            P("fsdp", "tp"),
            P("tp", "fsdp"),
            P("fsdp"),
            P("fsdp"),
        ),
        check_vma=False,
    )
```

time: 2270 us -> 835 us (0.37)
  waiting for transfers between devices: 1910 us -> 261 us
  other arithmetic: 60.2 us -> 209 us
  local copies, waits for them, and re-layouts: 33.3 us -> 83.1 us
  starting transfers between devices: 1.27 us -> 49.5 us
  matrix products: 189 us -> 155 us
    all_gather x7 -> x4, waiting for transfers between devices: 725 us -> 17 us  [the longest x1 17 us: body(): lax.all_gather(lax.dynamic_slice_in_dim(w_down, c * ff, ff, 0), 'fsdp', a...]
    reduce_scatter x7 -> x4, waiting for transfers between devices: 738 us -> 48.1 us  [the longest x1 25 us: body(): lax.psum_scatter(grad_qkv, 'fsdp', scatter_dimension=1, tiled=True)]
    psum x4 -> x0, waiting for transfers between devices: 419 us -> none  [the longest x1 176 us: body(): lax.psum(shard_query.astype(jnp.bfloat16), 'ctx').astype(jnp.float32)]
    ppermute x0 -> x52, waiting for transfers between devices: none -> 196 us  [the longest x20 105 us: far(): return lax.ppermute(v, 'ctx', [(i, i ^ 2) for i in range(4)])]
    concatenate x1 -> x23, other arithmetic: 0.02 us -> 103 us  [the longest x4 79 us: spread(): mine = jnp.concatenate([left_all, right_all], axis=1)]
    ppermute x0 -> x52, starting transfers between devices: none -> 49.2 us  [the longest x20 24.4 us: far(): return lax.ppermute(v, 'ctx', [(i, i ^ 2) for i in range(4)])]
    psum x1, blocking collectives: 6.44 us -> 51.4 us  [body(): lax.psum(jnp.stack([jnp.sum(d_n1 * hat_one, axis=0), jnp.sum(d_n2 * hat_t...]
    all_gather x4 -> x0, blocking collectives: 43.1 us -> none  [the longest x1 13.7 us: attn_weights(): lax.all_gather(gain_attn, 'fsdp', axis=0, tiled=True)]
  transfers between devices with their start and end apart: 20 -> 60, of which waited for: 17 -> 28; matrix products, arithmetic and copies ran while one was open for 8% -> 44% of each run, Pallas kernels for 0% -> 0%
where the time goes in v1:
time: 835 us; the launch traced here: 825 us
  waiting for transfers between devices  261 us (31%)
  other arithmetic  209 us (25%)
  matrix products  155 us (19%)
  local copies, waits for them, and re-layouts  83.1 us (10%)
  blocking collectives  51.4 us (6%)
  starting transfers between devices  49.5 us (6%)
  between operations  16.4 us (2%)
    dot_general x12, matrix products, dot(): lax.dot_general(a, b, (((ca,), (cb,)), ((), ())), preferred_element_type=...  111 us
    ppermute x20, waiting for transfers between devices, far(): return lax.ppermute(v, 'ctx', [(i, i ^ 2) for i in range(4)])  105 us
    ppermute x18, waiting for transfers between devices, side(): return lax.ppermute(v, 'tp', [(0, 1), (1, 0)])  88.7 us
    concatenate x4, other arithmetic, spread(): mine = jnp.concatenate([left_all, right_all], axis=1)  79 us
    psum x1, blocking collectives, body(): lax.psum(jnp.stack([jnp.sum(d_n1 * hat_one, axis=0), jnp.sum(d_n2 * hat_t...  51.4 us
    unnamed x208, local copies, waits for them, and re-layouts  27.8 us
    reduce_scatter x1, waiting for transfers between devices, body(): lax.psum_scatter(grad_qkv, 'fsdp', scatter_dimension=1, tiled=True)  25 us
    ppermute x20, starting transfers between devices, far(): return lax.ppermute(v, 'ctx', [(i, i ^ 2) for i in range(4)])  24.4 us
  transfers between devices with their start and end apart: 60, of which 28 were waited for; matrix products, arithmetic and copies ran while one was open for 44% of the time, Pallas kernels for 0%

profile of v1, /device:TPU:0, one launch (start us, length us, event | category | flops | bytes accessed | tf_op | source)
XLA Modules:
  0.0 825.4 jit_solution(8399771713944028795)
XLA Ops:
  15.6 3.0 collective-permute-start
  20.2 7.6 collective-permute-done
  31.3 15.3 %collective-permute-done.1 = bf16[384,1024]{1,0:T(8,128)(2,1)S(1)} collective-permute-done((bf16[384,1024]{1,0:T(8,128)(2,1)S(1)}, bf16[384,1024]{1,0:T(8,128)(2,1)S(1)}, u32[]{:S(2)}, u32[]{:S(2)}) %collective-permute-start.1) | collective-permute-done | bytes 786464 | tf_op jit(solution)/shard_map/ppermute | solution.py:65
  47.9 19.6 %maximum_maximum_fusion = bf16[768,2048]{1,0:T(8,128)(2,1)} fusion(bf16[384,1024]{1,0:T(8,128)(2,1)S(1)} %collective-permute-done.3, bf16[192,1024]{1,0:T(8,128)(2,1)S(1)} %collective-permute-done.2, bf16[192,1024]{1,0:T(8,128)(2,1)S(1)} %get-tuple-element.104, bf16[192,1024]{1,0:T(8,128)(2,1)S(1)} %get-tuple-element.102, ...), kind=kLoop, calls=%fused_computation.45 | loop fusion | flops 22020096 | bytes 6291456 | tf_op jit(solution)/shard_map/concatenate | solution.py:77
  69.9 5.2 or_and_fusion
  76.9 6.0 fusion.7
  82.9 3.0 fusion.26
  90.2 5.6 fusion.5
  95.8 6.0 fusion.6
  102.9 8.3 %fusion.16 = bf16[128,2,1536]{2,0,1:T(8,128)(2,1)} fusion(f32[1536,1536,2]{1,0,2:T(8,128)S(1)} %get-tuple-element.123, f32[2,1536]{1,0:T(2,128)S(1)} %fusion.6, f32[2,1536]{1,0:T(2,128)S(1)} %get-tuple-element.122, pred[1536,1536]{0,1:T(8,128)(4,1)} %or_and_fusion, bf16[1536,128]{0,1:T(8,128)(2,1)S(1)} %fusion.55, pred[]{:T(512)S(6)} %eq.48, ...), kind=kOutput, calls=%fused_computation.54 | convolution fusion | flops 1228210176 | bytes 22831104 | tf_op jit(solution)/shard_map/hqk,kd->qhd/dot_general | solution.py:211
  111.2 3.3 convolution_convert_fusion
  114.6 2.7 copy-done.4
  125.3 4.2 add_convert_fusion.3
  132.0 17.4 %collective-permute-done.7 = bf16[384,1024]{1,0:T(8,128)(2,1)S(1)} collective-permute-done((bf16[384,1024]{1,0:T(8,128)(2,1)S(1)}, bf16[384,1024]{1,0:T(8,128)(2,1)S(1)}, u32[]{:S(2)}, u32[]{:S(2)}) %collective-permute-start.7) | collective-permute-done | bytes 786464 | tf_op jit(solution)/shard_map/ppermute | solution.py:57
  152.3 7.9 collective-permute-done.8
  165.6 7.0 collective-permute-done.22
  177.6 15.6 %collective-permute-done.23 = bf16[384,1024]{1,0:T(8,128)(2,1)S(1)} collective-permute-done((bf16[384,1024]{1,0:T(8,128)(2,1)S(1)}, bf16[384,1024]{1,0:T(8,128)(2,1)S(1)}, u32[]{:S(2)}, u32[]{:S(2)}) %collective-permute-start.23) | collective-permute-done | bytes 786464 | tf_op jit(solution)/shard_map/ppermute | solution.py:65
  195.0 20.0 %maximum_maximum_fusion.2 = bf16[768,2048]{1,0:T(8,128)(2,1)} fusion(bf16[384,1024]{1,0:T(8,128)(2,1)S(1)} %collective-permute-done.25, bf16[192,1024]{1,0:T(8,128)(2,1)S(1)} %collective-permute-done.24, bf16[192,1024]{1,0:T(8,128)(2,1)S(1)} %get-tuple-element.96, bf16[192,1024]{1,0:T(8,128)(2,1)S(1)} %get-tuple-element.94, ...), kind=kLoop, calls=%fused_computation.47 | loop fusion | flops 22020096 | bytes 6291456 | tf_op jit(solution)/shard_map/concatenate | solution.py:77
  217.0 18.1 %collective-permute-done.12 = bf16[384,1024]{1,0:T(8,128)(2,1)S(1)} collective-permute-done((bf16[384,1024]{1,0:T(8,128)(2,1)S(1)}, bf16[384,1024]{1,0:T(8,128)(2,1)S(1)}, u32[]{:S(2)}, u32[]{:S(2)}) %collective-permute-start.12) | collective-permute-done | bytes 786464 | tf_op jit(solution)/shard_map/ppermute | solution.py:65
  235.6 19.7 %maximum_maximum_fusion.1 = bf16[768,2048]{1,0:T(8,128)(2,1)} fusion(bf16[384,1024]{1,0:T(8,128)(2,1)S(1)} %collective-permute-done.14, bf16[192,1024]{1,0:T(8,128)(2,1)S(1)} %collective-permute-done.13, bf16[192,1024]{1,0:T(8,128)(2,1)S(1)} %get-tuple-element.100, bf16[192,1024]{1,0:T(8,128)(2,1)S(1)} %get-tuple-element.98, ...), kind=kLoop, calls=%fused_computation.46 | loop fusion | flops 22020096 | bytes 6291456 | tf_op jit(solution)/shard_map/concatenate | solution.py:77
  256.5 7.4 pad_maximum_fusion.2
  264.0 35.3 %fusion.121 = f32[1408,1536]{1,0:T(8,128)} fusion(bf16[1408,2048]{0,1:T(8,128)(2,1)} %all-gather.9.cloned.1.call-done, bf16[768,2048]{1,0:T(8,128)(2,1)} %collective-permute-done.15, bf16[384,1024]{1,0:T(8,128)(2,1)} %copy-done.73, bf16[192,1024]{1,0:T(8,128)(2,1)S(1)} %copy-done.61, bf16[192,1024]{1,0:T(8,128)(2,1)S(1)} %copy-done.42, ...), kind=kOutput, calls=%fused_computation.277 | convolution fusion | flops 8908701696 | bytes 20709376 | tf_op jit(solution)/shard_map/dot_general | solution.py:16
  299.3 17.0 %all-gather.11.cloned.1.call-done = bf16[704,2048]{1,0:T(8,128)(2,1)} async-done(((bf16[704,512]{1,0:T(8,128)(2,1)}), bf16[704,2048]{1,0:T(8,128)(2,1)}) %all-gather.11.cloned.1.call-update) | async-done | bytes 2883600 | tf_op jit(solution)/shard_map/all_gather | solution.py:171
  316.3 13.8 %multiply_convert_fusion.1 = (bf16[704,1536]{1,0:T(8,128)(2,1)S(1)}, bf16[704,1536]{1,0:T(8,128)(2,1)}, bf16[704,1536]{1,0:T(8,128)(2,1)S(1)}) fusion(f32[1408,1536]{1,0:T(8,128)} %fusion.121, bf16[704,2048]{1,0:T(8,128)(2,1)} %all-gather.11.cloned.1.call-done, bf16[1536,2048]{1,0:T(8,128)(2,1)} %pad_maximum_fusion.2), kind=kOutput, calls=%fused_computation.40 | convolution fusion | flops 4445405184 | bytes 24313856 | tf_op jit(solution)/shard_map/dot_general | solution.py:16
  330.1 12.3 %convolution_convert_fusion.3 = bf16[1536,2048]{1,0:T(8,128)(2,1)S(1)} fusion(bf16[1408,2048]{0,1:T(8,128)(2,1)S(1)} %copy-done.93, bf16[704,1536]{1,0:T(8,128)(2,1)} %get-tuple-element.48, bf16[704,1536]{1,0:T(8,128)(2,1)S(1)} %get-tuple-element.47), kind=kOutput, calls=%fused_computation.26 | convolution fusion | flops 8870166528 | bytes 16384000 | tf_op jit(solution)/shard_map/dot_general | solution.py:16
  347.0 5.3 convolution_convert_fusion.4
  356.4 6.2 convolution_convert_fusion.5
  362.7 4.2 add_convert_fusion.1
  370.3 4.2 add_convert_fusion.2
  376.1 11.5 %collective-permute-done.28 = bf16[384,1024]{1,0:T(8,128)(2,1)S(1)} collective-permute-done((bf16[384,1024]{1,0:T(8,128)(2,1)S(1)}, bf16[384,1024]{1,0:T(8,128)(2,1)S(1)}, u32[]{:S(2)}, u32[]{:S(2)}) %collective-permute-start.28) | collective-permute-done | bytes 786464 | tf_op jit(solution)/shard_map/ppermute | solution.py:57
  391.4 13.0 %collective-permute-done.17 = bf16[384,1024]{1,0:T(8,128)(2,1)S(1)} collective-permute-done((bf16[384,1024]{1,0:T(8,128)(2,1)S(1)}, bf16[384,1024]{1,0:T(8,128)(2,1)S(1)}, u32[]{:S(2)}, u32[]{:S(2)}) %collective-permute-start.17) | collective-permute-done | bytes 786464 | tf_op jit(solution)/shard_map/ppermute | solution.py:57
  408.2 6.3 collective-permute-done.29
  417.2 4.5 collective-permute-done.18
  427.9 7.9 collective-permute-done.32
  438.1 15.2 %collective-permute-done.33 = bf16[384,1024]{1,0:T(8,128)(2,1)S(1)} collective-permute-done((bf16[384,1024]{1,0:T(8,128)(2,1)S(1)}, bf16[384,1024]{1,0:T(8,128)(2,1)S(1)}, u32[]{:S(2)}, u32[]{:S(2)}) %collective-permute-start.33) | collective-permute-done | bytes 786464 | tf_op jit(solution)/shard_map/ppermute | solution.py:65
  454.6 19.7 %maximum_maximum_fusion.3 = bf16[768,2048]{1,0:T(8,128)(2,1)} fusion(bf16[384,1024]{1,0:T(8,128)(2,1)S(1)} %collective-permute-done.35, bf16[192,1024]{1,0:T(8,128)(2,1)S(1)} %collective-permute-done.34, bf16[192,1024]{1,0:T(8,128)(2,1)S(1)} %get-tuple-element.92, bf16[192,1024]{1,0:T(8,128)(2,1)S(1)} %get-tuple-element.90, ...), kind=kLoop, calls=%fused_computation.48 | loop fusion | flops 22020096 | bytes 6291456 | tf_op jit(solution)/shard_map/concatenate | solution.py:77
  476.2 17.1 %collective-permute-done.50 = bf16[704,512]{1,0:T(8,128)(2,1)} collective-permute-done((bf16[704,512]{1,0:T(8,128)(2,1)}, bf16[704,512]{1,0:T(8,128)(2,1)}, u32[]{:S(2)}, u32[]{:S(2)}) %collective-permute-start.50) | collective-permute-done | bytes 720928 | tf_op jit(solution)/shard_map/ppermute | solution.py:57
  495.8 6.1 pad_maximum_fusion.3
  501.9 2.7 copy-done.19
  504.6 2.8 convolution_convert_fusion.7
  507.5 16.6 %convolution_convert_fusion.1 = bf16[1408,2048]{1,0:T(8,128)(2,1)} fusion(bf16[704,1536]{1,0:T(8,128)(2,1)} %get-tuple-element.48, bf16[704,1536]{1,0:T(8,128)(2,1)} %copy-done.96, bf16[768,2048]{1,0:T(8,128)(2,1)} %collective-permute-done.15, bf16[384,1024]{1,0:T(8,128)(2,1)} %copy-done.73, bf16[192,1024]{1,0:T(8,128)(2,1)S(1)} %copy-done.62, ...), kind=kOutput, calls=%fused_computation.24 | convolution fusion | flops 8920236032 | bytes 16384000 | tf_op jit(solution)/shard_map/dot_general | solution.py:16
  527.6 3.4 maximum_select_fusion
  542.2 13.0 %fusion = (f32[2,1536]{1,0:T(2,128)S(1)}, f32[1536,1536,2]{1,0,2:T(8,128)}) fusion(f32[1536,1536,2]{1,0,2:T(8,128)} %copy-done.2, f32[2,1536]{1,0:T(2,128)S(1)} %log_add_fusion, pred[1536,1536]{0,1:T(8,128)(4,1)S(1)} %copy-done.3, bf16[1536,2,128]{0,2,1:T(8,128)(2,1)S(1)} %bitcast.232, bf16[1536,128]{0,1:T(8,128)(2,1)S(1)} %copy-done.12, ...), kind=kOutput, calls=%fused_computation.2 | convolution fusion | flops 1227813888 | bytes 41705472 | tf_op jit(solution)/shard_map/qhd,kd->hqk/dot_general | solution.py:245
  555.2 13.7 %fusion.2 = bf16[2,1536,1536]{1,2,0:T(8,128)(2,1)S(1)} fusion(f32[1536,1536,2]{1,0,2:T(8,128)} %get-tuple-element.125, f32[1536,1536,2]{1,0,2:T(8,128)} %copy-done.2, f32[2,1536]{1,0:T(2,128)S(1)} %get-tuple-element.124, f32[2,1536]{1,0:T(2,128)S(1)} %log_add_fusion, pred[1536,1536]{0,1:T(8,128)(4,1)S(1)} %copy-done.3), kind=kLoop, calls=%fused_computation.4 | loop fusion | flops 23592960 | bytes 49569792 | tf_op jit(solution)/shard_map/convert_element_type | solution.py:247
  568.9 4.0 convolution_bitcast_fusion
  572.9 12.0 %select_convert_fusion = (bf16[1536,128]{0,1:T(8,128)(2,1)}, f32[1536,128]{0,1:T(8,128)}) fusion(f32[1536,128]{0,1:T(8,128)} %convolution_bitcast_fusion, pred[]{:T(512)S(6)} %eq.48, bf16[1536,2,128]{0,2,1:T(8,128)(2,1)} %bitcast.233, f32[1536,1536,2]{1,0,2:T(8,128)} %copy-done.2, f32[2,1536]{1,0:T(2,128)S(1)} %log_add_fusion, ...), kind=kOutput, calls=%fused_computation.147 | convolution fusion | flops 1222311936 | bytes 23998464 | tf_op jit(solution)/shard_map/hqk,qhd->kd/dot_general | solution.py:250
  591.2 3.8 convolution_convert_fusion.2
  599.6 6.7 convolution_convert_fusion.6
  607.6 5.2 bitcast_convert_fusion
  613.0 23.2 %reduce-scatter.9.cloned.1.call-done = bf16[1408,512]{1,0:T(8,128)(2,1)} async-done(((bf16[1408,2048]{1,0:T(8,128)(2,1)}), bf16[1408,512]{1,0:T(8,128)(2,1)}) %reduce-scatter.9.cloned.1.call-update) | async-done | bytes 1441808 | tf_op jit(solution)/shard_map/reduce_scatter | solution.py:233
  639.3 3.4 broadcast_in_dim.90
  644.0 3.4 add_convert_fusion
  649.9 25.0 %reduce-scatter.5.cloned.1.call-done = bf16[384,512]{1,0:T(8,128)(2,1)} async-done(((bf16[384,2048]{1,0:T(8,128)(2,1)}), bf16[384,512]{1,0:T(8,128)(2,1)}) %reduce-scatter.5.cloned.1.call-update) | async-done | bytes 393232 | tf_op jit(solution)/shard_map/reduce_scatter | solution.py:257
  678.3 16.7 %collective-permute-done.44 = bf16[384,512]{1,0:T(8,128)(2,1)S(1)} collective-permute-done((bf16[384,512]{1,0:T(8,128)(2,1)}, bf16[384,512]{1,0:T(8,128)(2,1)S(1)}, u32[]{:S(2)}, u32[]{:S(2)}) %collective-permute-start.44) | collective-permute-done | bytes 393248 | tf_op jit(solution)/shard_map/ppermute | solution.py:57
  696.1 3.8 pad_maximum_fusion.5
  708.2 5.1 collective-permute-done.40
  718.7 51.4 %psum.7 = f32[2,2048]{1,0:T(2,128)S(1)} all-reduce(f32[2,2048]{1,0:T(2,128)S(1)} %pad_maximum_fusion.26), channel_id=1, replica_groups=mesh['fsdp'=4,'ctx'=4,'tp'=2] {'fsdp','ctx','tp'}, use_global_device_ids=true, to_apply=%region_15.16 | all-reduce | flops 4096 | bytes 32768 | tf_op jit(solution)/shard_map/psum | solution.py:265
  770.7 4.5 fusion.32
  783.9 3.2 maximum_select_fusion.1
  792.2 4.7 fusion.123
  796.9 3.5 convert_bitcast_fusion
  800.5 6.2 copy.72
  806.7 5.2 convert_bitcast_fusion.1
  811.9 6.2 copy.71
  (457 shorter events, 157.5 us)
Async XLA Ops:
  7.2 248.3 %copy-start = (bf16[2816,512]{1,0:T(8,128)(2,1)S(1)}, bf16[2816,512]{1,0:T(8,128)(2,1)}, u32[]{:S(2)}) copy-start(bf16[2816,512]{1,0:T(8,128)(2,1)} %param.26) | copy-start | bytes 8650756
  7.2 67.9 %all-gather.5.cloned.1.call-start = ((), (), s32[]{:S(2)}) async-start(), calls=%async_computation.4 | async-start | bytes 2621440 | tf_op jit(solution)/shard_map/all_gather | solution.py:158
  13.6 97.7 %all-gather.7.cloned.1.call-start = ((), (), s32[]{:S(2)}) async-start(), calls=%async_computation.5 | async-start | bytes 1310720 | tf_op jit(solution)/shard_map/all_gather | solution.py:165
  15.6 12.1 %collective-permute-start = (bf16[192,1024]{1,0:T(8,128)(2,1)S(1)}, bf16[192,1024]{1,0:T(8,128)(2,1)S(1)}, u32[]{:S(2)}, u32[]{:S(2)}) collective-permute-start(bf16[192,1024]{1,0:T(8,128)(2,1)S(1)} %get-tuple-element.103), channel_id=1, source_target_pairs={{0,4},{2,6},{4,0},{6,2},{1,5},{3,7},{5,1},{7,3},{8,12},{10,14},{12... | collective-permute-start | bytes 1179656 | tf_op jit(solution)/shard_map/ppermute | solution.py:57
  18.6 11.0 %collective-permute-start.2 = (bf16[192,1024]{1,0:T(8,128)(2,1)S(1)}, bf16[192,1024]{1,0:T(8,128)(2,1)S(1)}, u32[]{:S(2)}, u32[]{:S(2)}) collective-permute-start(bf16[192,1024]{1,0:T(8,128)(2,1)S(1)} %get-tuple-element.104), channel_id=1, source_target_pairs={{0,1},{1,0},{2,3},{3,2},{4,5},{5,4},{6,7},{7,6},{8,9},{9,8},{10,11... | collective-permute-start | bytes 1179656 | tf_op jit(solution)/shard_map/ppermute | solution.py:65
  27.8 18.8 %collective-permute-start.1 = (bf16[384,1024]{1,0:T(8,128)(2,1)S(1)}, bf16[384,1024]{1,0:T(8,128)(2,1)S(1)}, u32[]{:S(2)}, u32[]{:S(2)}) collective-permute-start(bf16[384,1024]{1,0:T(8,128)(2,1)S(1)} %pad_maximum_fusion.13), channel_id=1, source_target_pairs={{0,1},{1,0},{2,3},{3,2},{4,5},{5,4},{6,7},{7,6},{8,9},{9,8},{10,11... | collective-permute-start | bytes 2359304 | tf_op jit(solution)/shard_map/ppermute | solution.py:65
  29.7 18.2 %collective-permute-start.3 = (bf16[384,1024]{1,0:T(8,128)(2,1)S(1)}, bf16[384,1024]{1,0:T(8,128)(2,1)S(1)}, u32[]{:S(2)}, u32[]{:S(2)}) collective-permute-start(bf16[384,1024]{1,0:T(8,128)(2,1)S(1)} %pad_maximum_fusion.14), channel_id=1, source_target_pairs={{0,4},{2,6},{4,0},{6,2},{1,5},{3,7},{5,1},{7,3},{8,12},{10,14},{12... | collective-permute-start | bytes 2359304 | tf_op jit(solution)/shard_map/ppermute | solution.py:57
  67.5 9.4 %collective-permute-start.4 = (bf16[768,2048]{1,0:T(8,128)(2,1)}, bf16[768,2048]{1,0:T(8,128)(2,1)}, u32[]{:S(2)}, u32[]{:S(2)}) collective-permute-start(bf16[768,2048]{1,0:T(8,128)(2,1)} %maximum_maximum_fusion), channel_id=1, source_target_pairs={{0,2},{2,0},{4,6},{6,4},{1,3},{3,1},{5,7},{7,5},{8,10},{10,8},{12,... | collective-permute-start | bytes 9437192 | tf_op jit(solution)/shard_map/ppermute | solution.py:61
  69.3 194.7 %all-gather.9.cloned.1.call-start = ((), (), s32[]{:S(2)}) async-start(), calls=%async_computation.6 | async-start | bytes 7208960 | tf_op jit(solution)/shard_map/all_gather | solution.py:170
  87.7 2.5 collective-permute-start.5
  119.3 6.0 collective-permute-start.6
  123.1 193.2 %all-gather.11.cloned.1.call-start = ((), (), s32[]{:S(2)}) async-start(), calls=%async_computation.7 | async-start | bytes 3604480 | tf_op jit(solution)/shard_map/all_gather | solution.py:171
  129.7 19.6 %collective-permute-start.7 = (bf16[384,1024]{1,0:T(8,128)(2,1)S(1)}, bf16[384,1024]{1,0:T(8,128)(2,1)S(1)}, u32[]{:S(2)}, u32[]{:S(2)}) collective-permute-start(bf16[384,1024]{1,0:T(8,128)(2,1)S(1)} %slice.429), channel_id=1, source_target_pairs={{0,4},{2,6},{4,0},{6,2},{1,5},{3,7},{5,1},{7,3},{8,12},{10,14},{12... | collective-permute-start | bytes 2359304 | tf_op jit(solution)/shard_map/ppermute | solution.py:57
  131.4 19.6 %collective-permute-start.9 = (bf16[384,1024]{1,0:T(8,128)(2,1)S(1)}, bf16[384,1024]{1,0:T(8,128)(2,1)S(1)}, u32[]{:S(2)}, u32[]{:S(2)}) collective-permute-start(bf16[384,1024]{1,0:T(8,128)(2,1)S(1)} %bitcast.231), channel_id=1, source_target_pairs={{0,1},{1,0},{2,3},{3,2},{4,5},{5,4},{6,7},{7,6},{8,9},{9,8},{10,11... | collective-permute-start | bytes 2359304 | tf_op jit(solution)/shard_map/ppermute | solution.py:65
  149.7 10.5 %collective-permute-start.8 = (bf16[192,1024]{1,0:T(8,128)(2,1)S(1)}, bf16[192,1024]{1,0:T(8,128)(2,1)S(1)}, u32[]{:S(2)}, u32[]{:S(2)}) collective-permute-start(bf16[192,1024]{1,0:T(8,128)(2,1)S(1)} %slice.431), channel_id=1, source_target_pairs={{0,1},{1,0},{2,3},{3,2},{4,5},{5,4},{6,7},{7,6},{8,9},{9,8},{10,11... | collective-permute-start | bytes 1179656 | tf_op jit(solution)/shard_map/ppermute | solution.py:65
  151.4 10.2 %collective-permute-start.10 = (bf16[192,1024]{1,0:T(8,128)(2,1)S(1)}, bf16[192,1024]{1,0:T(8,128)(2,1)S(1)}, u32[]{:S(2)}, u32[]{:S(2)}) collective-permute-start(bf16[192,1024]{1,0:T(8,128)(2,1)S(1)} %slice.436), channel_id=1, source_target_pairs={{0,4},{2,6},{4,0},{6,2},{1,5},{3,7},{5,1},{7,3},{8,12},{10,14},{12... | collective-permute-start | bytes 1179656 | tf_op jit(solution)/shard_map/ppermute | solution.py:57
  163.2 9.4 %collective-permute-start.22 = (bf16[192,1024]{1,0:T(8,128)(2,1)S(1)}, bf16[192,1024]{1,0:T(8,128)(2,1)S(1)}, u32[]{:S(2)}, u32[]{:S(2)}) collective-permute-start(bf16[192,1024]{1,0:T(8,128)(2,1)S(1)} %get-tuple-element.95), channel_id=1, source_target_pairs={{0,4},{2,6},{4,0},{6,2},{1,5},{3,7},{5,1},{7,3},{8,12},{10,14},{12... | collective-permute-start | bytes 1179656 | tf_op jit(solution)/shard_map/ppermute | solution.py:57
  164.3 10.1 %collective-permute-start.24 = (bf16[192,1024]{1,0:T(8,128)(2,1)S(1)}, bf16[192,1024]{1,0:T(8,128)(2,1)S(1)}, u32[]{:S(2)}, u32[]{:S(2)}) collective-permute-start(bf16[192,1024]{1,0:T(8,128)(2,1)S(1)} %get-tuple-element.96), channel_id=1, source_target_pairs={{0,1},{1,0},{2,3},{3,2},{4,5},{5,4},{6,7},{7,6},{8,9},{9,8},{10,11... | collective-permute-start | bytes 1179656 | tf_op jit(solution)/shard_map/ppermute | solution.py:65
  172.6 20.5 %collective-permute-start.23 = (bf16[384,1024]{1,0:T(8,128)(2,1)S(1)}, bf16[384,1024]{1,0:T(8,128)(2,1)S(1)}, u32[]{:S(2)}, u32[]{:S(2)}) collective-permute-start(bf16[384,1024]{1,0:T(8,128)(2,1)S(1)} %pad_maximum_fusion.17), channel_id=1, source_target_pairs={{0,1},{1,0},{2,3},{3,2},{4,5},{5,4},{6,7},{7,6},{8,9},{9,8},{10,11... | collective-permute-start | bytes 2359304 | tf_op jit(solution)/shard_map/ppermute | solution.py:65
  174.5 20.5 %collective-permute-start.25 = (bf16[384,1024]{1,0:T(8,128)(2,1)S(1)}, bf16[384,1024]{1,0:T(8,128)(2,1)S(1)}, u32[]{:S(2)}, u32[]{:S(2)}) collective-permute-start(bf16[384,1024]{1,0:T(8,128)(2,1)S(1)} %pad_maximum_fusion.18), channel_id=1, source_target_pairs={{0,4},{2,6},{4,0},{6,2},{1,5},{3,7},{5,1},{7,3},{8,12},{10,14},{12... | collective-permute-start | bytes 2359304 | tf_op jit(solution)/shard_map/ppermute | solution.py:57
  175.4 60.2 %copy-start.39 = (bf16[192,1024]{1,0:T(8,128)(2,1)}, bf16[192,1024]{1,0:T(8,128)(2,1)S(1)}, u32[]{:S(2)}) copy-start(bf16[192,1024]{1,0:T(8,128)(2,1)S(1)} %get-tuple-element.99) | copy-start | bytes 1179652
  175.4 60.2 %copy-start.41 = (bf16[192,1024]{1,0:T(8,128)(2,1)}, bf16[192,1024]{1,0:T(8,128)(2,1)S(1)}, u32[]{:S(2)}) copy-start(bf16[192,1024]{1,0:T(8,128)(2,1)S(1)} %get-tuple-element.100) | copy-start | bytes 1179652
  175.4 39.6 %collective-permute-start.11 = (bf16[192,1024]{1,0:T(8,128)(2,1)S(1)}, bf16[192,1024]{1,0:T(8,128)(2,1)S(1)}, u32[]{:S(2)}, u32[]{:S(2)}) collective-permute-start(bf16[192,1024]{1,0:T(8,128)(2,1)S(1)} %get-tuple-element.99), channel_id=1, source_target_pairs={{0,4},{2,6},{4,0},{6,2},{1,5},{3,7},{5,1},{7,3},{8,12},{10,14},{12... | collective-permute-start | bytes 1179656 | tf_op jit(solution)/shard_map/ppermute | solution.py:57
  177.0 38.9 %collective-permute-start.13 = (bf16[192,1024]{1,0:T(8,128)(2,1)S(1)}, bf16[192,1024]{1,0:T(8,128)(2,1)S(1)}, u32[]{:S(2)}, u32[]{:S(2)}) collective-permute-start(bf16[192,1024]{1,0:T(8,128)(2,1)S(1)} %get-tuple-element.100), channel_id=1, source_target_pairs={{0,1},{1,0},{2,3},{3,2},{4,5},{5,4},{6,7},{7,6},{8,9},{9,8},{10,11... | collective-permute-start | bytes 1179656 | tf_op jit(solution)/shard_map/ppermute | solution.py:65
  215.0 41.5 %collective-permute-start.26 = (bf16[768,2048]{1,0:T(8,128)(2,1)}, bf16[768,2048]{1,0:T(8,128)(2,1)}, u32[]{:S(2)}, u32[]{:S(2)}) collective-permute-start(bf16[768,2048]{1,0:T(8,128)(2,1)} %maximum_maximum_fusion.2), channel_id=1, source_target_pairs={{0,2},{2,0},{4,6},{6,4},{1,3},{3,1},{5,7},{7,5},{8,10},{10,8},{12,... | collective-permute-start | bytes 9437192 | tf_op jit(solution)/shard_map/ppermute | solution.py:61
  215.2 20.0 %collective-permute-start.12 = (bf16[384,1024]{1,0:T(8,128)(2,1)S(1)}, bf16[384,1024]{1,0:T(8,128)(2,1)S(1)}, u32[]{:S(2)}, u32[]{:S(2)}) collective-permute-start(bf16[384,1024]{1,0:T(8,128)(2,1)S(1)} %pad_maximum_fusion.15), channel_id=1, source_target_pairs={{0,1},{1,0},{2,3},{3,2},{4,5},{5,4},{6,7},{7,6},{8,9},{9,8},{10,11... | collective-permute-start | bytes 2359304 | tf_op jit(solution)/shard_map/ppermute | solution.py:65
  215.9 19.7 %collective-permute-start.14 = (bf16[384,1024]{1,0:T(8,128)(2,1)S(1)}, bf16[384,1024]{1,0:T(8,128)(2,1)S(1)}, u32[]{:S(2)}, u32[]{:S(2)}) collective-permute-start(bf16[384,1024]{1,0:T(8,128)(2,1)S(1)} %pad_maximum_fusion.16), channel_id=1, source_target_pairs={{0,4},{2,6},{4,0},{6,2},{1,5},{3,7},{5,1},{7,3},{8,12},{10,14},{12... | collective-permute-start | bytes 2359304 | tf_op jit(solution)/shard_map/ppermute | solution.py:57
  255.4 8.6 %collective-permute-start.15 = (bf16[768,2048]{1,0:T(8,128)(2,1)}, bf16[768,2048]{1,0:T(8,128)(2,1)}, u32[]{:S(2)}, u32[]{:S(2)}) collective-permute-start(bf16[768,2048]{1,0:T(8,128)(2,1)} %maximum_maximum_fusion.1), channel_id=1, source_target_pairs={{0,2},{2,0},{4,6},{6,4},{1,3},{3,1},{5,7},{7,5},{8,10},{10,8},{12,... | collective-permute-start | bytes 9437192 | tf_op jit(solution)/shard_map/ppermute | solution.py:61
  256.5 217.9 %reduce-scatter.11.cloned.1.call-start = ((), (), s32[]{:S(2)}) async-start(), calls=%async_computation.11 | async-start | bytes 3604480 | tf_op jit(solution)/shard_map/reduce_scatter | solution.py:234
  347.0 15.7 %collective-permute-start.27 = (bf16[768,2048]{1,0:T(8,128)(2,1)}, bf16[768,2048]{1,0:T(8,128)(2,1)}, u32[]{:S(2)}, u32[]{:S(2)}) collective-permute-start(bf16[768,2048]{1,0:T(8,128)(2,1)} %slice.460), channel_id=1, source_target_pairs={{0,2},{2,0},{4,6},{6,4},{1,3},{3,1},{5,7},{7,5},{8,10},{10,8},{12,... | collective-permute-start | bytes 9437192 | tf_op jit(solution)/shard_map/ppermute | solution.py:61
  355.9 14.4 %collective-permute-start.16 = (bf16[768,2048]{1,0:T(8,128)(2,1)}, bf16[768,2048]{1,0:T(8,128)(2,1)}, u32[]{:S(2)}, u32[]{:S(2)}) collective-permute-start(bf16[768,2048]{1,0:T(8,128)(2,1)} %slice.445), channel_id=1, source_target_pairs={{0,2},{2,0},{4,6},{6,4},{1,3},{3,1},{5,7},{7,5},{8,10},{10,8},{12,... | collective-permute-start | bytes 9437192 | tf_op jit(solution)/shard_map/ppermute | solution.py:61
  362.6 235.9 %reduce-scatter.7.cloned.1.call-start = ((), (), s32[]{:S(2)}) async-start(), calls=%async_computation.9 | async-start | bytes 1310720 | tf_op jit(solution)/shard_map/reduce_scatter | solution.py:241
  367.1 20.5 %collective-permute-start.28 = (bf16[384,1024]{1,0:T(8,128)(2,1)S(1)}, bf16[384,1024]{1,0:T(8,128)(2,1)S(1)}, u32[]{:S(2)}, u32[]{:S(2)}) collective-permute-start(bf16[384,1024]{1,0:T(8,128)(2,1)S(1)} %slice.462), channel_id=1, source_target_pairs={{0,4},{2,6},{4,0},{6,2},{1,5},{3,7},{5,1},{7,3},{8,12},{10,14},{12... | collective-permute-start | bytes 2359304 | tf_op jit(solution)/shard_map/ppermute | solution.py:57
  368.7 20.7 %collective-permute-start.30 = (bf16[384,1024]{1,0:T(8,128)(2,1)S(1)}, bf16[384,1024]{1,0:T(8,128)(2,1)S(1)}, u32[]{:S(2)}, u32[]{:S(2)}) collective-permute-start(bf16[384,1024]{1,0:T(8,128)(2,1)S(1)} %bitcast.230), channel_id=1, source_target_pairs={{0,1},{1,0},{2,3},{3,2},{4,5},{5,4},{6,7},{7,6},{8,9},{9,8},{10,11... | collective-permute-start | bytes 2359304 | tf_op jit(solution)/shard_map/ppermute | solution.py:65
  374.7 29.7 %collective-permute-start.17 = (bf16[384,1024]{1,0:T(8,128)(2,1)S(1)}, bf16[384,1024]{1,0:T(8,128)(2,1)S(1)}, u32[]{:S(2)}, u32[]{:S(2)}) collective-permute-start(bf16[384,1024]{1,0:T(8,128)(2,1)S(1)} %slice.447), channel_id=1, source_target_pairs={{0,4},{2,6},{4,0},{6,2},{1,5},{3,7},{5,1},{7,3},{8,12},{10,14},{12... | collective-permute-start | bytes 2359304 | tf_op jit(solution)/shard_map/ppermute | solution.py:57
  375.4 30.9 %collective-permute-start.19 = (bf16[384,1024]{1,0:T(8,128)(2,1)S(1)}, bf16[384,1024]{1,0:T(8,128)(2,1)S(1)}, u32[]{:S(2)}, u32[]{:S(2)}) collective-permute-start(bf16[384,1024]{1,0:T(8,128)(2,1)S(1)} %bitcast.229), channel_id=1, source_target_pairs={{0,1},{1,0},{2,3},{3,2},{4,5},{5,4},{6,7},{7,6},{8,9},{9,8},{10,11... | collective-permute-start | bytes 2359304 | tf_op jit(solution)/shard_map/ppermute | solution.py:65
  387.9 26.6 %collective-permute-start.29 = (bf16[192,1024]{1,0:T(8,128)(2,1)S(1)}, bf16[192,1024]{1,0:T(8,128)(2,1)S(1)}, u32[]{:S(2)}, u32[]{:S(2)}) collective-permute-start(bf16[192,1024]{1,0:T(8,128)(2,1)S(1)} %slice.464), channel_id=1, source_target_pairs={{0,1},{1,0},{2,3},{3,2},{4,5},{5,4},{6,7},{7,6},{8,9},{9,8},{10,11... | collective-permute-start | bytes 1179656 | tf_op jit(solution)/shard_map/ppermute | solution.py:65
  389.8 25.8 %collective-permute-start.31 = (bf16[192,1024]{1,0:T(8,128)(2,1)S(1)}, bf16[192,1024]{1,0:T(8,128)(2,1)S(1)}, u32[]{:S(2)}, u32[]{:S(2)}) collective-permute-start(bf16[192,1024]{1,0:T(8,128)(2,1)S(1)} %slice.469), channel_id=1, source_target_pairs={{0,4},{2,6},{4,0},{6,2},{1,5},{3,7},{5,1},{7,3},{8,12},{10,14},{12... | collective-permute-start | bytes 1179656 | tf_op jit(solution)/shard_map/ppermute | solution.py:57
  404.8 16.9 %collective-permute-start.18 = (bf16[192,1024]{1,0:T(8,128)(2,1)S(1)}, bf16[192,1024]{1,0:T(8,128)(2,1)S(1)}, u32[]{:S(2)}, u32[]{:S(2)}) collective-permute-start(bf16[192,1024]{1,0:T(8,128)(2,1)S(1)} %slice.449), channel_id=1, source_target_pairs={{0,1},{1,0},{2,3},{3,2},{4,5},{5,4},{6,7},{7,6},{8,9},{9,8},{10,11... | collective-permute-start | bytes 1179656 | tf_op jit(solution)/shard_map/ppermute | solution.py:65
  406.7 16.0 %collective-permute-start.20 = (bf16[192,1024]{1,0:T(8,128)(2,1)S(1)}, bf16[192,1024]{1,0:T(8,128)(2,1)S(1)}, u32[]{:S(2)}, u32[]{:S(2)}) collective-permute-start(bf16[192,1024]{1,0:T(8,128)(2,1)S(1)} %slice.454), channel_id=1, source_target_pairs={{0,4},{2,6},{4,0},{6,2},{1,5},{3,7},{5,1},{7,3},{8,12},{10,14},{12... | collective-permute-start | bytes 1179656 | tf_op jit(solution)/shard_map/ppermute | solution.py:57
  425.8 10.0 %collective-permute-start.32 = (bf16[192,1024]{1,0:T(8,128)(2,1)S(1)}, bf16[192,1024]{1,0:T(8,128)(2,1)S(1)}, u32[]{:S(2)}, u32[]{:S(2)}) collective-permute-start(bf16[192,1024]{1,0:T(8,128)(2,1)S(1)} %get-tuple-element.91), channel_id=1, source_target_pairs={{0,4},{2,6},{4,0},{6,2},{1,5},{3,7},{5,1},{7,3},{8,12},{10,14},{12... | collective-permute-start | bytes 1179656 | tf_op jit(solution)/shard_map/ppermute | solution.py:57
  426.5 10.9 %collective-permute-start.34 = (bf16[192,1024]{1,0:T(8,128)(2,1)S(1)}, bf16[192,1024]{1,0:T(8,128)(2,1)S(1)}, u32[]{:S(2)}, u32[]{:S(2)}) collective-permute-start(bf16[192,1024]{1,0:T(8,128)(2,1)S(1)} %get-tuple-element.92), channel_id=1, source_target_pairs={{0,1},{1,0},{2,3},{3,2},{4,5},{5,4},{6,7},{7,6},{8,9},{9,8},{10,11... | collective-permute-start | bytes 1179656 | tf_op jit(solution)/shard_map/ppermute | solution.py:65
  435.8 17.5 %collective-permute-start.33 = (bf16[384,1024]{1,0:T(8,128)(2,1)S(1)}, bf16[384,1024]{1,0:T(8,128)(2,1)S(1)}, u32[]{:S(2)}, u32[]{:S(2)}) collective-permute-start(bf16[384,1024]{1,0:T(8,128)(2,1)S(1)} %pad_maximum_fusion.19), channel_id=1, source_target_pairs={{0,1},{1,0},{2,3},{3,2},{4,5},{5,4},{6,7},{7,6},{8,9},{9,8},{10,11... | collective-permute-start | bytes 2359304 | tf_op jit(solution)/shard_map/ppermute | solution.py:65
  437.5 17.2 %collective-permute-start.35 = (bf16[384,1024]{1,0:T(8,128)(2,1)S(1)}, bf16[384,1024]{1,0:T(8,128)(2,1)S(1)}, u32[]{:S(2)}, u32[]{:S(2)}) collective-permute-start(bf16[384,1024]{1,0:T(8,128)(2,1)S(1)} %pad_maximum_fusion.20), channel_id=1, source_target_pairs={{0,4},{2,6},{4,0},{6,2},{1,5},{3,7},{5,1},{7,3},{8,12},{10,14},{12... | collective-permute-start | bytes 2359304 | tf_op jit(solution)/shard_map/ppermute | solution.py:57
  474.4 21.4 %collective-permute-start.36 = (bf16[768,2048]{1,0:T(8,128)(2,1)}, bf16[768,2048]{1,0:T(8,128)(2,1)}, u32[]{:S(2)}, u32[]{:S(2)}) collective-permute-start(bf16[768,2048]{1,0:T(8,128)(2,1)} %maximum_maximum_fusion.3), channel_id=1, source_target_pairs={{0,2},{2,0},{4,6},{6,4},{1,3},{3,1},{5,7},{7,5},{8,10},{10,8},{12,... | collective-permute-start | bytes 9437192 | tf_op jit(solution)/shard_map/ppermute | solution.py:61
  474.4 18.9 %collective-permute-start.50 = (bf16[704,512]{1,0:T(8,128)(2,1)}, bf16[704,512]{1,0:T(8,128)(2,1)}, u32[]{:S(2)}, u32[]{:S(2)}) collective-permute-start(bf16[704,512]{1,0:T(8,128)(2,1)} %reduce-scatter.11.cloned.1.call-done), channel_id=1, source_target_pairs={{0,4},{2,6},{4,0},{6,2},{1,5},{3,7},{5,1},{7,3},{8,12},{10,14},{12... | collective-permute-start | bytes 2162696 | tf_op jit(solution)/shard_map/ppermute | solution.py:57
  475.0 52.5 %collective-permute-start.21 = (bf16[192,2048]{1,0:T(8,128)(2,1)}, bf16[192,2048]{1,0:T(8,128)(2,1)}, u32[]{:S(2)}, u32[]{:S(2)}) collective-permute-start(bf16[192,2048]{1,0:T(8,128)(2,1)} %get-tuple-element.62), channel_id=1, source_target_pairs={{0,1},{1,0},{2,3},{3,2},{4,5},{5,4},{6,7},{7,6},{8,9},{9,8},{10,11... | collective-permute-start | bytes 2359304 | tf_op jit(solution)/shard_map/ppermute | solution.py:65
  495.8 40.0 %collective-permute-start.51 = (bf16[2,704,512]{2,1,0:T(8,128)(2,1)}, bf16[2,704,512]{2,1,0:T(8,128)(2,1)}, u32[]{:S(2)}, u32[]{:S(2)}) collective-permute-start(bf16[2,704,512]{2,1,0:T(8,128)(2,1)} %pad_maximum_fusion.11), channel_id=1, source_target_pairs={{0,2},{2,0},{4,6},{6,4},{1,3},{3,1},{5,7},{7,5},{8,10},{10,8},{12,... | collective-permute-start | bytes 4325384 | tf_op jit(solution)/shard_map/ppermute | solution.py:61
  507.4 128.7 %reduce-scatter.9.cloned.1.call-start = ((), (), s32[]{:S(2)}) async-start(), calls=%async_computation.10 | async-start | bytes 7208960 | tf_op jit(solution)/shard_map/reduce_scatter | solution.py:233
  524.2 150.7 %reduce-scatter.5.cloned.1.call-start = ((), (), s32[]{:S(2)}) async-start(), calls=%async_computation.8 | async-start | bytes 1966080 | tf_op jit(solution)/shard_map/reduce_scatter | solution.py:257
  584.9 4.1 collective-permute-start.37
  598.6 45.4 %collective-permute-start.38 = (bf16[768,2048]{1,0:T(8,128)(2,1)}, bf16[768,2048]{1,0:T(8,128)(2,1)}, u32[]{:S(2)}, u32[]{:S(2)}) collective-permute-start(bf16[768,2048]{1,0:T(8,128)(2,1)} %slice.483), channel_id=1, source_target_pairs={{0,2},{2,0},{4,6},{6,4},{1,3},{3,1},{5,7},{7,5},{8,10},{10,8},{12,... | collective-permute-start | bytes 9437192 | tf_op jit(solution)/shard_map/ppermute | solution.py:61
  598.6 8.9 %collective-permute-start.46 = (bf16[256,512]{1,0:T(8,128)(2,1)}, bf16[256,512]{1,0:T(8,128)(2,1)S(1)}, u32[]{:S(2)}, u32[]{:S(2)}) collective-permute-start(bf16[256,512]{1,0:T(8,128)(2,1)} %reduce-scatter.7.cloned.1.call-done), channel_id=1, source_target_pairs={{0,4},{2,6},{4,0},{6,2},{1,5},{3,7},{5,1},{7,3},{8,12},{10,14},{12... | collective-permute-start | bytes 786440 | tf_op jit(solution)/shard_map/ppermute | solution.py:57
  607.6 30.0 %collective-permute-start.47 = (bf16[2,256,512]{2,1,0:T(8,128)(2,1)S(1)}, bf16[2,256,512]{2,1,0:T(8,128)(2,1)S(1)}, u32[]{:S(2)}, u32[]{:S(2)}) collective-permute-start(bf16[2,256,512]{2,1,0:T(8,128)(2,1)S(1)} %pad_maximum_fusion.24), channel_id=1, source_target_pairs={{0,2},{2,0},{4,6},{6,4},{1,3},{3,1},{5,7},{7,5},{8,10},{10,8},{12,... | collective-permute-start | bytes 1572872 | tf_op jit(solution)/shard_map/ppermute | solution.py:61
  636.1 59.9 %collective-permute-start.48 = (bf16[1408,512]{1,0:T(8,128)(2,1)}, bf16[1408,512]{1,0:T(8,128)(2,1)}, u32[]{:S(2)}, u32[]{:S(2)}) collective-permute-start(bf16[1408,512]{1,0:T(8,128)(2,1)} %reduce-scatter.9.cloned.1.call-done), channel_id=1, source_target_pairs={{0,4},{2,6},{4,0},{6,2},{1,5},{3,7},{5,1},{7,3},{8,12},{10,14},{12... | collective-permute-start | bytes 4325384 | tf_op jit(solution)/shard_map/ppermute | solution.py:57
  649.5 50.9 %collective-permute-start.39 = (bf16[384,1024]{1,0:T(8,128)(2,1)}, bf16[384,1024]{1,0:T(8,128)(2,1)}, u32[]{:S(2)}, u32[]{:S(2)}) collective-permute-start(bf16[384,1024]{1,0:T(8,128)(2,1)} %slice.485), channel_id=1, source_target_pairs={{0,4},{2,6},{4,0},{6,2},{1,5},{3,7},{5,1},{7,3},{8,12},{10,14},{12... | collective-permute-start | bytes 2359304 | tf_op jit(solution)/shard_map/ppermute | solution.py:57
  674.9 20.1 %collective-permute-start.44 = (bf16[384,512]{1,0:T(8,128)(2,1)}, bf16[384,512]{1,0:T(8,128)(2,1)S(1)}, u32[]{:S(2)}, u32[]{:S(2)}) collective-permute-start(bf16[384,512]{1,0:T(8,128)(2,1)} %reduce-scatter.5.cloned.1.call-done), channel_id=1, source_target_pairs={{0,4},{2,6},{4,0},{6,2},{1,5},{3,7},{5,1},{7,3},{8,12},{10,14},{12... | collective-permute-start | bytes 1179656 | tf_op jit(solution)/shard_map/ppermute | solution.py:57
  676.6 27.1 %collective-permute-start.41 = (bf16[384,1024]{1,0:T(8,128)(2,1)S(1)}, bf16[384,1024]{1,0:T(8,128)(2,1)S(1)}, u32[]{:S(2)}, u32[]{:S(2)}) collective-permute-start(bf16[384,1024]{1,0:T(8,128)(2,1)S(1)} %bitcast.228), channel_id=1, source_target_pairs={{0,1},{1,0},{2,3},{3,2},{4,5},{5,4},{6,7},{7,6},{8,9},{9,8},{10,11... | collective-permute-start | bytes 2359304 | tf_op jit(solution)/shard_map/ppermute | solution.py:65
  696.0 79.2 %collective-permute-start.45 = (bf16[2,384,512]{2,1,0:T(8,128)(2,1)}, bf16[2,384,512]{2,1,0:T(8,128)(2,1)}, u32[]{:S(2)}, u32[]{:S(2)}) collective-permute-start(bf16[2,384,512]{2,1,0:T(8,128)(2,1)} %pad_maximum_fusion.21), channel_id=1, source_target_pairs={{0,2},{2,0},{4,6},{6,4},{1,3},{3,1},{5,7},{7,5},{8,10},{10,8},{12,... | collective-permute-start | bytes 2359304 | tf_op jit(solution)/shard_map/ppermute | solution.py:61
  699.9 87.2 %collective-permute-start.49 = (bf16[2,1408,512]{2,1,0:T(8,128)(2,1)}, bf16[2,1408,512]{2,1,0:T(8,128)(2,1)}, u32[]{:S(2)}, u32[]{:S(2)}) collective-permute-start(bf16[2,1408,512]{2,1,0:T(8,128)(2,1)} %pad_maximum_fusion.5), channel_id=1, source_target_pairs={{0,2},{2,0},{4,6},{6,4},{1,3},{3,1},{5,7},{7,5},{8,10},{10,8},{12,... | collective-permute-start | bytes 8650760 | tf_op jit(solution)/shard_map/ppermute | solution.py:61
  702.1 11.1 %collective-permute-start.40 = (bf16[192,1024]{1,0:T(8,128)(2,1)S(1)}, bf16[192,1024]{1,0:T(8,128)(2,1)S(1)}, u32[]{:S(2)}, u32[]{:S(2)}) collective-permute-start(bf16[192,1024]{1,0:T(8,128)(2,1)S(1)} %slice.487), channel_id=1, source_target_pairs={{0,1},{1,0},{2,3},{3,2},{4,5},{5,4},{6,7},{7,6},{8,9},{9,8},{10,11... | collective-permute-start | bytes 1179656 | tf_op jit(solution)/shard_map/ppermute | solution.py:65
  704.1 10.8 %collective-permute-start.42 = (bf16[192,1024]{1,0:T(8,128)(2,1)S(1)}, bf16[192,1024]{1,0:T(8,128)(2,1)S(1)}, u32[]{:S(2)}, u32[]{:S(2)}) collective-permute-start(bf16[192,1024]{1,0:T(8,128)(2,1)S(1)} %slice.492), channel_id=1, source_target_pairs={{0,4},{2,6},{4,0},{6,2},{1,5},{3,7},{5,1},{7,3},{8,12},{10,14},{12... | collective-permute-start | bytes 1179656 | tf_op jit(solution)/shard_map/ppermute | solution.py:57
  715.9 54.8 %copy-start.16 = (f32[1,192,1024]{2,1,0:T(8,128)S(1)}, f32[1,192,1024]{2,1,0:T(8,128)}, u32[]{:S(2)}) copy-start(f32[1,192,1024]{2,1,0:T(8,128)} %get-tuple-element.81) | copy-start | bytes 2359300
  717.8 66.1 %collective-permute-start.43 = (bf16[192,2048]{1,0:T(8,128)(2,1)}, bf16[192,2048]{1,0:T(8,128)(2,1)}, u32[]{:S(2)}, u32[]{:S(2)}) collective-permute-start(bf16[192,2048]{1,0:T(8,128)(2,1)} %fusion.38), channel_id=1, source_target_pairs={{0,1},{1,0},{2,3},{3,2},{4,5},{5,4},{6,7},{7,6},{8,9},{9,8},{10,11... | collective-permute-start | bytes 2359304 | tf_op jit(solution)/shard_map/ppermute | solution.py:65
  (99 other events, 1204.4 us)
Sparse Core Ops, SparseCore 0:
  13.7 48.6 all-gather.4
  69.4 28.4 all-gather.6
  123.2 107.1 all-gather.8
  256.5 59.6 all-gather.10
  362.7 54.8 reduce-scatter.10
  507.5 24.5 reduce-scatter.6
  535.2 100.9 reduce-scatter.8
  639.1 35.7 reduce-scatter.4

commit v2 on v1

v2 whole, which is shorter than its diff:
```python
import functools
import math

import jax
import jax.numpy as jnp
from jax import lax
from jax.experimental import pallas as pl
from jax.experimental.pallas import tpu as pltpu
from jax.sharding import PartitionSpec as P

HEAD = 128
norm_eps = 1e-05
rope_base = 10000.0
F32 = jnp.float32
BF16 = jnp.bfloat16
ANY_VMEM = pl.BlockSpec(memory_space=pltpu.VMEM)
ANY_SMEM = pl.BlockSpec(memory_space=pltpu.SMEM)


def dot(a, b, ca, cb):
    return lax.dot_general(a, b, (((ca,), (cb,)), ((), ())), preferred_element_type=F32)


def after(v, *others):
    return lax.optimization_barrier((v,) + others)[0] if others else v


def fenced(flag, stage, *values):
    shapes = jax.eval_shape(stage, *values)

    def empty(*_):
        return jax.tree.map(lambda a: jnp.zeros(a.shape, a.dtype), shapes)

    return lax.cond(flag, stage, empty, *values)


def norm_back(d_normed, hat, inv_rms, gain):
    scaled = d_normed * gain
    return inv_rms * (scaled - hat * jnp.mean(scaled * hat, axis=-1, keepdims=True))


def far(v):
    return lax.ppermute(v, "ctx", [(i, i ^ 2) for i in range(4)])


def near(v):
    return lax.ppermute(v, "ctx", [(i, i ^ 1) for i in range(4)])


def side(v):
    return lax.ppermute(v, "tp", [(0, 1), (1, 0)])


def join_kernel(count, *refs):
    pieces, out_ref, sem = refs[:count], refs[-2], refs[-1]
    copies, row = [], 0
    for k, piece in enumerate(pieces):
        n = piece.shape[0]
        copies.append(pltpu.make_async_copy(piece, out_ref.at[pl.ds(row, n), :], sem.at[k]))
        copies[-1].start()
        row += n
    for copy in copies:
        copy.wait()


def join(*pieces, others=()):
    rows = sum(p.shape[0] for p in pieces)
    return pl.pallas_call(
        functools.partial(join_kernel, len(pieces)),
        out_shape=jax.ShapeDtypeStruct((rows, pieces[0].shape[1]), pieces[0].dtype),
        in_specs=[pl.BlockSpec(memory_space=pl.ANY)] * (len(pieces) + len(others)),
        out_specs=ANY_VMEM,
        scratch_shapes=[pltpu.SemaphoreType.DMA((len(pieces),))],
        name="join",
    )(*pieces, *others)


def spread_start(v):
    h = v.shape[0] // 2
    one, two = v[:h], v[h:]
    return one, two, far(one), side(two), side(one), far(two)


def spread_more(parts):
    one, two, one_far, two_side, one_side, two_far = parts
    return one_far, two_side, one_side, two_far, side(one_far), far(two_side)


def spread_join(ready, others=()):
    one, two, one_far, two_side, one_side, two_far, one_both, two_both = ready
    return join(one, one_far, one_side, one_both, two, two_side, two_far, two_both, others=others)


def spread(v, others=()):
    parts = spread_start(v)
    mine = spread_join(parts[:2] + spread_more(parts), others)
    return mine, near(mine)


def arrival_starts(c, t, tok_rows):
    own = tok_rows // 2
    starts = []
    for near_bit in range(2):
        for second in range(2):
            order = ((0, 0), (1, 0), (0, 1), (1, 1)) if second == 0 else ((0, 0), (0, 1), (1, 0), (1, 1))
            for far_bit, side_bit in order:
                ctx = c ^ (near_bit + 2 * far_bit)
                starts.append(ctx * tok_rows + (t ^ side_bit) * own + second * (own // 2))
    return starts


def collect_split(both):
    h = both.shape[0] // 8
    one = both[: 4 * h].reshape(2, 2, h, -1)
    two = both[4 * h :].reshape(2, 2, h, -1)
    return [v[:, k].reshape(2 * h, -1) for k in range(2) for v in (one, two)]


def collect_send(split):
    one, two, one_sent, two_sent = split
    return one, two, far(one_sent), side(two_sent)


def collect_first(both):
    return collect_send(collect_split(both))


def collect_second(state):
    one, two, one_far, two_side = state
    return add(one, one_far), add(two, two_side)


def collect_start(p_mine, p_other):
    return collect_second(collect_first(join_cores(p_mine, p_other)))


def join_cores(p_mine, p_other):
    return add(lax.optimization_barrier(p_mine), near(p_other))


def collect_end(state):
    one, two = state
    h = one.shape[0] // 2
    one_side = side(one[h:])
    two_far = far(two[h:])
    return jnp.concatenate(
        [
            one[:h].astype(F32) + one_side.astype(F32),
            two[:h].astype(F32) + two_far.astype(F32),
        ],
        axis=0,
    )


def collect(p_mine, p_other):
    return collect_end(collect_start(p_mine, p_other))


def in_order(v, other, t):
    return jnp.where(
        t == 0, jnp.concatenate([v, other], axis=0), jnp.concatenate([other, v], axis=0)
    )


def gather_whole(v):
    return lax.all_gather(v, "fsdp", axis=1, tiled=True)


def scatter_whole(g):
    return lax.psum_scatter(g, "fsdp", scatter_dimension=1, tiled=True)


def add(a, b):
    return (a.astype(F32) + b.astype(F32)).astype(BF16)


def pack_first_kernel(at_ref, wq_ref, wk_ref, wv_ref, wo_ref, one_ref, two_ref, out_ref):
    q_cols = wq_ref.shape[1]
    qkv = q_cols + HEAD
    out_ref[:q_cols, :] = wq_ref[...].astype(F32).T.astype(BF16)
    w_kv = jnp.where(at_ref[1] == 0, wk_ref[...].astype(F32), wv_ref[...].astype(F32))
    out_ref[q_cols:qkv, :] = w_kv.T.astype(BF16)
    row = lax.broadcasted_iota(jnp.int32, (16, out_ref.shape[1]), 0)
    one, two = one_ref[...].astype(F32)[None, :], two_ref[...].astype(F32)[None, :]
    out_ref[qkv : qkv + 16, :] = jnp.where(row == 0, one, jnp.where(row == 1, two, 0.0)).astype(BF16)
    out_ref[qkv + 16 :, :] = wo_ref[...]


def pack_first(at, w_query, w_key, w_value, w_out, gain_one, gain_two):
    depth = w_query.shape[0]
    q_cols = w_query.shape[1] // 4
    rows = 2 * q_cols + HEAD + 16
    gain = pl.BlockSpec((depth,), lambda i, at: (0,))
    return pl.pallas_call(
        pack_first_kernel,
        out_shape=jax.ShapeDtypeStruct((rows, depth), BF16),
        grid_spec=pltpu.PrefetchScalarGridSpec(
            num_scalar_prefetch=1,
            grid=(1,),
            in_specs=[
                pl.BlockSpec((depth, q_cols), lambda i, at: (0, at[0])),
                pl.BlockSpec((depth, HEAD), lambda i, at: (0, at[2])),
                pl.BlockSpec((depth, HEAD), lambda i, at: (0, at[2])),
                pl.BlockSpec((q_cols, depth), lambda i, at: (at[0], 0)),
                gain,
                gain,
            ],
            out_specs=pl.BlockSpec((rows, depth), lambda i, at: (0, 0)),
        ),
        name="pack_first",
    )(at, w_query, w_key, w_value, w_out, gain_one, gain_two)


def turn(u, cosine, sine):
    return u * cosine + pltpu.roll(u, HEAD // 2, 1) * sine


def qkv_kernel(heads, core_ref, x_ref, w_ref, gain_ref, cos_ref, sin_ref, n1_ref, q_ref, kv_ref):
    x = x_ref[...].astype(F32)
    inv = lax.rsqrt(jnp.mean(x * x, axis=-1, keepdims=True) + norm_eps)
    n1 = (x * inv * gain_ref[0:1, :].astype(F32)).astype(BF16)
    n1_ref[...] = n1
    pre = dot(n1, w_ref[...], 1, 1)
    cosine, sine = cos_ref[...], sin_ref[...]
    scale = 1.0 / math.sqrt(HEAD)
    for h in range(heads):
        u = pre[:, h * HEAD : (h + 1) * HEAD]
        q_ref[:, h * HEAD : (h + 1) * HEAD] = (turn(u, cosine, sine) * scale).astype(BF16)
    u = pre[:, heads * HEAD :]
    kv_ref[...] = jnp.where(core_ref[0] == 0, turn(u, cosine, sine), u).astype(BF16)


def qkv_half(core, x, first, cols, cosine, sine):
    rows, width = x.shape
    heads = cols // HEAD - 1
    tile = rows // 3
    return pl.pallas_call(
        functools.partial(qkv_kernel, heads),
        out_shape=(
            jax.ShapeDtypeStruct((rows, width), BF16),
            jax.ShapeDtypeStruct((rows, heads * HEAD), BF16),
            jax.ShapeDtypeStruct((rows, HEAD), BF16),
        ),
        grid=(rows // tile,),
        in_specs=[
            ANY_SMEM,
            pl.BlockSpec((tile, width), lambda r: (r, 0)),
            pl.BlockSpec((cols, width), lambda r: (0, 0)),
            pl.BlockSpec((16, width), lambda r: (cols // 16, 0)),
            pl.BlockSpec((tile, HEAD), lambda r: (r, 0)),
            pl.BlockSpec((tile, HEAD), lambda r: (r, 0)),
        ],
        out_specs=(
            pl.BlockSpec((tile, width), lambda r: (r, 0)),
            pl.BlockSpec((tile, heads * HEAD), lambda r: (r, 0)),
            pl.BlockSpec((tile, HEAD), lambda r: (r, 0)),
        ),
        cost_estimate=pl.CostEstimate(
            flops=2 * rows * width * cols, bytes_accessed=rows * width * 4 + cols * width * 2, transcendentals=0
        ),
        name="qkv",
    )(core, x, first, first, cosine, sine)


def to_order(starts_ref, mine, other, dest, block):
    per = mine.shape[0] // block
    for a in range(2 * per):
        src = mine if a < per else other
        at = pl.multiple_of(starts_ref[a], block)
        row = (a % per) * block
        for h in range(dest.shape[0]):
            dest[h, pl.ds(at, block), :] = src[row : row + block, h * HEAD : (h + 1) * HEAD]


def keys_in_order(starts_ref, own, got, k_n, v_n, block):
    @pl.when(starts_ref[16] == 0)
    def _():
        to_order(starts_ref, *own, k_n, block)
        to_order(starts_ref, *got, v_n, block)

    @pl.when(starts_ref[16] != 0)
    def _():
        to_order(starts_ref, *own, v_n, block)
        to_order(starts_ref, *got, k_n, block)


def over_queries(heads, seq, slot, step, visit):
    per = slot // step
    for first in range(0, seq, slot):

        def one(i, carry):
            visit(i // per, pl.multiple_of(first + lax.rem(i, per) * step, step), first + slot)
            return carry

        lax.fori_loop(0, heads * per, one, 0)


def attn_forward_kernel(
    slot, block, starts_ref, qm, qo, km, ko, rm, ro, lo_ref, hi_ref, om, oo, lse_ref, q_n, k_n, v_n, o_n, vt_n
):
    heads, seq, _ = q_n.shape
    to_order(starts_ref, qm, qo, q_n, block)
    keys_in_order(starts_ref, (km, ko), (rm, ro), k_n, v_n, block)
    vt_n[...] = v_n[0].astype(F32).T.astype(BF16)
    step = 256

    def visit(h, row, nk):
        rows = pl.ds(row, step)
        s = dot(k_n[0, :nk, :], q_n[h, rows, :], 1, 1)
        j = lax.broadcasted_iota(jnp.int32, s.shape, 0)
        ok = (j >= lo_ref[:, rows]) & (j <= hi_ref[:, rows])
        s = jnp.where(ok, s, -1e30)
        top = jnp.max(s, axis=0, keepdims=True)
        e = jnp.exp(s - top)
        total = jnp.sum(e, axis=0, keepdims=True)
        soft = (e * (1.0 / total)).astype(BF16)
        out = dot(vt_n[:, :nk], soft, 1, 0)
        o_n[h, rows, :] = out.T.astype(BF16)
        lse_ref[h, :, rows] = top + jnp.log(total)

    over_queries(heads, seq, slot, step, visit)
    per = om.shape[0] // block
    for a in range(2 * per):
        dest = om if a < per else oo
        row = (a % per) * block
        for h in range(heads):
            dest[row : row + block, h * HEAD : (h + 1) * HEAD] = o_n[
                h, pl.ds(pl.multiple_of(starts_ref[a], block), block), :
            ]


def attn_forward(starts, q, own, got, lo, hi, slot):
    half, q_cols = q[0].shape
    heads = q_cols // HEAD
    seq = 2 * half
    return pl.pallas_call(
        functools.partial(attn_forward_kernel, slot, seq // 16),
        out_shape=(
            jax.ShapeDtypeStruct((half, q_cols), BF16),
            jax.ShapeDtypeStruct((half, q_cols), BF16),
            jax.ShapeDtypeStruct((heads, 1, seq), F32),
        ),
        in_specs=[ANY_SMEM] + [ANY_VMEM] * 8,
        out_specs=(ANY_VMEM, ANY_VMEM, ANY_VMEM),
        scratch_shapes=[
            pltpu.VMEM((heads, seq, HEAD), BF16),
            pltpu.VMEM((1, seq, HEAD), BF16),
            pltpu.VMEM((1, seq, HEAD), BF16),
            pltpu.VMEM((heads, seq, HEAD), BF16),
            pltpu.VMEM((HEAD, seq), BF16),
        ],
        cost_estimate=pl.CostEstimate(
            flops=12 * seq * seq * q_cols, bytes_accessed=seq * q_cols * 8, transcendentals=heads * seq * seq
        ),
        name="attn_forward",
    )(starts, q[0], q[1], own[0], own[1], got[0], got[1], lo, hi)


def attn_backward_kernel(
    slot, block, starts_ref, qm, qo, km, ko, rm, ro, dom, doo, om, oo, lse_ref, lo_ref, hi_ref, cos_ref, sin_ref,
    dqm, dqo, keepm, keepo, sendm, sendo, q_n, k_n, v_n, do_n, o_n, kt_n, dq_n, dk_n, dv_n,
):
    heads, seq, _ = q_n.shape
    to_order(starts_ref, qm, qo, q_n, block)
    to_order(starts_ref, dom, doo, do_n, block)
    to_order(starts_ref, om, oo, o_n, block)
    keys_in_order(starts_ref, (km, ko), (rm, ro), k_n, v_n, block)
    kt_n[...] = k_n[0].astype(F32).T.astype(BF16)
    dk_n[...] = jnp.zeros_like(dk_n)
    dv_n[...] = jnp.zeros_like(dv_n)
    step = slot

    def visit(h, row, nk):
        rows = pl.ds(row, step)
        q = q_n[h, rows, :]
        d_out = do_n[h, rows, :]
        s = dot(k_n[0, :nk, :], q, 1, 1)
        j = lax.broadcasted_iota(jnp.int32, s.shape, 0)
        ok = (j >= lo_ref[:, rows]) & (j <= hi_ref[:, rows])
        soft = jnp.exp(jnp.where(ok, s - lse_ref[h, :, rows], -1e30))
        d_soft = dot(v_n[0, :nk, :], d_out, 1, 1)
        delta = jnp.sum((d_out.astype(F32) * o_n[h, rows, :].astype(F32)).T, axis=0, keepdims=True)
        d_s = (soft * (d_soft - delta)).astype(BF16)
        dv_n[:nk, :] += dot(soft.astype(BF16), d_out, 1, 0)
        dk_n[:nk, :] += dot(d_s, q, 1, 0)
        dq_n[h, rows, :] = dot(kt_n[:, :nk], d_s, 1, 0).T

    over_queries(heads, seq, slot, step, visit)
    per = dqm.shape[0] // block
    scale = 1.0 / math.sqrt(HEAD)
    first = starts_ref[16] == 0
    for a in range(2 * per):
        dq_to, keep_to, send_to = (dqm, keepm, sendm) if a < per else (dqo, keepo, sendo)
        row = (a % per) * block
        here = slice(row, row + block)
        there = pl.ds(pl.multiple_of(starts_ref[a], block), block)
        cosine, sine = cos_ref[a * block : (a + 1) * block, :], -sin_ref[a * block : (a + 1) * block, :]
        for h in range(heads):
            dq_to[here, h * HEAD : (h + 1) * HEAD] = (
                turn(dq_n[h, there, :], cosine, sine) * scale
            ).astype(BF16)
        dk = turn(dk_n[there, :], cosine, sine)
        dv = dv_n[there, :]
        keep_to[here, :] = jnp.where(first, dk, dv)
        send_to[here, :] = jnp.where(first, dv, dk).astype(BF16)


def attn_backward(starts, q, own, got, d_out, out, lse, lo, hi, cosine, sine, slot):
    half, q_cols = q[0].shape
    heads = q_cols // HEAD
    seq = 2 * half
    pair = lambda cols, dtype: [jax.ShapeDtypeStruct((half, cols), dtype)] * 2
    return pl.pallas_call(
        functools.partial(attn_backward_kernel, slot, seq // 16),
        out_shape=tuple(pair(q_cols, BF16) + pair(HEAD, F32) + pair(HEAD, BF16)),
        in_specs=[ANY_SMEM] + [ANY_VMEM] * 15,
        out_specs=(ANY_VMEM,) * 6,
        scratch_shapes=[
            pltpu.VMEM((heads, seq, HEAD), BF16),
            pltpu.VMEM((1, seq, HEAD), BF16),
            pltpu.VMEM((1, seq, HEAD), BF16),
            pltpu.VMEM((heads, seq, HEAD), BF16),
            pltpu.VMEM((heads, seq, HEAD), BF16),
            pltpu.VMEM((HEAD, seq), BF16),
            pltpu.VMEM((heads, seq, HEAD), F32),
            pltpu.VMEM((seq, HEAD), F32),
            pltpu.VMEM((seq, HEAD), F32),
        ],
        cost_estimate=pl.CostEstimate(
            flops=24 * seq * seq * q_cols, bytes_accessed=seq * q_cols * 16, transcendentals=heads * seq * seq
        ),
        name="attn_backward",
    )(starts, *q, *own, *got, *d_out, *out, lse, lo, hi, cosine, sine)


def hidden_kernel(ff, w_ref, n2_ref, df_ref, out_ref):
    dh = dot(w_ref[2 * ff :, :], df_ref[...], 1, 1)
    gu = dot(w_ref[: 2 * ff, :], n2_ref[...], 1, 1)
    gate, up = gu[:ff], gu[ff:]
    sig = jax.nn.sigmoid(gate)
    silu = gate * sig
    out_ref[:ff, :] = (dh * up * (sig * (1.0 + gate * (1.0 - sig)))).astype(BF16)
    out_ref[ff : 2 * ff, :] = (dh * silu).astype(BF16)
    out_ref[2 * ff :, :] = (silu * up).astype(BF16)


def hidden_half(w, n2, df):
    rows, width = n2.shape
    ff = w.shape[0] // 3
    tile = rows // 3
    return pl.pallas_call(
        functools.partial(hidden_kernel, ff),
        out_shape=jax.ShapeDtypeStruct((3 * ff, rows), BF16),
        grid=(rows // tile,),
        in_specs=[
            pl.BlockSpec((3 * ff, width), lambda r: (0, 0), pipeline_mode=pl.Buffered(1)),
            pl.BlockSpec((tile, width), lambda r: (r, 0)),
            pl.BlockSpec((tile, width), lambda r: (r, 0)),
        ],
        out_specs=pl.BlockSpec((3 * ff, tile), lambda r: (0, r)),
        cost_estimate=pl.CostEstimate(
            flops=6 * rows * width * ff, bytes_accessed=6 * ff * width, transcendentals=ff * rows
        ),
        name="hidden",
    )(w, n2, df)


def grads_kernel(ff, lm_ref, lo_ref, nm_ref, no_ref, dm_ref, do_ref, out_ref):
    out_ref[: 2 * ff, :] = (
        dot(lm_ref[: 2 * ff, :], nm_ref[...], 1, 0) + dot(lo_ref[: 2 * ff, :], no_ref[...], 1, 0)
    ).astype(BF16)
    out_ref[2 * ff :, :] = (
        dot(lm_ref[2 * ff :, :], dm_ref[...], 1, 0) + dot(lo_ref[2 * ff :, :], do_ref[...], 1, 0)
    ).astype(BF16)


def feed_grads(left, n2, df):
    rows, half = left[0].shape
    width = n2[0].shape[1]
    tile = 256
    whole = pl.BlockSpec((rows, half), lambda j: (0, 0), pipeline_mode=pl.Buffered(1))
    part = pl.BlockSpec((half, tile), lambda j: (0, j))
    return pl.pallas_call(
        functools.partial(grads_kernel, rows // 3),
        out_shape=jax.ShapeDtypeStruct((rows, width), BF16),
        grid=(width // tile,),
        in_specs=[whole, whole, part, part, part, part],
        out_specs=pl.BlockSpec((rows, tile), lambda j: (0, j)),
        cost_estimate=pl.CostEstimate(
            flops=4 * rows * half * width, bytes_accessed=rows * width * 2, transcendentals=0
        ),
        name="feed_grads",
    )(*left, *n2, *df)


def add_last_kernel(a0, b0, a1, b1, *rest):
    out, rows = rest[-1], b0.shape[0]
    out[:rows, :] = a0[:rows, :].astype(F32) + b0[...].astype(F32)
    out[rows:, :] = a1[:rows, :].astype(F32) + b1[...].astype(F32)


def collect_end_after(state, *others):
    one, two = state
    h, width = one.shape[0] // 2, one.shape[1]
    return pl.pallas_call(
        add_last_kernel,
        out_shape=jax.ShapeDtypeStruct((2 * h, width), F32),
        in_specs=[ANY_VMEM] * 4 + [pl.BlockSpec(memory_space=pl.ANY)] * len(others),
        out_specs=ANY_VMEM,
        name="add_last",
    )(one, side(one[h:]), two, far(two[h:]), *others)


def hold_kernel(v_ref, *rest):
    rest[-1][...] = v_ref[...]


def hold(v, *others):
    rows, width = v.shape
    tile = rows // 3 if rows % 48 == 0 else rows
    return pl.pallas_call(
        hold_kernel,
        out_shape=jax.ShapeDtypeStruct(v.shape, v.dtype),
        grid=(rows // tile,),
        in_specs=[pl.BlockSpec((tile, width), lambda i: (i, 0))] + [pl.BlockSpec(memory_space=pl.ANY)] * len(others),
        out_specs=pl.BlockSpec((tile, width), lambda i: (i, 0)),
        name="hold",
    )(v, *others)


def bring(c_ref, first, rows, refs, buf, sems):
    copies = [
        pltpu.make_async_copy(
            ref.at[pl.ds(start, rows), :], buf.at[lax.bitwise_xor(c_ref[0], bits)], sems.at[bits]
        )
        for bits, (ref, start) in enumerate(zip(refs, first))
    ]
    for copy in copies:
        copy.start()
    for copy in copies:
        copy.wait()


def finish_kernel(turned, sizes, c_ref, *refs):
    parts = len(sizes)
    pieces, out_ref, bufs, sems = refs[: 4 * parts], refs[4 * parts], refs[4 * parts + 1 : -1], refs[-1]
    for part, rows in enumerate(sizes):
        bring(c_ref, turned[1][part], rows, pieces[4 * part : 4 * part + 4], bufs[part], sems.at[part])
    at = 0
    for k in range(4):
        for part, rows in enumerate(sizes):
            v = bufs[part][k].astype(F32)
            if turned[0]:
                out_ref[:, at : at + rows] = v.T
            else:
                out_ref[at : at + rows, :] = v
            at += rows


def finish(c, sizes, turned, parts):
    width = parts[0][0][0].shape[1]
    total = 4 * sum(sizes)
    shape = (width, total) if turned else (total, width)
    firsts = [[first for _, first in part] for part in parts]
    return pl.pallas_call(
        functools.partial(finish_kernel, (turned, firsts), sizes),
        out_shape=jax.ShapeDtypeStruct(shape, F32),
        in_specs=[ANY_SMEM] + [pl.BlockSpec(memory_space=pl.ANY)] * (4 * len(parts)),
        out_specs=ANY_VMEM,
        scratch_shapes=[pltpu.VMEM((4, rows, width), BF16) for rows in sizes]
        + [pltpu.SemaphoreType.DMA((len(parts), 4))],
        name="finish",
    )(c, *[v for part in parts for v, _ in part])


def finish_attn_kernel(q_cols, c_ref, r0, r1, r2, r3, q_ref, k_ref, v_ref, o_ref, gain_ref, buf, sems):
    rows = buf.shape[1]
    bring(c_ref, (0,) * 4, rows, (r0, r1, r2, r3), buf, sems)
    qkv = q_cols + HEAD
    for k in range(4):
        q_ref[:, k * q_cols : (k + 1) * q_cols] = buf[k, :q_cols, :].astype(F32).T
        to = v_ref if k % 2 else k_ref
        to[:, (k // 2) * HEAD : (k // 2 + 1) * HEAD] = buf[k, q_cols:qkv, :].astype(F32).T
        o_ref[k * q_cols : (k + 1) * q_cols, :] = buf[k, qkv + 16 :, :].astype(F32)
    gain_ref[...] = sum(buf[k, qkv : qkv + 16, :].astype(F32) for k in range(4))


def finish_attn(c, q_cols, pieces):
    rows, width = pieces[0].shape
    shapes = [(width, 4 * q_cols), (width, 2 * HEAD), (width, 2 * HEAD), (4 * q_cols, width), (16, width)]
    return pl.pallas_call(
        functools.partial(finish_attn_kernel, q_cols),
        out_shape=tuple(jax.ShapeDtypeStruct(shape, F32) for shape in shapes),
        in_specs=[ANY_SMEM] + [pl.BlockSpec(memory_space=pl.ANY)] * 4,
        out_specs=(ANY_VMEM,) * 5,
        scratch_shapes=[pltpu.VMEM((4, rows, width), BF16), pltpu.SemaphoreType.DMA((4,))],
        name="finish_attn",
    )(c, *pieces)


def tables(c, t, core, tok_rows, seq_ids, pic_starts, pic_lengths):
    seq_len = seq_ids.shape[1]
    start_list = arrival_starts(c, t, tok_rows)
    starts = jnp.stack(start_list + [core]).astype(jnp.int32)
    positions = (starts[:16, None] + jnp.arange(seq_len // 16, dtype=jnp.int32)[None, :]).reshape(-1)
    frequency = jnp.power(rope_base, -jnp.arange(HEAD // 2, dtype=F32) * 2.0 / HEAD)
    angles = positions.astype(F32)[:, None] * frequency[None, :]
    cosine, sine = jnp.cos(angles), jnp.sin(angles)
    cosine = jnp.concatenate([cosine, cosine], axis=1)
    sine = jnp.concatenate([-sine, sine], axis=1)
    docs = seq_ids[0]
    index = jnp.arange(seq_len, dtype=jnp.int32)
    lo = jnp.sum((docs[:, None] < docs[None, :]).astype(jnp.int32), axis=0)
    doc_end = jnp.sum((docs[:, None] <= docs[None, :]).astype(jnp.int32), axis=0) - 1
    pic_ends = pic_starts[0] + pic_lengths[0]
    inside = (index[:, None] >= pic_starts[0][None, :]) & (index[:, None] < pic_ends[None, :])
    last = jnp.max(jnp.where(inside, pic_ends[None, :] - 1, -1), axis=1)
    hi = jnp.minimum(doc_end, jnp.maximum(index, last))
    lo, hi = lo[None, :], hi[None, :]
    return starts, cosine, sine, lo, hi


def body(
    tokens,
    seq_ids,
    pic_starts,
    pic_lengths,
    skip_mask,
    w_query,
    w_key,
    w_value,
    w_out,
    w_gate,
    w_up,
    w_down,
    gain_attn,
    gain_ffn,
    cotangent,
):
    tok_rows = tokens.shape[1]
    own = tok_rows // 2
    seq_len = seq_ids.shape[1]
    slot = seq_len // pic_starts.shape[1]
    c = lax.axis_index("ctx")
    t = lax.axis_index("tp")
    core = (c & 1).astype(jnp.int32)
    q_cols = w_query.shape[1] // 4
    ff = w_gate.shape[1] // 4
    part_a = (ff * 5 // 8 + 15) // 16 * 16
    part_b = ff - part_a

    flag = seq_ids[0, 0] >= 0
    qkv_cols = q_cols + HEAD
    half = seq_len // 2
    core_flag = core.reshape(1)
    first_own = pack_first(
        jnp.stack([c, core, c >> 1]).astype(jnp.int32), w_query, w_key, w_value, w_out, gain_attn, gain_ffn
    )
    first = gather_whole(first_own)

    def start_stage(tokens, skip_mask, cotangent, w_gate, w_up, w_down, seq_ids, pic_starts, pic_lengths):
        x_own_b = lax.dynamic_slice_in_dim(tokens[0], t * own, own, 0)
        keep_own = lax.dynamic_slice_in_dim(skip_mask[0], t * own, own, 0).astype(F32)[:, None]
        dy_own = lax.dynamic_slice_in_dim(cotangent[0], t * own, own, 0).astype(F32)
        parts = spread_start(x_own_b)
        wd_own = lax.dynamic_slice_in_dim(w_down, c * ff, ff, 0)
        wg_t = lax.dynamic_slice_in_dim(w_gate, c * ff, ff, 1).T
        wu_t = lax.dynamic_slice_in_dim(w_up, c * ff, ff, 1).T
        weights = [
            jnp.concatenate([v[first:last] for v in (wg_t, wu_t, wd_own)], axis=0)
            for first, last in ((0, part_a), (part_a, ff))
        ]
        parts = after(parts, weights)
        ready = parts[:2] + spread_more(parts)
        table = tables(c, t, core, tok_rows, seq_ids, pic_starts, pic_lengths)
        d_ffn_own = (keep_own * dy_own).astype(BF16)
        x_mine = spread_join(after(ready, table, d_ffn_own))
        x_other = near(x_mine)
        return x_own_b.astype(F32), keep_own, dy_own, d_ffn_own, x_mine, x_other, weights, table

    x_own, keep_own, dy_own, d_ffn_own, x_mine, x_other, weights, (starts, cosine, sine, lo, hi) = fenced(
        flag, start_stage,
        *after((tokens, skip_mask, cotangent, w_gate, w_up, w_down, seq_ids, pic_starts, pic_lengths), first_own)
    )
    weights = after(weights, x_other)
    wa, wb = gather_whole(weights[0]), gather_whole(weights[1])

    def forward_stage(x_mine, x_other, first, d_ffn_own, x_own, keep_own, cosine, sine, lo, hi, starts):
        wo = first[qkv_cols + 16 :]
        gain_two = first[qkv_cols + 1 : qkv_cols + 2].astype(F32)
        df_parts = spread_start(d_ffn_own)
        n1m, qm, kvm = qkv_half(core_flag, x_mine, first, qkv_cols, cosine[:half], sine[:half])
        n1o, qo, kvo = qkv_half(core_flag, x_other, first, qkv_cols, cosine[half:], sine[half:])
        q, own_kv = (qm, qo), (kvm, kvo)
        got = (near(kvo), near(kvm))
        q = after(q, df_parts)
        df_ready = df_parts[:2] + spread_more(df_parts)
        hm, ho, lse = attn_forward(starts, q, own_kv, got, lo, hi, slot)
        hm, ho = after((hm, ho), df_ready)
        both = join_cores(dot(hm, wo, 1, 0).astype(BF16), dot(ho, wo, 1, 0).astype(BF16))
        state = collect_first(both)
        dfm = spread_join(after(df_ready, both))
        attn = collect_end(collect_second(after(state, dfm)))
        dfo = near(dfm)
        mid = x_own + keep_own * attn
        inv_two = lax.rsqrt(jnp.mean(mid * mid, axis=-1, keepdims=True) + norm_eps)
        hat_two = mid * inv_two
        n2m, n2o = spread((hat_two * gain_two).astype(BF16))
        return n1m, n1o, q, own_kv, got, hm, ho, lse, dfm, dfo, n2m, n2o, mid, inv_two, hat_two

    n1m, n1o, q, own_kv, got, hm, ho, lse, dfm, dfo, n2m, n2o, mid, inv_two, hat_two = fenced(
        flag, forward_stage, x_mine, x_other, first, d_ffn_own, x_own, keep_own, cosine, sine, lo, hi, starts
    )

    am, ao = hidden_half(wa, n2m, dfm), hidden_half(wa, n2o, dfo)
    grad_a = feed_grads((am, ao), (n2m, n2o), (dfm, dfo))
    shard_a = scatter_whole(grad_a)
    pao = dot(ao[: 2 * part_a], wa[: 2 * part_a], 0, 0).astype(BF16)
    bm, bo = hidden_half(wb, n2m, dfm), hidden_half(wb, n2o, dfo)
    grad_b = feed_grads((bm, bo), (n2m, n2o), (dfm, dfo))
    shard_b = scatter_whole(grad_b)

    def middle_stage(am, ao, bm, bo, pao, wa, wb, first, dy_own, keep_own, hat_two, inv_two):
        gain_two = first[qkv_cols + 1 : qkv_cols + 2].astype(F32)
        p_other = (pao.astype(F32) + dot(bo[: 2 * part_b], wb[: 2 * part_b], 0, 0)).astype(BF16)
        p_mine = (
            dot(am[: 2 * part_a], wa[: 2 * part_a], 0, 0) + dot(bm[: 2 * part_b], wb[: 2 * part_b], 0, 0)
        ).astype(BF16)
        both = join_cores(p_mine, p_other)
        state = collect_first(both)
        am, ao, bm, bo = after((am, ao, bm, bo), both)

        def feed_out(a, b):
            return (
                dot(a[2 * part_a :], wa[2 * part_a :], 0, 0) + dot(b[2 * part_b :], wb[2 * part_b :], 0, 0)
            ).astype(BF16)

        f_other, f_mine = feed_out(ao, bo), feed_out(am, bm)
        d_n2 = collect_end(collect_second(after(state, f_other, f_mine)))
        d_mid = dy_own + norm_back(d_n2, hat_two, inv_two, gain_two)
        share_two = jnp.sum(d_n2 * hat_two, axis=0, keepdims=True)
        f_split = collect_split(join_cores(f_mine, f_other))
        dam, dao = spread((keep_own * d_mid).astype(BF16), f_split)
        d_head_m = dot(dam, first[qkv_cols + 16 :], 1, 1).astype(BF16)
        return d_mid, share_two, dam, dao, f_split, d_head_m

    bm, bo = after((bm, bo), grad_b)
    d_mid, share_two, dam, dao, f_split, d_head_m = fenced(
        flag, middle_stage, am, ao, bm, bo, pao, wa, wb, first, dy_own, keep_own, hat_two, inv_two
    )

    def backward_stage(
        share_two, dam, dao, f_split, d_head_m, first, q, own_kv, got, hm, ho, lse, lo, hi, cosine, sine, starts,
        x_mine, x_other, n1m, n1o, shard_a
    ):
        wqkv, wo = first[:qkv_cols], first[qkv_cols + 16 :]
        f_state = collect_send(f_split)
        d_head = (d_head_m, dot(dao, wo, 1, 1).astype(BF16))
        dqm, dqo, keepm, keepo, sendm, sendo = attn_backward(
            starts, q, own_kv, got, d_head, (hm, ho), lse, lo, hi, cosine, sine, slot
        )
        sendm, sendo = after((sendm, sendo), f_state)
        a_far = far(shard_a[: 2 * part_a])
        got_m, got_o = near(sendo), near(sendm)
        do = jnp.concatenate([dqo, (keepo + got_o.astype(F32)).astype(BF16)], axis=1)
        e_other = dot(do, wqkv, 1, 0).astype(BF16)
        dm = jnp.concatenate([dqm, (keepm + got_m.astype(F32)).astype(BF16)], axis=1)
        e_mine = dot(dm, wqkv, 1, 0).astype(BF16)
        both = join_cores(e_mine, e_other)
        state = collect_first(both)
        dm, do, hm, ho, x_mine, x_other = after((dm, do, hm, ho, x_mine, x_other), both)
        grad_qkv = (dot(dm, n1m, 0, 0) + dot(do, n1o, 0, 0)).astype(BF16)

        def gain_share(e, x):
            x = x.astype(F32)
            inv = lax.rsqrt(jnp.mean(x * x, axis=-1, keepdims=True) + norm_eps)
            return jnp.sum(e.astype(F32) * (x * inv), axis=0, keepdims=True)

        share_one = gain_share(e_mine, x_mine) + gain_share(e_other, x_other)
        shares = jnp.concatenate(
            [share_one, share_two, jnp.zeros((14, share_one.shape[1]), F32)], axis=0
        )
        shares_side = side(shares.astype(BF16))
        state = collect_second(after(state, grad_qkv, shares))
        hm, ho, dam, dao = after((hm, ho, dam, dao), state)
        grad_out = (dot(hm, dam, 0, 0) + dot(ho, dao, 0, 0)).astype(BF16)
        shares = (shares + shares_side.astype(F32)).astype(BF16)
        grad_attn = jnp.concatenate([grad_qkv, shares, grad_out], axis=0)
        d_n1 = collect_end_after(state, grad_out)
        return d_n1, grad_attn, collect_second(f_state), a_far

    d_n1, grad_attn, f_state, a_far = fenced(
        flag, backward_stage, share_two, dam, dao, f_split, d_head_m, first, q, own_kv, got, hm, ho, lse, lo, hi,
        cosine, sine, starts, x_mine, x_other, n1m, n1o, shard_a
    )
    shard_attn = scatter_whole(after(grad_attn, shard_b))
    member = c.astype(jnp.int32).reshape(1)

    def end_stage(d_n1, f_state, x_own, d_mid, first, mid, keep_own, shard_a, a_far, shard_b):
        gain_one = first[qkv_cols : qkv_cols + 1].astype(F32)
        ffn = collect_end(f_state)
        inv_one = lax.rsqrt(jnp.mean(x_own * x_own, axis=-1, keepdims=True) + norm_eps)
        hat_one = x_own * inv_one
        input_grad = (d_mid + norm_back(d_n1, hat_one, inv_one, gain_one)).astype(BF16)
        output = (mid + keep_own * ffn).astype(BF16)
        gate_far = far(hold(shard_b[:part_b], ffn))
        a_near, a_near_far, b_near = near(shard_a), near(a_far), near(shard_b)
        grad_gate = finish(
            member, sizes, True,
            [
                [(shard_a, 0), (a_near, 0), (a_far, 0), (a_near_far, 0)],
                [(shard_b, 0), (b_near, 0), (gate_far, 0), (near(gate_far), 0)],
            ],
        )
        rest = jnp.concatenate([shard_a[2 * part_a :], shard_b[part_b:]], axis=0)
        rest_far = hold(far(hold(rest, ffn)), grad_gate)
        return (
            in_order(input_grad, side(input_grad), t), output, grad_gate, a_near, a_near_far, b_near, rest_far, near(rest_far)
        )

    sizes = (part_a, part_b)
    input_grad, output, grad_gate, a_near, a_near_far, b_near, rest_far, near_far = fenced(
        flag, end_stage, d_n1, f_state, x_own, d_mid, first, mid, keep_own, shard_a, a_far, shard_b
    )

    def last_stage(shard_a, shard_b, a_near, a_far, a_near_far, b_near, rest_far, near_far, shard_attn, output):
        attn_far = far(shard_attn)
        up = [
            [(shard_a, part_a), (a_near, part_a), (a_far, part_a), (a_near_far, part_a)],
            [(shard_b, part_b), (b_near, part_b), (rest_far, part_a), (near_far, part_a)],
        ]
        down = [
            [(shard_a, 2 * part_a), (a_near, 2 * part_a), (rest_far, 0), (near_far, 0)],
            [(shard_b, 2 * part_b), (b_near, 2 * part_b), (rest_far, part_a + part_b), (near_far, part_a + part_b)],
        ]
        feed = finish(member, sizes, True, up), finish(member, sizes, False, down)
        attn_far = hold(attn_far, *feed)
        return feed, in_order(output, side(output), t), finish_attn(
            member, q_cols, (shard_attn, near(shard_attn), attn_far, near(attn_far))
        )

    (grad_up, grad_down), output, (grad_query, grad_key, grad_value, grad_out, gain_grads) = fenced(
        flag, last_stage, shard_a, shard_b, a_near, a_far, a_near_far, b_near, rest_far, near_far, shard_attn, output
    )
    return (
        output[None],
        input_grad[None],
        grad_query,
        grad_key,
        grad_value,
        grad_out,
        grad_gate,
        grad_up,
        grad_down,
        gain_grads[0],
        gain_grads[1],
    )


def solution(mesh):
    placed = (
        P("fsdp", "ctx", None),
        P("fsdp", None),
        P("fsdp", None),
        P("fsdp", None),
        P("fsdp", "ctx"),
        P("fsdp", "tp"),
        P("fsdp", "tp"),
        P("fsdp", "tp"),
        P("tp", "fsdp"),
        P("fsdp", "tp"),
        P("fsdp", "tp"),
        P("tp", "fsdp"),
        P("fsdp"),
        P("fsdp"),
        P("fsdp", "ctx", None),
    )
    return jax.shard_map(
        body,
        mesh=mesh,
        in_specs=placed,
        out_specs=(
            P("fsdp", "ctx", None),
            P("fsdp", "ctx", None),
            P("fsdp", "tp"),
            P("fsdp", "tp"),
            P("fsdp", "tp"),
            P("tp", "fsdp"),
            P("fsdp", "tp"),
            P("fsdp", "tp"),
            P("tp", "fsdp"),
            P("fsdp"),
            P("fsdp"),
        ),
        check_vma=False,
    )
```

time: 835 us -> 544 us (0.65)
  Pallas kernels: 0 us -> 154 us
  other arithmetic: 209 us -> 69.2 us
  waiting for transfers between devices: 261 us -> 139 us
  matrix products: 155 us -> 49.4 us
  blocking collectives: 51.4 us -> 0 us
  local copies, waits for them, and re-layouts: 83.1 us -> 51 us
    pallas_call x0 -> x24, Pallas kernels: none -> 154 us  [the longest x4 32.6 us: hidden_half(): pl.pallas_call(functools.partial(hidden_kernel, ff), out_shape=jax.ShapeD...]
    concatenate x23 -> x7, other arithmetic: 103 us -> 8.68 us  [the longest x1 3.07 us: collect_end(): jnp.concatenate([one[:h].astype(F32) + one_side.astype(F32), two[:h].asty...]
    dot_general x12 -> x18, matrix products: 111 us -> 49.4 us  [dot(): lax.dot_general(a, b, (((ca,), (cb,)), ((), ())), preferred_element_type=...]
    psum x1 -> x0, blocking collectives: 51.4 us -> none  [body(): lax.psum(jnp.stack([jnp.sum(d_n1 * hat_one, axis=0), jnp.sum(d_n2 * hat_t...]
    ppermute x18 -> x23, waiting for transfers between devices: 88.7 us -> 38.6 us  [side(): return lax.ppermute(v, 'tp', [(0, 1), (1, 0)])]
    reduce_scatter x4 -> x3, waiting for transfers between devices: 48.1 us -> 0.04 us  [scatter_whole(): return lax.psum_scatter(g, 'fsdp', scatter_dimension=1, tiled=True)]
    dot_general x6 -> x0, matrix products: 44.2 us -> none  [the longest x1 13 us: body(): jnp.einsum('qhd,kd->hqk', d_head, values, preferred_element_type=F32)]
    convert_element_type x31 -> x24, other arithmetic: 61.3 us -> 29.2 us  [the longest x12 16.2 us: add(): return (a.astype(F32) + b.astype(F32)).astype(BF16)]
  transfers between devices with their start and end apart: 60 -> 72, of which waited for: 28 -> 36; matrix products, arithmetic and copies ran while one was open for 44% -> 29% of each run, Pallas kernels for 0% -> 27%
where the time goes in v2:
time: 544 us; the launch traced here: 534 us
  Pallas kernels  154 us (28%)
  waiting for transfers between devices  139 us (26%)
  other arithmetic  69.2 us (13%)
  starting transfers between devices  53.1 us (10%)
  local copies, waits for them, and re-layouts  51 us (9%)
  matrix products  49.4 us (9%)
  between operations  15.3 us (3%)
    ppermute x24, waiting for transfers between devices, far(): return lax.ppermute(v, 'ctx', [(i, i ^ 2) for i in range(4)])  74.9 us
    dot_general x18, matrix products, dot(): lax.dot_general(a, b, (((ca,), (cb,)), ((), ())), preferred_element_type=...  49.4 us
    ppermute x23, waiting for transfers between devices, side(): return lax.ppermute(v, 'tp', [(0, 1), (1, 0)])  38.6 us
    pallas_call x4, Pallas kernels, hidden_half(): pl.pallas_call(functools.partial(hidden_kernel, ff), out_shape=jax.ShapeD...  32.6 us
    pallas_call x2, Pallas kernels, feed_grads(): pl.pallas_call(functools.partial(grads_kernel, rows // 3), out_shape=jax....  26.5 us
    ppermute x24, starting transfers between devices, far(): return lax.ppermute(v, 'ctx', [(i, i ^ 2) for i in range(4)])  26.1 us
    ppermute x23, starting transfers between devices, side(): return lax.ppermute(v, 'tp', [(0, 1), (1, 0)])  24.9 us
    ppermute x19, waiting for transfers between devices, near(): return lax.ppermute(v, 'ctx', [(i, i ^ 1) for i in range(4)])  19.1 us
  transfers between devices with their start and end apart: 72, of which 36 were waited for; matrix products, arithmetic and copies ran while one was open for 29% of the time, Pallas kernels for 27%

profile of v2, /device:TPU:0, one launch (start us, length us, event | category | flops | bytes accessed | tf_op | source)
XLA Modules:
  0.0 533.8 jit_solution(5125642033571208749)
XLA Ops:
  12.0 50.9 %conditional.6 = (f32[192,2048]{1,0:T(8,128)S(1)}, f32[192,1]{0,1:T(1,128)S(1)}, f32[192,2048]{1,0:T(8,128)S(1)}, bf16[192,2048]{1,0:T(8,128)(2,1)}, bf16[768,20...) conditional(s32[]{:T(128)} %bitcast.69, () %tuple.79, ...), branch_computations={%region_0.0_spmd, %region_1.5_spmd} | conditional | flops 18704426 | bytes 76132200 | solution.py:34
  14.1 2.9 collective-permute-start.59
  19.1 3.2 copy.84
  28.8 4.4 fusion.32
  35.5 3.4 concatenate.57
  45.3 5.7 %collective-permute-done.63.refs_3_ = bf16[96,2048]{1,0:T(8,128)(2,1)S(1)} collective-permute-done((bf16[96,2048]{1,0:T(8,128)(2,1)}, bf16[96,2048]{1,0:T(8,128)(2,1)S(1)}, u32[]{:S(2)}, u32[]{:S(2)}) %collective-permute-start.63) | collective-permute-done | bytes 393248 | tf_op jit(solution)/shard_map/cond/branch_1_fun/ppermute | solution.py:51
  53.2 3.6 join.4
  58.2 4.6 collective-permute-done.65
  62.8 3.5 copy.85
  69.4 128.1 %conditional.7 = (bf16[768,2048]{1,0:T(8,128)(2,1)}, bf16[768,2048]{1,0:T(8,128)(2,1)}, bf16[768,256]{1,0:T(8,128)(2,1)}, bf16[768,256]{1,0:T(8,128)(2,1)}, bf16...) conditional(s32[]{:T(128)} %bitcast.69, () %tuple.83, ...), branch_computations={%region_5.6_spmd, %region_6.8_spmd} | conditional | flops 11291199488 | bytes 187464880 | solution.py:34
  79.1 5.6 %qkv.3 = (bf16[768,2048]{1,0:T(8,128)(2,1)}, bf16[768,256]{1,0:T(8,128)(2,1)}, bf16[768,128]{1,0:T(8,128)(2,1)}) custom-call(s32[1]{0:T(128)} %get-tuple-element.210.core_ref, bf16[768,2048]{1,0:T(8,128)(2,1)} %get-tuple-element.216.x_ref, bf16[656,2048]{1,0:T(8,128)(2,1)S(1)} %copy-done.1, bf16[656,2048]{1,0:T(8,128)(2,1)S(1)} %copy-done.1, ...), custom_call_target="tpu_custom_call" | custom-call | flops 1207959552 | bytes 7864320 | tf_op jit(solution)/shard_map/cond/branch_1_fun/qkv/pallas_call | solution.py:237
  84.8 5.5 %qkv.2 = (bf16[768,2048]{1,0:T(8,128)(2,1)}, bf16[768,256]{1,0:T(8,128)(2,1)}, bf16[768,128]{1,0:T(8,128)(2,1)}) custom-call(s32[1]{0:T(128)} %get-tuple-element.210.core_ref, bf16[768,2048]{1,0:T(8,128)(2,1)} %get-tuple-element.211.x_ref, bf16[656,2048]{1,0:T(8,128)(2,1)S(1)} %copy-done.1, bf16[656,2048]{1,0:T(8,128)(2,1)S(1)} %copy-done.1, ...), custom_call_target="tpu_custom_call" | custom-call | flops 1207959552 | bytes 7864320 | tf_op jit(solution)/shard_map/cond/branch_1_fun/qkv/pallas_call | solution.py:237
  95.0 14.3 %attn_forward.1 = (bf16[768,256]{1,0:T(8,128)(2,1)S(1)}, bf16[768,256]{1,0:T(8,128)(2,1)S(1)}, f32[2,1,1536]{2,1,0:T(1,128)S(1)}) custom-call(s32[17]{0:T(128)S(1)} %get-tuple-element.225.starts_ref, bf16[768,256]{1,0:T(8,128)(2,1)} %get-tuple-element.694.qm, bf16[768,256]{1,0:T(8,128)(2,1)} %get-tuple-element.695.qo, ...), custom_call_target="tpu_custom_call" | custom-call | flops 7247757312 | bytes 3145728 | tf_op jit(solution)/shard_map/cond/branch_1_fun/attn_forward/pallas_call | solution.py:336
  111.5 4.6 collective-permute-done.22
  122.3 3.6 join.5
  126.0 14.2 %collective-permute-done.24 = bf16[192,2048]{1,0:T(8,128)(2,1)} collective-permute-done((bf16[192,2048]{1,0:T(8,128)(2,1)}, bf16[192,2048]{1,0:T(8,128)(2,1)}, u32[]{:S(2)}, u32[]{:S(2)}) %collective-permute-start.24) | collective-permute-done | bytes 786464 | tf_op jit(solution)/shard_map/cond/branch_1_fun/ppermute | solution.py:43
  145.5 7.4 %collective-permute-done.27 = bf16[96,2048]{1,0:T(8,128)(2,1)S(1)} collective-permute-done((bf16[96,2048]{1,0:T(8,128)(2,1)S(1)}, bf16[96,2048]{1,0:T(8,128)(2,1)S(1)}, u32[]{:S(2)}, u32[]{:S(2)}) %collective-permute-start.27) | collective-permute-done | bytes 393248 | tf_op jit(solution)/shard_map/cond/branch_1_fun/ppermute | solution.py:43
  163.3 8.0 %collective-permute-done.28.refs_1_ = bf16[96,2048]{1,0:T(8,128)(2,1)S(1)} collective-permute-done((bf16[96,2048]{1,0:T(8,128)(2,1)S(1)}, bf16[96,2048]{1,0:T(8,128)(2,1)S(1)}, u32[]{:S(2)}, u32[]{:S(2)}) %collective-permute-start.28) | collective-permute-done | bytes 393248 | tf_op jit(solution)/shard_map/cond/branch_1_fun/ppermute | solution.py:43
  173.3 7.8 %collective-permute-done.29.refs_2_ = bf16[96,2048]{1,0:T(8,128)(2,1)S(1)} collective-permute-done((bf16[96,2048]{1,0:T(8,128)(2,1)S(1)}, bf16[96,2048]{1,0:T(8,128)(2,1)S(1)}, u32[]{:S(2)}, u32[]{:S(2)}) %collective-permute-start.29) | collective-permute-done | bytes 393248 | tf_op jit(solution)/shard_map/cond/branch_1_fun/ppermute | solution.py:51
  181.2 5.0 collective-permute-done.30.refs_3_
  187.7 3.6 join.6
  191.4 6.0 %collective-permute-done.34 = bf16[768,2048]{1,0:T(8,128)(2,1)} collective-permute-done((bf16[768,2048]{1,0:T(8,128)(2,1)}, bf16[768,2048]{1,0:T(8,128)(2,1)}, u32[]{:S(2)}, u32[]{:S(2)}) %collective-permute-start.34) | collective-permute-done | bytes 3145760 | tf_op jit(solution)/shard_map/cond/branch_1_fun/ppermute | solution.py:47
  197.5 8.5 %hidden.4.lm_ref = bf16[1344,768]{1,0:T(8,128)(2,1)S(1)} custom-call(bf16[1344,2048]{1,0:T(8,128)(2,1)} %all-gather.4.cloned.1.call-done.w_ref, bf16[768,2048]{1,0:T(8,128)(2,1)} %get-tuple-element.456.n2_ref.nm_ref, bf16[768,2048]{1,0:T(8,128)(2,1)} %get-tuple-element.457.df_ref.dm_ref), custom_call_target="tpu_custom_call" | custom-call | flops 4227858432 | bytes 5505024 | tf_op jit(solution)/shard_map/hidden/pallas_call | solution.py:451
  206.0 10.0 %hidden.5.lo_ref = bf16[1344,768]{1,0:T(8,128)(2,1)} custom-call(bf16[1344,2048]{1,0:T(8,128)(2,1)} %all-gather.4.cloned.1.call-done.w_ref, bf16[768,2048]{1,0:T(8,128)(2,1)} %get-tuple-element.458.n2_ref.no_ref, bf16[768,2048]{1,0:T(8,128)(2,1)} %get-tuple-element.459.df_ref.do_ref), custom_call_target="tpu_custom_call" | custom-call | flops 4227858432 | bytes 5505024 | tf_op jit(solution)/shard_map/hidden/pallas_call | solution.py:451
  216.0 14.5 %feed_grads.2 = bf16[1344,2048]{1,0:T(8,128)(2,1)} custom-call(bf16[1344,768]{1,0:T(8,128)(2,1)S(1)} %hidden.4.lm_ref, bf16[1344,768]{1,0:T(8,128)(2,1)} %hidden.5.lo_ref, bf16[768,2048]{1,0:T(8,128)(2,1)} %get-tuple-element.456.n2_ref.nm_ref, bf16[768,2048]{1,0:T(8,128)(2,1)} %get-tuple-element.458.n2_ref.no_ref, ...), custom_call_target="tpu_custom_call" | custom-call | flops 8455716864 | bytes 5505024 | tf_op jit(solution)/shard_map/feed_grads/pallas_call | solution.py:483
  230.6 5.6 %all-gather.8.cloned.1.call-done.w_ref = bf16[768,2048]{1,0:T(8,128)(2,1)} async-done(((bf16[768,512]{1,0:T(8,128)(2,1)}), bf16[768,2048]{1,0:T(8,128)(2,1)}) %all-gather.8.cloned.1.call-update) | async-done | bytes 3145744 | tf_op jit(solution)/shard_map/all_gather | solution.py:166
  236.1 7.7 %hidden.6.lm_ref = bf16[768,768]{1,0:T(8,128)(2,1)} custom-call(bf16[768,2048]{1,0:T(8,128)(2,1)} %all-gather.8.cloned.1.call-done.w_ref, bf16[768,2048]{1,0:T(8,128)(2,1)} %get-tuple-element.456.n2_ref.nm_ref, bf16[768,2048]{1,0:T(8,128)(2,1)} %get-tuple-element.457.df_ref.dm_ref), custom_call_target="tpu_custom_call" | custom-call | flops 2415919104 | bytes 3145728 | tf_op jit(solution)/shard_map/hidden/pallas_call | solution.py:451
  243.9 6.4 %hidden.7.lo_ref = bf16[768,768]{1,0:T(8,128)(2,1)} custom-call(bf16[768,2048]{1,0:T(8,128)(2,1)S(1)} %copy-done.7, bf16[768,2048]{1,0:T(8,128)(2,1)} %get-tuple-element.458.n2_ref.no_ref, bf16[768,2048]{1,0:T(8,128)(2,1)} %get-tuple-element.459.df_ref.do_ref), custom_call_target="tpu_custom_call" | custom-call | flops 2415919104 | bytes 3145728 | tf_op jit(solution)/shard_map/hidden/pallas_call | solution.py:451
  250.3 12.0 %feed_grads.3 = bf16[768,2048]{1,0:T(8,128)(2,1)} custom-call(bf16[768,768]{1,0:T(8,128)(2,1)} %hidden.6.lm_ref, bf16[768,768]{1,0:T(8,128)(2,1)} %hidden.7.lo_ref, bf16[768,2048]{1,0:T(8,128)(2,1)} %get-tuple-element.456.n2_ref.nm_ref, bf16[768,2048]{1,0:T(8,128)(2,1)} %get-tuple-element.458.n2_ref.no_ref, ...), custom_call_target="tpu_custom_call" | custom-call | flops 4831838208 | bytes 3145728 | tf_op jit(solution)/shard_map/feed_grads/pallas_call | solution.py:483
  262.4 6.1 %fusion.37 = bf16[768,2048]{1,0:T(8,128)(2,1)S(1)} fusion(bf16[1344,2048]{1,0:T(8,128)(2,1)} %all-gather.4.cloned.1.call-done.w_ref, bf16[1344,768]{1,0:T(8,128)(2,1)} %hidden.5.lo_ref), kind=kOutput, calls=%fused_computation.130 | convolution fusion | flops 2820145152 | bytes 8192000 | tf_op jit(solution)/shard_map/dot_general | solution.py:21
  268.6 86.4 %conditional.8 = (f32[192,2048]{1,0:T(8,128)}, f32[1,2048]{1,0:T(1,128)S(1)}, bf16[768,2048]{1,0:T(8,128)(2,1)}, bf16[768,2048]{1,0:T(8,128)(2,1)}, bf16[192,204...) conditional(s32[]{:T(128)} %bitcast.69, () %tuple.87, ...), branch_computations={%region_8.9_spmd, %region_9.12_spmd} | conditional | flops 11311054848 | bytes 239641952 | solution.py:34
  271.5 3.5 fusion.3
  282.5 3.5 fusion.9
  287.2 3.6 fusion.7
  291.9 7.0 %collective-permute-done.36 = bf16[192,2048]{1,0:T(8,128)(2,1)S(1)} collective-permute-done((bf16[192,2048]{1,0:T(8,128)(2,1)S(1)}, bf16[192,2048]{1,0:T(8,128)(2,1)S(1)}, u32[]{:S(2)}, u32[]{:S(2)}) %collective-permute-start.36) | collective-permute-done | bytes 786464 | tf_op jit(solution)/shard_map/cond/branch_1_fun/ppermute | solution.py:43
  304.1 7.3 %collective-permute-done.39 = bf16[96,2048]{1,0:T(8,128)(2,1)S(1)} collective-permute-done((bf16[96,2048]{1,0:T(8,128)(2,1)S(1)}, bf16[96,2048]{1,0:T(8,128)(2,1)S(1)}, u32[]{:S(2)}, u32[]{:S(2)}) %collective-permute-start.39) | collective-permute-done | bytes 393248 | tf_op jit(solution)/shard_map/cond/branch_1_fun/ppermute | solution.py:43
  314.0 3.1 multiply_convert_fusion.1
  321.3 8.0 %collective-permute-done.40.refs_1_ = bf16[96,2048]{1,0:T(8,128)(2,1)S(1)} collective-permute-done((bf16[96,2048]{1,0:T(8,128)(2,1)S(1)}, bf16[96,2048]{1,0:T(8,128)(2,1)S(1)}, u32[]{:S(2)}, u32[]{:S(2)}) %collective-permute-start.40) | collective-permute-done | bytes 393248 | tf_op jit(solution)/shard_map/cond/branch_1_fun/ppermute | solution.py:43
  339.1 4.7 collective-permute-done.42.refs_3_
  344.8 3.7 join.7
  348.5 3.7 convolution_convert_fusion.2
  355.0 83.9 %conditional.9 = (f32[192,2048]{1,0:T(8,128)}, bf16[656,2048]{1,0:T(8,128)(2,1)}, bf16[192,2048]{1,0:T(8,128)(2,1)}, bf16[192,2048]{1,0:T(8,128)(2,1)}, bf16[896,512]{1,0:T(8,128)(2,1)}) conditional(s32[]{:T(128)} %bitcast.69, () %tuple.86, (bf16[656,2048]{1,0:T(8,128)(2,1)S(1)}, bf16[768,2048]{1,0:T(8,128)(2,1)}, s32[17]{0:T(128)S(1)}, ...), branch_computations={%region_13.0_spmd, %region_14.19_spmd} | conditional | flops 21800714240 | bytes 172524608 | solution.py:34
  357.6 3.7 convolution_convert_fusion.5.doo
  361.3 16.1 %attn_backward.1 = (bf16[768,256]{1,0:T(8,128)(2,1)}, bf16[768,256]{1,0:T(8,128)(2,1)}, f32[768,128]{1,0:T(8,128)}, f32[768,128]{1,0:T(8,128)}, bf16[768,128]{1,0:T(8,128)(2,1)}, /*index=5*/bf16[768,128]{1,0:T(8,128)(2,1)}) custom-call(s32[17]{0:T(128)S(1)} %get-tuple-element.267.starts_ref, bf16[768,256]{1,0:T(8,128)(2,1)} %get-tuple-element.268.qm, ...), custom_call_target="tpu_custom_call" | custom-call | flops 14495514624 | bytes 6291456 | tf_op jit(solution)/shard_map/cond/branch_1_fun/attn_backward/pallas_call | solution.py:413
  380.2 2.9 convolution_convert_fusion.3
  396.2 4.2 fusion.21
  400.4 3.0 fusion.23
  403.4 3.0 fusion.26
  408.0 3.3 fusion.60
  411.3 3.4 add_convert_fusion.12
  416.6 7.4 %collective-permute-done.53 = bf16[192,2048]{1,0:T(8,128)(2,1)S(1)} collective-permute-done((bf16[192,2048]{1,0:T(8,128)(2,1)S(1)}, bf16[192,2048]{1,0:T(8,128)(2,1)S(1)}, u32[]{:S(2)}, u32[]{:S(2)}) %collective-permute-start.53) | collective-permute-done | bytes 786464 | tf_op jit(solution)/shard_map/cond/branch_1_fun/ppermute | solution.py:43
  426.3 2.9 fusion.61
  438.9 54.8 %conditional.10 = (bf16[192,2048]{1,0:T(8,128)(2,1)}, f32[512,2816]{1,0:T(8,128)}, bf16[1344,512]{1,0:T(8,128)(2,1)}, bf16[896,512]{1,0:T(8,128)(2,1)}, bf16[768...) conditional(s32[]{:T(128)} %bitcast.69, () %tuple.85, ...), branch_computations={%region_21.22_spmd, %region_22.25_spmd} | conditional | flops 16910528 | bytes 76845152 | solution.py:34
  452.8 3.1 pad_maximum_fusion.6
  458.7 3.0 hold.5
  467.1 3.3 add_convert_fusion.20
  471.5 6.7 %finish.3.rest_0_ = f32[512,2816]{1,0:T(8,128)} custom-call(s32[1]{0:T(128)} %get-tuple-element.321.c_ref, bf16[1344,512]{1,0:T(8,128)(2,1)S(1)} %copy-done.10, bf16[1344,512]{1,0:T(8,128)(2,1)} %collective-permute-done.2.refs_1_, bf16[896,512]{1,0:T(8,128)(2,1)} %get-tuple-element.323.refs_2_, bf16[896,512]{1,0:T(8,128)(2,1)} %collective-permute-done.3.refs_3_, ...), custom_call_target="tpu_custom_call" | custom-call | tf_op jit(solution)/shard_map/cond/branch_1_fun/finish/pallas_call | solution.py:565
  478.2 8.2 %collective-permute-done.7.v_ref = bf16[960,512]{1,0:T(8,128)(2,1)} collective-permute-done((bf16[960,512]{1,0:T(8,128)(2,1)}, bf16[960,512]{1,0:T(8,128)(2,1)}, u32[]{:S(2)}, u32[]{:S(2)}) %collective-permute-start.7) | collective-permute-done | bytes 983072 | tf_op jit(solution)/shard_map/cond/branch_1_fun/ppermute | solution.py:43
  486.4 3.0 hold.6
  490.5 3.2 maximum_select_fusion
  493.7 31.8 %conditional.11 = (f32[512,2816]{1,0:T(8,128)}, f32[2816,512]{1,0:T(8,128)}, f32[512,1024]{1,0:T(8,128)}, f32[512,256]{1,0:T(8,128)}, f32[512,256]{1,0:T(8,128)}...) conditional(s32[]{:T(128)} %bitcast.69, () %tuple.78, ...), branch_computations={%region_25.26_spmd, %region_26.27_spmd} | conditional | flops 7077889 | bytes 31080852 | solution.py:34
  495.7 5.7 %finish.5.rest_1_ = f32[2816,512]{1,0:T(8,128)} custom-call(s32[1]{0:T(128)} %get-tuple-element.330.c_ref, bf16[1344,512]{1,0:T(8,128)(2,1)} %get-tuple-element.331.refs_0_, bf16[1344,512]{1,0:T(8,128)(2,1)} %get-tuple-element.332.refs_1_, bf16[960,512]{1,0:T(8,128)(2,1)} %get-tuple-element.337.refs_6_.refs_2_, ...), custom_call_target="tpu_custom_call" | custom-call | tf_op jit(solution)/shard_map/cond/branch_1_fun/finish/pallas_call | solution.py:565
  501.4 6.7 %finish.4.rest_0_ = f32[512,2816]{1,0:T(8,128)} custom-call(s32[1]{0:T(128)} %get-tuple-element.330.c_ref, bf16[1344,512]{1,0:T(8,128)(2,1)S(1)} %copy-done.11, bf16[1344,512]{1,0:T(8,128)(2,1)} %get-tuple-element.332.refs_1_, bf16[896,512]{1,0:T(8,128)(2,1)} %get-tuple-element.333.refs_2_, bf16[896,512]{1,0:T(8,128)(2,1)} %get-tuple-element.334.refs_3_, ...), custom_call_target="tpu_custom_call" | custom-call | tf_op jit(solution)/shard_map/cond/branch_1_fun/finish/pallas_call | solution.py:565
  518.3 4.5 finish_attn.1
  (403 shorter events, 182.6 us)
Async XLA Ops:
  7.2 62.2 %all-gather.6.cloned.1.call-start = ((), (), s32[]{:S(2)}) async-start(), calls=%async_computation.4 | async-start | bytes 3358720 | tf_op jit(solution)/shard_map/all_gather | solution.py:166
  10.7 186.8 %all-gather.4.cloned.1.call-start = ((), (), s32[]{:S(2)}) async-start(), calls=%async_computation.3 | async-start | bytes 6881280 | tf_op jit(solution)/shard_map/all_gather | solution.py:166
  14.1 26.6 %collective-permute-start.59 = (bf16[96,2048]{1,0:T(8,128)(2,1)}, bf16[96,2048]{1,0:T(8,128)(2,1)}, u32[]{:S(2)}, u32[]{:S(2)}) collective-permute-start(bf16[96,2048]{1,0:T(8,128)(2,1)} %get-tuple-element.202.refs_0_), channel_id=1, source_target_pairs={{0,4},{2,6},{4,0},{6,2},{1,5},{3,7},{5,1},{7,3},{8,12},{10,14},{12... | collective-permute-start | bytes 1179656 | tf_op jit(solution)/shard_map/cond/branch_1_fun/ppermute | solution.py:43
  17.0 23.7 %collective-permute-start.61 = (bf16[96,2048]{1,0:T(8,128)(2,1)}, bf16[96,2048]{1,0:T(8,128)(2,1)}, u32[]{:S(2)}, u32[]{:S(2)}) collective-permute-start(bf16[96,2048]{1,0:T(8,128)(2,1)} %get-tuple-element.202.refs_0_), channel_id=1, source_target_pairs={{0,1},{1,0},{2,3},{3,2},{4,5},{5,4},{6,7},{7,6},{8,9},{9,8},{10,11... | collective-permute-start | bytes 1179656 | tf_op jit(solution)/shard_map/cond/branch_1_fun/ppermute | solution.py:51
  18.6 22.2 %collective-permute-start.60 = (bf16[96,2048]{1,0:T(8,128)(2,1)}, bf16[96,2048]{1,0:T(8,128)(2,1)}, u32[]{:S(2)}, u32[]{:S(2)}) collective-permute-start(bf16[96,2048]{1,0:T(8,128)(2,1)} %get-tuple-element.206.refs_4_), channel_id=1, source_target_pairs={{0,1},{1,0},{2,3},{3,2},{4,5},{5,4},{6,7},{7,6},{8,9},{9,8},{10,11... | collective-permute-start | bytes 1179656 | tf_op jit(solution)/shard_map/cond/branch_1_fun/ppermute | solution.py:51
  19.1 21.7 %collective-permute-start.62 = (bf16[96,2048]{1,0:T(8,128)(2,1)}, bf16[96,2048]{1,0:T(8,128)(2,1)}, u32[]{:S(2)}, u32[]{:S(2)}) collective-permute-start(bf16[96,2048]{1,0:T(8,128)(2,1)} %get-tuple-element.206.refs_4_), channel_id=1, source_target_pairs={{0,4},{2,6},{4,0},{6,2},{1,5},{3,7},{5,1},{7,3},{8,12},{10,14},{12... | collective-permute-start | bytes 1179656 | tf_op jit(solution)/shard_map/cond/branch_1_fun/ppermute | solution.py:43
  40.8 10.3 %collective-permute-start.63 = (bf16[96,2048]{1,0:T(8,128)(2,1)}, bf16[96,2048]{1,0:T(8,128)(2,1)S(1)}, u32[]{:S(2)}, u32[]{:S(2)}) collective-permute-start(bf16[96,2048]{1,0:T(8,128)(2,1)} %collective-permute-done.59.refs_1_), channel_id=1, source_target_pairs={{0,1},{1,0},{2,3},{3,2},{4,5},{5,4},{6,7},{7,6},{8,9},{9,8},{10,11... | collective-permute-start | bytes 1179656 | tf_op jit(solution)/shard_map/cond/branch_1_fun/ppermute | solution.py:51
  42.8 9.7 %collective-permute-start.64 = (bf16[96,2048]{1,0:T(8,128)(2,1)}, bf16[96,2048]{1,0:T(8,128)(2,1)S(1)}, u32[]{:S(2)}, u32[]{:S(2)}) collective-permute-start(bf16[96,2048]{1,0:T(8,128)(2,1)} %collective-permute-done.60.refs_5_), channel_id=1, source_target_pairs={{0,4},{2,6},{4,0},{6,2},{1,5},{3,7},{5,1},{7,3},{8,12},{10,14},{12... | collective-permute-start | bytes 1179656 | tf_op jit(solution)/shard_map/cond/branch_1_fun/ppermute | solution.py:43
  56.8 6.1 %collective-permute-start.65 = (bf16[768,2048]{1,0:T(8,128)(2,1)}, bf16[768,2048]{1,0:T(8,128)(2,1)}, u32[]{:S(2)}, u32[]{:S(2)}) collective-permute-start(bf16[768,2048]{1,0:T(8,128)(2,1)} %join.4), channel_id=1, source_target_pairs={{0,2},{2,0},{4,6},{6,4},{1,3},{3,1},{5,7},{7,5},{8,10},{10,8},{12,... | collective-permute-start | bytes 9437192 | tf_op jit(solution)/shard_map/cond/branch_1_fun/ppermute | solution.py:47
  66.3 169.8 %all-gather.8.cloned.1.call-start = ((), (), s32[]{:S(2)}) async-start(), calls=%async_computation.6 | async-start | bytes 3932160 | tf_op jit(solution)/shard_map/all_gather | solution.py:166
  68.8 286.2 %reduce-scatter.4.cloned.1.call-start = ((), (), s32[]{:S(2)}) async-start(), calls=%async_computation.5 | async-start | bytes 6881280 | tf_op jit(solution)/shard_map/reduce_scatter | solution.py:170
  72.3 18.0 %collective-permute-start.14 = (bf16[96,2048]{1,0:T(8,128)(2,1)S(1)}, bf16[96,2048]{1,0:T(8,128)(2,1)}, u32[]{:S(2)}, u32[]{:S(2)}) collective-permute-start(bf16[96,2048]{1,0:T(8,128)(2,1)S(1)} %get-tuple-element.233.refs_0_), channel_id=1, source_target_pairs={{0,4},{2,6},{4,0},{6,2},{1,5},{3,7},{5,1},{7,3},{8,12},{10,14},{12... | collective-permute-start | bytes 1179656 | tf_op jit(solution)/shard_map/cond/branch_1_fun/ppermute | solution.py:43
  73.9 19.1 %collective-permute-start.16 = (bf16[96,2048]{1,0:T(8,128)(2,1)S(1)}, bf16[96,2048]{1,0:T(8,128)(2,1)}, u32[]{:S(2)}, u32[]{:S(2)}) collective-permute-start(bf16[96,2048]{1,0:T(8,128)(2,1)S(1)} %get-tuple-element.233.refs_0_), channel_id=1, source_target_pairs={{0,1},{1,0},{2,3},{3,2},{4,5},{5,4},{6,7},{7,6},{8,9},{9,8},{10,11... | collective-permute-start | bytes 1179656 | tf_op jit(solution)/shard_map/cond/branch_1_fun/ppermute | solution.py:51
  75.4 17.6 %collective-permute-start.15 = (bf16[96,2048]{1,0:T(8,128)(2,1)S(1)}, bf16[96,2048]{1,0:T(8,128)(2,1)}, u32[]{:S(2)}, u32[]{:S(2)}) collective-permute-start(bf16[96,2048]{1,0:T(8,128)(2,1)S(1)} %get-tuple-element.237.refs_4_), channel_id=1, source_target_pairs={{0,1},{1,0},{2,3},{3,2},{4,5},{5,4},{6,7},{7,6},{8,9},{9,8},{10,11... | collective-permute-start | bytes 1179656 | tf_op jit(solution)/shard_map/cond/branch_1_fun/ppermute | solution.py:51
  75.9 17.1 %collective-permute-start.17 = (bf16[96,2048]{1,0:T(8,128)(2,1)S(1)}, bf16[96,2048]{1,0:T(8,128)(2,1)}, u32[]{:S(2)}, u32[]{:S(2)}) collective-permute-start(bf16[96,2048]{1,0:T(8,128)(2,1)S(1)} %get-tuple-element.237.refs_4_), channel_id=1, source_target_pairs={{0,4},{2,6},{4,0},{6,2},{1,5},{3,7},{5,1},{7,3},{8,12},{10,14},{12... | collective-permute-start | bytes 1179656 | tf_op jit(solution)/shard_map/cond/branch_1_fun/ppermute | solution.py:43
  84.7 10.3 %collective-permute-start.18 = (bf16[768,128]{1,0:T(8,128)(2,1)}, bf16[768,128]{1,0:T(8,128)(2,1)}, u32[]{:S(2)}, u32[]{:S(2)}) collective-permute-start(bf16[768,128]{1,0:T(8,128)(2,1)} %get-tuple-element.697.ko), channel_id=1, source_target_pairs={{0,2},{2,0},{4,6},{6,4},{1,3},{3,1},{5,7},{7,5},{8,10},{10,8},{12,... | collective-permute-start | bytes 589832 | tf_op jit(solution)/shard_map/cond/branch_1_fun/ppermute | solution.py:47
  93.0 16.4 %collective-permute-start.20 = (bf16[96,2048]{1,0:T(8,128)(2,1)}, bf16[96,2048]{1,0:T(8,128)(2,1)}, u32[]{:S(2)}, u32[]{:S(2)}) collective-permute-start(bf16[96,2048]{1,0:T(8,128)(2,1)} %collective-permute-done.14.refs_1_), channel_id=1, source_target_pairs={{0,1},{1,0},{2,3},{3,2},{4,5},{5,4},{6,7},{7,6},{8,9},{9,8},{10,11... | collective-permute-start | bytes 1179656 | tf_op jit(solution)/shard_map/cond/branch_1_fun/ppermute | solution.py:51
  94.5 14.9 %collective-permute-start.21 = (bf16[96,2048]{1,0:T(8,128)(2,1)}, bf16[96,2048]{1,0:T(8,128)(2,1)}, u32[]{:S(2)}, u32[]{:S(2)}) collective-permute-start(bf16[96,2048]{1,0:T(8,128)(2,1)} %collective-permute-done.15.refs_5_), channel_id=1, source_target_pairs={{0,4},{2,6},{4,0},{6,2},{1,5},{3,7},{5,1},{7,3},{8,12},{10,14},{12... | collective-permute-start | bytes 1179656 | tf_op jit(solution)/shard_map/cond/branch_1_fun/ppermute | solution.py:43
  120.3 19.9 %collective-permute-start.24 = (bf16[192,2048]{1,0:T(8,128)(2,1)}, bf16[192,2048]{1,0:T(8,128)(2,1)}, u32[]{:S(2)}, u32[]{:S(2)}) collective-permute-start(bf16[192,2048]{1,0:T(8,128)(2,1)} %bitcast.34), channel_id=1, source_target_pairs={{0,4},{2,6},{4,0},{6,2},{1,5},{3,7},{5,1},{7,3},{8,12},{10,14},{12... | collective-permute-start | bytes 2359304 | tf_op jit(solution)/shard_map/cond/branch_1_fun/ppermute | solution.py:43
  121.8 19.6 %collective-permute-start.25 = (bf16[192,2048]{1,0:T(8,128)(2,1)}, bf16[192,2048]{1,0:T(8,128)(2,1)}, u32[]{:S(2)}, u32[]{:S(2)}) collective-permute-start(bf16[192,2048]{1,0:T(8,128)(2,1)} %bitcast.35), channel_id=1, source_target_pairs={{0,1},{1,0},{2,3},{3,2},{4,5},{5,4},{6,7},{7,6},{8,9},{9,8},{10,11... | collective-permute-start | bytes 2359304 | tf_op jit(solution)/shard_map/cond/branch_1_fun/ppermute | solution.py:51
  142.8 10.1 %collective-permute-start.27 = (bf16[96,2048]{1,0:T(8,128)(2,1)S(1)}, bf16[96,2048]{1,0:T(8,128)(2,1)S(1)}, u32[]{:S(2)}, u32[]{:S(2)}) collective-permute-start(bf16[96,2048]{1,0:T(8,128)(2,1)S(1)} %slice.276), channel_id=1, source_target_pairs={{0,4},{2,6},{4,0},{6,2},{1,5},{3,7},{5,1},{7,3},{8,12},{10,14},{12... | collective-permute-start | bytes 1179656 | tf_op jit(solution)/shard_map/cond/branch_1_fun/ppermute | solution.py:43
  144.9 9.8 %collective-permute-start.26 = (bf16[96,2048]{1,0:T(8,128)(2,1)S(1)}, bf16[96,2048]{1,0:T(8,128)(2,1)S(1)}, u32[]{:S(2)}, u32[]{:S(2)}) collective-permute-start(bf16[96,2048]{1,0:T(8,128)(2,1)S(1)} %slice.274), channel_id=1, source_target_pairs={{0,1},{1,0},{2,3},{3,2},{4,5},{5,4},{6,7},{7,6},{8,9},{9,8},{10,11... | collective-permute-start | bytes 1179656 | tf_op jit(solution)/shard_map/cond/branch_1_fun/ppermute | solution.py:51
  159.2 12.1 %collective-permute-start.28 = (bf16[96,2048]{1,0:T(8,128)(2,1)S(1)}, bf16[96,2048]{1,0:T(8,128)(2,1)S(1)}, u32[]{:S(2)}, u32[]{:S(2)}) collective-permute-start(bf16[96,2048]{1,0:T(8,128)(2,1)S(1)} %get-tuple-element.614.refs_0_), channel_id=1, source_target_pairs={{0,4},{2,6},{4,0},{6,2},{1,5},{3,7},{5,1},{7,3},{8,12},{10,14},{12... | collective-permute-start | bytes 1179656 | tf_op jit(solution)/shard_map/cond/branch_1_fun/ppermute | solution.py:43
  160.7 12.1 %collective-permute-start.31 = (bf16[96,2048]{1,0:T(8,128)(2,1)S(1)}, bf16[96,2048]{1,0:T(8,128)(2,1)S(1)}, u32[]{:S(2)}, u32[]{:S(2)}) collective-permute-start(bf16[96,2048]{1,0:T(8,128)(2,1)S(1)} %get-tuple-element.613.refs_4_), channel_id=1, source_target_pairs={{0,1},{1,0},{2,3},{3,2},{4,5},{5,4},{6,7},{7,6},{8,9},{9,8},{10,11... | collective-permute-start | bytes 1179656 | tf_op jit(solution)/shard_map/cond/branch_1_fun/ppermute | solution.py:51
  161.2 19.9 %collective-permute-start.29 = (bf16[96,2048]{1,0:T(8,128)(2,1)S(1)}, bf16[96,2048]{1,0:T(8,128)(2,1)S(1)}, u32[]{:S(2)}, u32[]{:S(2)}) collective-permute-start(bf16[96,2048]{1,0:T(8,128)(2,1)S(1)} %get-tuple-element.614.refs_0_), channel_id=1, source_target_pairs={{0,1},{1,0},{2,3},{3,2},{4,5},{5,4},{6,7},{7,6},{8,9},{9,8},{10,11... | collective-permute-start | bytes 1179656 | tf_op jit(solution)/shard_map/cond/branch_1_fun/ppermute | solution.py:51
  162.7 18.5 %collective-permute-start.32 = (bf16[96,2048]{1,0:T(8,128)(2,1)S(1)}, bf16[96,2048]{1,0:T(8,128)(2,1)S(1)}, u32[]{:S(2)}, u32[]{:S(2)}) collective-permute-start(bf16[96,2048]{1,0:T(8,128)(2,1)S(1)} %get-tuple-element.613.refs_4_), channel_id=1, source_target_pairs={{0,4},{2,6},{4,0},{6,2},{1,5},{3,7},{5,1},{7,3},{8,12},{10,14},{12... | collective-permute-start | bytes 1179656 | tf_op jit(solution)/shard_map/cond/branch_1_fun/ppermute | solution.py:43
  171.3 14.8 %collective-permute-start.30 = (bf16[96,2048]{1,0:T(8,128)(2,1)S(1)}, bf16[96,2048]{1,0:T(8,128)(2,1)S(1)}, u32[]{:S(2)}, u32[]{:S(2)}) collective-permute-start(bf16[96,2048]{1,0:T(8,128)(2,1)S(1)} %collective-permute-done.28.refs_1_), channel_id=1, source_target_pairs={{0,1},{1,0},{2,3},{3,2},{4,5},{5,4},{6,7},{7,6},{8,9},{9,8},{10,11... | collective-permute-start | bytes 1179656 | tf_op jit(solution)/shard_map/cond/branch_1_fun/ppermute | solution.py:51
  172.7 13.4 %collective-permute-start.33 = (bf16[96,2048]{1,0:T(8,128)(2,1)S(1)}, bf16[96,2048]{1,0:T(8,128)(2,1)S(1)}, u32[]{:S(2)}, u32[]{:S(2)}) collective-permute-start(bf16[96,2048]{1,0:T(8,128)(2,1)S(1)} %collective-permute-done.31.refs_5_), channel_id=1, source_target_pairs={{0,4},{2,6},{4,0},{6,2},{1,5},{3,7},{5,1},{7,3},{8,12},{10,14},{12... | collective-permute-start | bytes 1179656 | tf_op jit(solution)/shard_map/cond/branch_1_fun/ppermute | solution.py:43
  173.3 18.0 %collective-permute-start.23 = (bf16[768,2048]{1,0:T(8,128)(2,1)}, bf16[768,2048]{1,0:T(8,128)(2,1)}, u32[]{:S(2)}, u32[]{:S(2)}) collective-permute-start(bf16[768,2048]{1,0:T(8,128)(2,1)} %join.5), channel_id=1, source_target_pairs={{0,2},{2,0},{4,6},{6,4},{1,3},{3,1},{5,7},{7,5},{8,10},{10,8},{12,... | collective-permute-start | bytes 9437192 | tf_op jit(solution)/shard_map/cond/branch_1_fun/ppermute | solution.py:47
  191.3 6.1 %collective-permute-start.34 = (bf16[768,2048]{1,0:T(8,128)(2,1)}, bf16[768,2048]{1,0:T(8,128)(2,1)}, u32[]{:S(2)}, u32[]{:S(2)}) collective-permute-start(bf16[768,2048]{1,0:T(8,128)(2,1)} %join.6), channel_id=1, source_target_pairs={{0,2},{2,0},{4,6},{6,4},{1,3},{3,1},{5,7},{7,5},{8,10},{10,8},{12,... | collective-permute-start | bytes 9437192 | tf_op jit(solution)/shard_map/cond/branch_1_fun/ppermute | solution.py:47
  230.5 208.4 %reduce-scatter.6.cloned.1.call-start = ((), (), s32[]{:S(2)}) async-start(), calls=%async_computation.7 | async-start | bytes 3932160 | tf_op jit(solution)/shard_map/reduce_scatter | solution.py:170
  262.3 231.4 %reduce-scatter.8.cloned.1.call-start = ((), (), s32[]{:S(2)}) async-start(), calls=%async_computation.8 | async-start | bytes 3358720 | tf_op jit(solution)/shard_map/reduce_scatter | solution.py:170
  270.7 6.3 %collective-permute-start.35 = (bf16[768,2048]{1,0:T(8,128)(2,1)S(1)}, bf16[768,2048]{1,0:T(8,128)(2,1)S(1)}, u32[]{:S(2)}, u32[]{:S(2)}) collective-permute-start(bf16[768,2048]{1,0:T(8,128)(2,1)S(1)} %add_convert_fusion.7), channel_id=1, source_target_pairs={{0,2},{2,0},{4,6},{6,4},{1,3},{3,1},{5,7},{7,5},{8,10},{10,8},{12,... | collective-permute-start | bytes 9437192 | tf_op jit(solution)/shard_map/cond/branch_1_fun/ppermute | solution.py:47
  279.4 19.4 %collective-permute-start.36 = (bf16[192,2048]{1,0:T(8,128)(2,1)S(1)}, bf16[192,2048]{1,0:T(8,128)(2,1)S(1)}, u32[]{:S(2)}, u32[]{:S(2)}) collective-permute-start(bf16[192,2048]{1,0:T(8,128)(2,1)S(1)} %bitcast.146), channel_id=1, source_target_pairs={{0,4},{2,6},{4,0},{6,2},{1,5},{3,7},{5,1},{7,3},{8,12},{10,14},{12... | collective-permute-start | bytes 2359304 | tf_op jit(solution)/shard_map/cond/branch_1_fun/ppermute | solution.py:43
  281.0 19.2 %collective-permute-start.37 = (bf16[192,2048]{1,0:T(8,128)(2,1)S(1)}, bf16[192,2048]{1,0:T(8,128)(2,1)}, u32[]{:S(2)}, u32[]{:S(2)}) collective-permute-start(bf16[192,2048]{1,0:T(8,128)(2,1)S(1)} %bitcast.147), channel_id=1, source_target_pairs={{0,1},{1,0},{2,3},{3,2},{4,5},{5,4},{6,7},{7,6},{8,9},{9,8},{10,11... | collective-permute-start | bytes 2359304 | tf_op jit(solution)/shard_map/cond/branch_1_fun/ppermute | solution.py:51
  287.1 45.1 %collective-permute-start.46 = (bf16[768,2048]{1,0:T(8,128)(2,1)S(1)}, bf16[768,2048]{1,0:T(8,128)(2,1)S(1)}, u32[]{:S(2)}, u32[]{:S(2)}) collective-permute-start(bf16[768,2048]{1,0:T(8,128)(2,1)S(1)} %add_convert_fusion.5), channel_id=1, source_target_pairs={{0,2},{2,0},{4,6},{6,4},{1,3},{3,1},{5,7},{7,5},{8,10},{10,8},{12,... | collective-permute-start | bytes 9437192 | tf_op jit(solution)/shard_map/cond/branch_1_fun/ppermute | solution.py:47
  301.6 9.8 %collective-permute-start.39 = (bf16[96,2048]{1,0:T(8,128)(2,1)S(1)}, bf16[96,2048]{1,0:T(8,128)(2,1)S(1)}, u32[]{:S(2)}, u32[]{:S(2)}) collective-permute-start(bf16[96,2048]{1,0:T(8,128)(2,1)S(1)} %slice.288), channel_id=1, source_target_pairs={{0,4},{2,6},{4,0},{6,2},{1,5},{3,7},{5,1},{7,3},{8,12},{10,14},{12... | collective-permute-start | bytes 1179656 | tf_op jit(solution)/shard_map/cond/branch_1_fun/ppermute | solution.py:43
  302.5 9.6 %collective-permute-start.38 = (bf16[96,2048]{1,0:T(8,128)(2,1)S(1)}, bf16[96,2048]{1,0:T(8,128)(2,1)S(1)}, u32[]{:S(2)}, u32[]{:S(2)}) collective-permute-start(bf16[96,2048]{1,0:T(8,128)(2,1)S(1)} %slice.286), channel_id=1, source_target_pairs={{0,1},{1,0},{2,3},{3,2},{4,5},{5,4},{6,7},{7,6},{8,9},{9,8},{10,11... | collective-permute-start | bytes 1179656 | tf_op jit(solution)/shard_map/cond/branch_1_fun/ppermute | solution.py:51
  317.2 12.1 %collective-permute-start.40 = (bf16[96,2048]{1,0:T(8,128)(2,1)S(1)}, bf16[96,2048]{1,0:T(8,128)(2,1)S(1)}, u32[]{:S(2)}, u32[]{:S(2)}) collective-permute-start(bf16[96,2048]{1,0:T(8,128)(2,1)S(1)} %get-tuple-element.636.refs_0_), channel_id=1, source_target_pairs={{0,4},{2,6},{4,0},{6,2},{1,5},{3,7},{5,1},{7,3},{8,12},{10,14},{12... | collective-permute-start | bytes 1179656 | tf_op jit(solution)/shard_map/cond/branch_1_fun/ppermute | solution.py:43
  318.6 12.1 %collective-permute-start.43 = (bf16[96,2048]{1,0:T(8,128)(2,1)S(1)}, bf16[96,2048]{1,0:T(8,128)(2,1)S(1)}, u32[]{:S(2)}, u32[]{:S(2)}) collective-permute-start(bf16[96,2048]{1,0:T(8,128)(2,1)S(1)} %get-tuple-element.635.refs_4_), channel_id=1, source_target_pairs={{0,1},{1,0},{2,3},{3,2},{4,5},{5,4},{6,7},{7,6},{8,9},{9,8},{10,11... | collective-permute-start | bytes 1179656 | tf_op jit(solution)/shard_map/cond/branch_1_fun/ppermute | solution.py:51
  320.1 19.0 %collective-permute-start.41 = (bf16[96,2048]{1,0:T(8,128)(2,1)S(1)}, bf16[96,2048]{1,0:T(8,128)(2,1)S(1)}, u32[]{:S(2)}, u32[]{:S(2)}) collective-permute-start(bf16[96,2048]{1,0:T(8,128)(2,1)S(1)} %get-tuple-element.636.refs_0_), channel_id=1, source_target_pairs={{0,1},{1,0},{2,3},{3,2},{4,5},{5,4},{6,7},{7,6},{8,9},{9,8},{10,11... | collective-permute-start | bytes 1179656 | tf_op jit(solution)/shard_map/cond/branch_1_fun/ppermute | solution.py:51
  320.7 18.5 %collective-permute-start.44 = (bf16[96,2048]{1,0:T(8,128)(2,1)S(1)}, bf16[96,2048]{1,0:T(8,128)(2,1)S(1)}, u32[]{:S(2)}, u32[]{:S(2)}) collective-permute-start(bf16[96,2048]{1,0:T(8,128)(2,1)S(1)} %get-tuple-element.635.refs_4_), channel_id=1, source_target_pairs={{0,4},{2,6},{4,0},{6,2},{1,5},{3,7},{5,1},{7,3},{8,12},{10,14},{12... | collective-permute-start | bytes 1179656 | tf_op jit(solution)/shard_map/cond/branch_1_fun/ppermute | solution.py:43
  329.3 14.6 %collective-permute-start.42 = (bf16[96,2048]{1,0:T(8,128)(2,1)S(1)}, bf16[96,2048]{1,0:T(8,128)(2,1)S(1)}, u32[]{:S(2)}, u32[]{:S(2)}) collective-permute-start(bf16[96,2048]{1,0:T(8,128)(2,1)S(1)} %collective-permute-done.40.refs_1_), channel_id=1, source_target_pairs={{0,1},{1,0},{2,3},{3,2},{4,5},{5,4},{6,7},{7,6},{8,9},{9,8},{10,11... | collective-permute-start | bytes 1179656 | tf_op jit(solution)/shard_map/cond/branch_1_fun/ppermute | solution.py:51
  330.8 13.1 %collective-permute-start.45 = (bf16[96,2048]{1,0:T(8,128)(2,1)S(1)}, bf16[96,2048]{1,0:T(8,128)(2,1)S(1)}, u32[]{:S(2)}, u32[]{:S(2)}) collective-permute-start(bf16[96,2048]{1,0:T(8,128)(2,1)S(1)} %collective-permute-done.43.refs_5_), channel_id=1, source_target_pairs={{0,4},{2,6},{4,0},{6,2},{1,5},{3,7},{5,1},{7,3},{8,12},{10,14},{12... | collective-permute-start | bytes 1179656 | tf_op jit(solution)/shard_map/cond/branch_1_fun/ppermute | solution.py:43
  355.0 22.4 %collective-permute-start.48 = (bf16[192,2048]{1,0:T(8,128)(2,1)}, bf16[192,2048]{1,0:T(8,128)(2,1)}, u32[]{:S(2)}, u32[]{:S(2)}) collective-permute-start(bf16[192,2048]{1,0:T(8,128)(2,1)} %get-tuple-element.290), channel_id=1, source_target_pairs={{0,4},{2,6},{4,0},{6,2},{1,5},{3,7},{5,1},{7,3},{8,12},{10,14},{12... | collective-permute-start | bytes 2359304 | tf_op jit(solution)/shard_map/cond/branch_1_fun/ppermute | solution.py:43
  356.2 21.2 %collective-permute-start.49 = (bf16[192,2048]{1,0:T(8,128)(2,1)}, bf16[192,2048]{1,0:T(8,128)(2,1)}, u32[]{:S(2)}, u32[]{:S(2)}) collective-permute-start(bf16[192,2048]{1,0:T(8,128)(2,1)} %get-tuple-element.291), channel_id=1, source_target_pairs={{0,1},{1,0},{2,3},{3,2},{4,5},{5,4},{6,7},{7,6},{8,9},{9,8},{10,11... | collective-permute-start | bytes 2359304 | tf_op jit(solution)/shard_map/cond/branch_1_fun/ppermute | solution.py:51
  383.1 9.3 %collective-permute-start.52 = (bf16[768,2048]{1,0:T(8,128)(2,1)S(1)}, bf16[768,2048]{1,0:T(8,128)(2,1)S(1)}, u32[]{:S(2)}, u32[]{:S(2)}) collective-permute-start(bf16[768,2048]{1,0:T(8,128)(2,1)S(1)} %convolution_convert_fusion.3), channel_id=1, source_target_pairs={{0,2},{2,0},{4,6},{6,4},{1,3},{3,1},{5,7},{7,5},{8,10},{10,8},{12,... | collective-permute-start | bytes 9437192 | tf_op jit(solution)/shard_map/cond/branch_1_fun/ppermute | solution.py:47
  384.3 54.4 %collective-permute-start.58 = (bf16[896,512]{1,0:T(8,128)(2,1)}, bf16[896,512]{1,0:T(8,128)(2,1)}, u32[]{:S(2)}, u32[]{:S(2)}) collective-permute-start(bf16[896,512]{1,0:T(8,128)(2,1)} %slice.249), channel_id=1, source_target_pairs={{0,4},{2,6},{4,0},{6,2},{1,5},{3,7},{5,1},{7,3},{8,12},{10,14},{12... | collective-permute-start | bytes 2752520 | tf_op jit(solution)/shard_map/cond/branch_1_fun/ppermute | solution.py:43
  394.5 29.5 %collective-permute-start.53 = (bf16[192,2048]{1,0:T(8,128)(2,1)S(1)}, bf16[192,2048]{1,0:T(8,128)(2,1)S(1)}, u32[]{:S(2)}, u32[]{:S(2)}) collective-permute-start(bf16[192,2048]{1,0:T(8,128)(2,1)S(1)} %bitcast.144), channel_id=1, source_target_pairs={{0,4},{2,6},{4,0},{6,2},{1,5},{3,7},{5,1},{7,3},{8,12},{10,14},{12... | collective-permute-start | bytes 2359304 | tf_op jit(solution)/shard_map/cond/branch_1_fun/ppermute | solution.py:43
  395.6 28.4 %collective-permute-start.54 = (bf16[192,2048]{1,0:T(8,128)(2,1)S(1)}, bf16[192,2048]{1,0:T(8,128)(2,1)S(1)}, u32[]{:S(2)}, u32[]{:S(2)}) collective-permute-start(bf16[192,2048]{1,0:T(8,128)(2,1)S(1)} %bitcast.145), channel_id=1, source_target_pairs={{0,1},{1,0},{2,3},{3,2},{4,5},{5,4},{6,7},{7,6},{8,9},{9,8},{10,11... | collective-permute-start | bytes 2359304 | tf_op jit(solution)/shard_map/cond/branch_1_fun/ppermute | solution.py:51
  406.5 10.0 %collective-permute-start.57 = (bf16[16,2048]{1,0:T(8,128)(2,1)S(1)}, bf16[16,2048]{1,0:T(8,128)(2,1)S(1)}, u32[]{:S(2)}, u32[]{:S(2)}) collective-permute-start(bf16[16,2048]{1,0:T(8,128)(2,1)S(1)} %fusion.31), channel_id=1, source_target_pairs={{0,1},{1,0},{2,3},{3,2},{4,5},{5,4},{6,7},{7,6},{8,9},{9,8},{10,11... | collective-permute-start | bytes 196616 | tf_op jit(solution)/shard_map/cond/branch_1_fun/ppermute | solution.py:51
  424.3 10.6 %collective-permute-start.55 = (bf16[96,2048]{1,0:T(8,128)(2,1)S(1)}, bf16[96,2048]{1,0:T(8,128)(2,1)S(1)}, u32[]{:S(2)}, u32[]{:S(2)}) collective-permute-start(bf16[96,2048]{1,0:T(8,128)(2,1)S(1)} %slice.303), channel_id=1, source_target_pairs={{0,1},{1,0},{2,3},{3,2},{4,5},{5,4},{6,7},{7,6},{8,9},{9,8},{10,11... | collective-permute-start | bytes 1179656 | tf_op jit(solution)/shard_map/cond/branch_1_fun/ppermute | solution.py:51
  425.3 10.5 %collective-permute-start.56 = (bf16[96,2048]{1,0:T(8,128)(2,1)S(1)}, bf16[96,2048]{1,0:T(8,128)(2,1)}, u32[]{:S(2)}, u32[]{:S(2)}) collective-permute-start(bf16[96,2048]{1,0:T(8,128)(2,1)S(1)} %slice.304), channel_id=1, source_target_pairs={{0,4},{2,6},{4,0},{6,2},{1,5},{3,7},{5,1},{7,3},{8,12},{10,14},{12... | collective-permute-start | bytes 1179656 | tf_op jit(solution)/shard_map/cond/branch_1_fun/ppermute | solution.py:43
  440.1 9.8 %collective-permute-start.1 = (bf16[96,2048]{1,0:T(8,128)(2,1)S(1)}, bf16[96,2048]{1,0:T(8,128)(2,1)S(1)}, u32[]{:S(2)}, u32[]{:S(2)}) collective-permute-start(bf16[96,2048]{1,0:T(8,128)(2,1)S(1)} %slice.253), channel_id=1, source_target_pairs={{0,4},{2,6},{4,0},{6,2},{1,5},{3,7},{5,1},{7,3},{8,12},{10,14},{12... | collective-permute-start | bytes 1179656 | tf_op jit(solution)/shard_map/cond/branch_1_fun/ppermute | solution.py:43
  442.1 9.5 %collective-permute-start = (bf16[96,2048]{1,0:T(8,128)(2,1)S(1)}, bf16[96,2048]{1,0:T(8,128)(2,1)S(1)}, u32[]{:S(2)}, u32[]{:S(2)}) collective-permute-start(bf16[96,2048]{1,0:T(8,128)(2,1)S(1)} %slice.251), channel_id=1, source_target_pairs={{0,1},{1,0},{2,3},{3,2},{4,5},{5,4},{6,7},{7,6},{8,9},{9,8},{10,11... | collective-permute-start | bytes 1179656 | tf_op jit(solution)/shard_map/cond/branch_1_fun/ppermute | solution.py:51
  443.7 27.2 %collective-permute-start.2 = (bf16[1344,512]{1,0:T(8,128)(2,1)}, bf16[1344,512]{1,0:T(8,128)(2,1)}, u32[]{:S(2)}, u32[]{:S(2)}) collective-permute-start(bf16[1344,512]{1,0:T(8,128)(2,1)} %get-tuple-element.322.refs_0_), channel_id=1, source_target_pairs={{0,2},{2,0},{4,6},{6,4},{1,3},{3,1},{5,7},{7,5},{8,10},{10,8},{12,... | collective-permute-start | bytes 4128776 | tf_op jit(solution)/shard_map/cond/branch_1_fun/ppermute | solution.py:47
  443.7 27.2 %collective-permute-start.3 = (bf16[896,512]{1,0:T(8,128)(2,1)}, bf16[896,512]{1,0:T(8,128)(2,1)}, u32[]{:S(2)}, u32[]{:S(2)}) collective-permute-start(bf16[896,512]{1,0:T(8,128)(2,1)} %get-tuple-element.323.refs_2_), channel_id=1, source_target_pairs={{0,2},{2,0},{4,6},{6,4},{1,3},{3,1},{5,7},{7,5},{8,10},{10,8},{12,... | collective-permute-start | bytes 2752520 | tf_op jit(solution)/shard_map/cond/branch_1_fun/ppermute | solution.py:47
  444.2 26.2 %collective-permute-start.4 = (bf16[768,512]{1,0:T(8,128)(2,1)}, bf16[768,512]{1,0:T(8,128)(2,1)}, u32[]{:S(2)}, u32[]{:S(2)}) collective-permute-start(bf16[768,512]{1,0:T(8,128)(2,1)} %get-tuple-element.324.refs_4_), channel_id=1, source_target_pairs={{0,2},{2,0},{4,6},{6,4},{1,3},{3,1},{5,7},{7,5},{8,10},{10,8},{12,... | collective-permute-start | bytes 2359304 | tf_op jit(solution)/shard_map/cond/branch_1_fun/ppermute | solution.py:47
  457.6 9.5 %collective-permute-start.5 = (bf16[256,512]{1,0:T(8,128)(2,1)}, bf16[256,512]{1,0:T(8,128)(2,1)S(1)}, u32[]{:S(2)}, u32[]{:S(2)}) collective-permute-start(bf16[256,512]{1,0:T(8,128)(2,1)} %hold.4), channel_id=1, source_target_pairs={{0,4},{2,6},{4,0},{6,2},{1,5},{3,7},{5,1},{7,3},{8,12},{10,14},{12... | collective-permute-start | bytes 786440 | tf_op jit(solution)/shard_map/cond/branch_1_fun/ppermute | solution.py:43
  461.7 24.8 %collective-permute-start.7 = (bf16[960,512]{1,0:T(8,128)(2,1)}, bf16[960,512]{1,0:T(8,128)(2,1)}, u32[]{:S(2)}, u32[]{:S(2)}) collective-permute-start(bf16[960,512]{1,0:T(8,128)(2,1)} %hold.5), channel_id=1, source_target_pairs={{0,4},{2,6},{4,0},{6,2},{1,5},{3,7},{5,1},{7,3},{8,12},{10,14},{12... | collective-permute-start | bytes 2949128 | tf_op jit(solution)/shard_map/cond/branch_1_fun/ppermute | solution.py:43
  470.4 20.1 %collective-permute-start.9 = (bf16[192,2048]{1,0:T(8,128)(2,1)}, bf16[192,2048]{1,0:T(8,128)(2,1)S(1)}, u32[]{:S(2)}, u32[]{:S(2)}) collective-permute-start(bf16[192,2048]{1,0:T(8,128)(2,1)} %add_convert_fusion.20), channel_id=1, source_target_pairs={{0,1},{1,0},{2,3},{3,2},{4,5},{5,4},{6,7},{7,6},{8,9},{9,8},{10,11... | collective-permute-start | bytes 2359304 | tf_op jit(solution)/shard_map/cond/branch_1_fun/ppermute | solution.py:51
  493.7 17.0 %collective-permute-start.11 = (bf16[656,512]{1,0:T(8,128)(2,1)}, bf16[656,512]{1,0:T(8,128)(2,1)S(1)}, u32[]{:S(2)}, u32[]{:S(2)}) collective-permute-start(bf16[656,512]{1,0:T(8,128)(2,1)} %get-tuple-element.339.r0), channel_id=1, source_target_pairs={{0,4},{2,6},{4,0},{6,2},{1,5},{3,7},{5,1},{7,3},{8,12},{10,14},{12... | collective-permute-start | bytes 2015240 | tf_op jit(solution)/shard_map/cond/branch_1_fun/ppermute | solution.py:43
  494.8 19.1 %collective-permute-start.13 = (bf16[192,2048]{1,0:T(8,128)(2,1)}, bf16[192,2048]{1,0:T(8,128)(2,1)S(1)}, u32[]{:S(2)}, u32[]{:S(2)}) collective-permute-start(bf16[192,2048]{1,0:T(8,128)(2,1)} %get-tuple-element.346), channel_id=1, source_target_pairs={{0,1},{1,0},{2,3},{3,2},{4,5},{5,4},{6,7},{7,6},{8,9},{9,8},{10,11... | collective-permute-start | bytes 2359304 | tf_op jit(solution)/shard_map/cond/branch_1_fun/ppermute | solution.py:51
  495.7 21.7 %collective-permute-start.10 = (bf16[656,512]{1,0:T(8,128)(2,1)}, bf16[656,512]{1,0:T(8,128)(2,1)}, u32[]{:S(2)}, u32[]{:S(2)}) collective-permute-start(bf16[656,512]{1,0:T(8,128)(2,1)} %get-tuple-element.339.r0), channel_id=1, source_target_pairs={{0,2},{2,0},{4,6},{6,4},{1,3},{3,1},{5,7},{7,5},{8,10},{10,8},{12,... | collective-permute-start | bytes 2015240 | tf_op jit(solution)/shard_map/cond/branch_1_fun/ppermute | solution.py:47
  (85 other events, 493.9 us)
Sparse Core Ops, SparseCore 0:
  10.8 58.5 all-gather.5
  71.5 101.1 all-gather.3
  174.3 61.7 all-gather.7
  238.9 96.6 reduce-scatter.3
  337.8 60.7 reduce-scatter.5
  439.0 52.8 reduce-scatter.7

commit v3 on v2

--- a/solution.py
+++ b/solution.py
@@ -284,15 +284,17 @@
         to_order(starts_ref, *got, k_n, block)
 
 
-def over_queries(heads, seq, slot, step, visit):
-    per = slot // step
-    for first in range(0, seq, slot):
-
-        def one(i, carry):
-            visit(i // per, pl.multiple_of(first + lax.rem(i, per) * step, step), first + slot)
-            return carry
-
-        lax.fori_loop(0, heads * per, one, 0)
+def over_queries(heads, seq, slot, step, visit, unrolled):
+    def one(h, carry):
+        for row in range(0, seq, step):
+            visit(h, row, (row // slot + 1) * slot)
+        return carry
+
+    if unrolled:
+        for h in range(heads):
+            one(h, 0)
+    else:
+        lax.fori_loop(0, heads, one, 0)
 
 
 def attn_forward_kernel(
@@ -318,7 +320,7 @@
         o_n[h, rows, :] = out.T.astype(BF16)
         lse_ref[h, :, rows] = top + jnp.log(total)
 
-    over_queries(heads, seq, slot, step, visit)
+    over_queries(heads, seq, slot, step, visit, False)
     per = om.shape[0] // block
     for a in range(2 * per):
         dest = om if a < per else oo
@@ -385,7 +387,7 @@
         dk_n[:nk, :] += dot(d_s, q, 1, 0)
         dq_n[h, rows, :] = dot(kt_n[:, :nk], d_s, 1, 0).T
 
-    over_queries(heads, seq, slot, step, visit)
+    over_queries(heads, seq, slot, step, visit, True)
     per = dqm.shape[0] // block
     scale = 1.0 / math.sqrt(HEAD)
     first = starts_ref[16] == 0
@@ -646,7 +648,7 @@
     core = (c & 1).astype(jnp.int32)
     q_cols = w_query.shape[1] // 4
     ff = w_gate.shape[1] // 4
-    part_a = (ff * 5 // 8 + 15) // 16 * 16
+    part_a = (ff * 3 // 4 + 15) // 16 * 16
     part_b = ff - part_a
 
     flag = seq_ids[0, 0] >= 0

time: 544 us -> 540 us (level)
    cond x122 -> x112, local copies, waits for them, and re-layouts: 11.4 us -> 10.6 us
  transfers between devices with their start and end apart: 72 -> 72, of which waited for: 36 -> 35; matrix products, arithmetic and copies ran while one was open for 29% -> 30% of each run, Pallas kernels for 27% -> 27%
where the time goes in v3:
time: 540 us; the launch traced here: 530 us
  Pallas kernels  150 us (28%)
  waiting for transfers between devices  135 us (25%)
  other arithmetic  70.8 us (13%)
  starting transfers between devices  55.6 us (10%)
  matrix products  50.9 us (9%)
  local copies, waits for them, and re-layouts  50.2 us (9%)
  between operations  15.2 us (3%)
    ppermute x24, waiting for transfers between devices, far(): return lax.ppermute(v, 'ctx', [(i, i ^ 2) for i in range(4)])  75.8 us
    dot_general x18, matrix products, dot(): lax.dot_general(a, b, (((ca,), (cb,)), ((), ())), preferred_element_type=...  50.9 us
    ppermute x23, waiting for transfers between devices, side(): return lax.ppermute(v, 'tp', [(0, 1), (1, 0)])  37.1 us
    pallas_call x4, Pallas kernels, hidden_half(): pl.pallas_call(functools.partial(hidden_kernel, ff), out_shape=jax.ShapeD...  33.3 us
    ppermute x23, starting transfers between devices, side(): return lax.ppermute(v, 'tp', [(0, 1), (1, 0)])  26.9 us
    ppermute x24, starting transfers between devices, far(): return lax.ppermute(v, 'ctx', [(i, i ^ 2) for i in range(4)])  26.6 us
    pallas_call x2, Pallas kernels, feed_grads(): pl.pallas_call(functools.partial(grads_kernel, rows // 3), out_shape=jax....  26 us
    pallas_call x3, Pallas kernels, finish(): pl.pallas_call(functools.partial(finish_kernel, (turned, firsts), sizes),...  19.6 us
  transfers between devices with their start and end apart: 72, of which 35 were waited for; matrix products, arithmetic and copies ran while one was open for 30% of the time, Pallas kernels for 27%

profile of v3, /device:TPU:0, one launch (start us, length us, event | category | flops | bytes accessed | tf_op | source)
XLA Modules:
  0.0 530.3 jit_solution(6126807008662178453)
XLA Ops:
  7.9 2.8 pack_first.1
  12.0 53.0 %conditional.6 = (f32[192,2048]{1,0:T(8,128)S(1)}, f32[192,1]{0,1:T(1,128)S(1)}, f32[192,2048]{1,0:T(8,128)}, bf16[192,2048]{1,0:T(8,128)(2,1)}, bf16[768,2048]{...) conditional(s32[]{:T(128)} %bitcast.69, () %tuple.79, ...), branch_computations={%region_0.0_spmd, %region_1.5_spmd} | conditional | flops 17967146 | bytes 63024752 | solution.py:34
  14.1 2.9 collective-permute-start.59
  19.1 3.2 copy.84
  28.9 4.4 fusion.32
  36.5 3.0 concatenate.57
  39.7 3.1 pad_maximum_fusion.8
  47.9 5.2 collective-permute-done.63.refs_3_
  55.3 3.6 join.4
  60.3 4.6 collective-permute-done.65
  69.5 127.4 %conditional.7 = (bf16[768,2048]{1,0:T(8,128)(2,1)}, bf16[768,2048]{1,0:T(8,128)(2,1)}, bf16[768,256]{1,0:T(8,128)(2,1)}, bf16[768,256]{1,0:T(8,128)(2,1)}, bf16...) conditional(s32[]{:T(128)} %bitcast.69, () %tuple.83, ...), branch_computations={%region_5.6_spmd, %region_6.8_spmd} | conditional | flops 11291199488 | bytes 187464880 | solution.py:34
  79.0 5.8 %qkv.3 = (bf16[768,2048]{1,0:T(8,128)(2,1)}, bf16[768,256]{1,0:T(8,128)(2,1)}, bf16[768,128]{1,0:T(8,128)(2,1)}) custom-call(s32[1]{0:T(128)} %get-tuple-element.210.core_ref, bf16[768,2048]{1,0:T(8,128)(2,1)} %get-tuple-element.216.x_ref, bf16[656,2048]{1,0:T(8,128)(2,1)S(1)} %copy-done.1, bf16[656,2048]{1,0:T(8,128)(2,1)S(1)} %copy-done.1, ...), custom_call_target="tpu_custom_call" | custom-call | flops 1207959552 | bytes 7864320 | tf_op jit(solution)/shard_map/cond/branch_1_fun/qkv/pallas_call | solution.py:237
  84.9 5.5 %qkv.2 = (bf16[768,2048]{1,0:T(8,128)(2,1)}, bf16[768,256]{1,0:T(8,128)(2,1)}, bf16[768,128]{1,0:T(8,128)(2,1)}) custom-call(s32[1]{0:T(128)} %get-tuple-element.210.core_ref, bf16[768,2048]{1,0:T(8,128)(2,1)} %get-tuple-element.211.x_ref, bf16[656,2048]{1,0:T(8,128)(2,1)S(1)} %copy-done.1, bf16[656,2048]{1,0:T(8,128)(2,1)S(1)} %copy-done.1, ...), custom_call_target="tpu_custom_call" | custom-call | flops 1207959552 | bytes 7864320 | tf_op jit(solution)/shard_map/cond/branch_1_fun/qkv/pallas_call | solution.py:237
  94.7 13.8 %attn_forward.1 = (bf16[768,256]{1,0:T(8,128)(2,1)S(1)}, bf16[768,256]{1,0:T(8,128)(2,1)S(1)}, f32[2,1,1536]{2,1,0:T(1,128)S(1)}) custom-call(s32[17]{0:T(128)S(1)} %get-tuple-element.225.starts_ref, bf16[768,256]{1,0:T(8,128)(2,1)} %get-tuple-element.694.qm, bf16[768,256]{1,0:T(8,128)(2,1)} %get-tuple-element.695.qo, ...), custom_call_target="tpu_custom_call" | custom-call | flops 7247757312 | bytes 3145728 | tf_op jit(solution)/shard_map/cond/branch_1_fun/attn_forward/pallas_call | solution.py:338
  110.7 4.6 collective-permute-done.22
  122.0 3.7 join.5
  125.7 13.8 %collective-permute-done.24 = bf16[192,2048]{1,0:T(8,128)(2,1)} collective-permute-done((bf16[192,2048]{1,0:T(8,128)(2,1)}, bf16[192,2048]{1,0:T(8,128)(2,1)}, u32[]{:S(2)}, u32[]{:S(2)}) %collective-permute-start.24) | collective-permute-done | bytes 786464 | tf_op jit(solution)/shard_map/cond/branch_1_fun/ppermute | solution.py:43
  145.2 6.9 %collective-permute-done.27 = bf16[96,2048]{1,0:T(8,128)(2,1)S(1)} collective-permute-done((bf16[96,2048]{1,0:T(8,128)(2,1)S(1)}, bf16[96,2048]{1,0:T(8,128)(2,1)S(1)}, u32[]{:S(2)}, u32[]{:S(2)}) %collective-permute-start.27) | collective-permute-done | bytes 393248 | tf_op jit(solution)/shard_map/cond/branch_1_fun/ppermute | solution.py:43
  162.6 8.0 %collective-permute-done.28.refs_1_ = bf16[96,2048]{1,0:T(8,128)(2,1)S(1)} collective-permute-done((bf16[96,2048]{1,0:T(8,128)(2,1)S(1)}, bf16[96,2048]{1,0:T(8,128)(2,1)S(1)}, u32[]{:S(2)}, u32[]{:S(2)}) %collective-permute-start.28) | collective-permute-done | bytes 393248 | tf_op jit(solution)/shard_map/cond/branch_1_fun/ppermute | solution.py:43
  173.0 7.5 %collective-permute-done.29.refs_2_ = bf16[96,2048]{1,0:T(8,128)(2,1)S(1)} collective-permute-done((bf16[96,2048]{1,0:T(8,128)(2,1)S(1)}, bf16[96,2048]{1,0:T(8,128)(2,1)S(1)}, u32[]{:S(2)}, u32[]{:S(2)}) %collective-permute-start.29) | collective-permute-done | bytes 393248 | tf_op jit(solution)/shard_map/cond/branch_1_fun/ppermute | solution.py:51
  180.4 5.0 collective-permute-done.30.refs_3_
  186.9 3.5 join.6
  190.6 6.0 %collective-permute-done.34 = bf16[768,2048]{1,0:T(8,128)(2,1)} collective-permute-done((bf16[768,2048]{1,0:T(8,128)(2,1)}, bf16[768,2048]{1,0:T(8,128)(2,1)}, u32[]{:S(2)}, u32[]{:S(2)}) %collective-permute-start.34) | collective-permute-done | bytes 3145760 | tf_op jit(solution)/shard_map/cond/branch_1_fun/ppermute | solution.py:47
  197.0 9.6 %hidden.4.lm_ref = bf16[1584,768]{1,0:T(8,128)(2,1)S(1)} custom-call(bf16[1584,2048]{1,0:T(8,128)(2,1)} %all-gather.4.cloned.1.call-done.w_ref, bf16[768,2048]{1,0:T(8,128)(2,1)} %get-tuple-element.456.n2_ref.nm_ref, bf16[768,2048]{1,0:T(8,128)(2,1)} %get-tuple-element.457.df_ref.dm_ref), custom_call_target="tpu_custom_call" | custom-call | flops 4982833152 | bytes 6488064 | tf_op jit(solution)/shard_map/hidden/pallas_call | solution.py:453
  206.6 11.3 %hidden.5.lo_ref = bf16[1584,768]{1,0:T(8,128)(2,1)} custom-call(bf16[1584,2048]{1,0:T(8,128)(2,1)} %all-gather.4.cloned.1.call-done.w_ref, bf16[768,2048]{1,0:T(8,128)(2,1)} %get-tuple-element.458.n2_ref.no_ref, bf16[768,2048]{1,0:T(8,128)(2,1)} %get-tuple-element.459.df_ref.do_ref), custom_call_target="tpu_custom_call" | custom-call | flops 4982833152 | bytes 6488064 | tf_op jit(solution)/shard_map/hidden/pallas_call | solution.py:453
  217.9 15.7 %feed_grads.2 = bf16[1584,2048]{1,0:T(8,128)(2,1)} custom-call(bf16[1584,768]{1,0:T(8,128)(2,1)S(1)} %hidden.4.lm_ref, bf16[1584,768]{1,0:T(8,128)(2,1)} %hidden.5.lo_ref, bf16[768,2048]{1,0:T(8,128)(2,1)} %get-tuple-element.456.n2_ref.nm_ref, bf16[768,2048]{1,0:T(8,128)(2,1)} %get-tuple-element.458.n2_ref.no_ref, ...), custom_call_target="tpu_custom_call" | custom-call | flops 9965666304 | bytes 6488064 | tf_op jit(solution)/shard_map/feed_grads/pallas_call | solution.py:485
  236.0 6.0 %hidden.6.lm_ref = bf16[528,768]{1,0:T(8,128)(2,1)S(1)} custom-call(bf16[528,2048]{1,0:T(8,128)(2,1)} %all-gather.8.cloned.1.call-done.w_ref, bf16[768,2048]{1,0:T(8,128)(2,1)} %get-tuple-element.456.n2_ref.nm_ref, bf16[768,2048]{1,0:T(8,128)(2,1)} %get-tuple-element.457.df_ref.dm_ref), custom_call_target="tpu_custom_call" | custom-call | flops 1660944384 | bytes 2162688 | tf_op jit(solution)/shard_map/hidden/pallas_call | solution.py:453
  242.0 6.3 %hidden.7.lo_ref = bf16[528,768]{1,0:T(8,128)(2,1)} custom-call(bf16[528,2048]{1,0:T(8,128)(2,1)S(1)} %copy-done.10, bf16[768,2048]{1,0:T(8,128)(2,1)} %get-tuple-element.458.n2_ref.no_ref, bf16[768,2048]{1,0:T(8,128)(2,1)} %get-tuple-element.459.df_ref.do_ref), custom_call_target="tpu_custom_call" | custom-call | flops 1660944384 | bytes 2162688 | tf_op jit(solution)/shard_map/hidden/pallas_call | solution.py:453
  248.3 10.3 %feed_grads.3 = bf16[528,2048]{1,0:T(8,128)(2,1)} custom-call(bf16[528,768]{1,0:T(8,128)(2,1)S(1)} %hidden.6.lm_ref, bf16[528,768]{1,0:T(8,128)(2,1)} %hidden.7.lo_ref, bf16[768,2048]{1,0:T(8,128)(2,1)} %get-tuple-element.456.n2_ref.nm_ref, bf16[768,2048]{1,0:T(8,128)(2,1)} %get-tuple-element.458.n2_ref.no_ref, ...), custom_call_target="tpu_custom_call" | custom-call | flops 3321888768 | bytes 2162688 | tf_op jit(solution)/shard_map/feed_grads/pallas_call | solution.py:485
  258.8 7.1 %fusion.37 = bf16[768,2048]{1,0:T(8,128)(2,1)S(1)} fusion(bf16[1584,2048]{1,0:T(8,128)(2,1)} %all-gather.4.cloned.1.call-done.w_ref, bf16[1584,768]{1,0:T(8,128)(2,1)} %hidden.5.lo_ref), kind=kOutput, calls=%fused_computation.130 | convolution fusion | flops 3323461632 | bytes 9093120 | tf_op jit(solution)/shard_map/dot_general | solution.py:21
  266.0 84.8 %conditional.8 = (f32[192,2048]{1,0:T(8,128)}, f32[1,2048]{1,0:T(1,128)S(1)}, bf16[768,2048]{1,0:T(8,128)(2,1)}, bf16[768,2048]{1,0:T(8,128)(2,1)}, bf16[192,204...) conditional(s32[]{:T(128)} %bitcast.69, () %tuple.87, ...), branch_computations={%region_8.9_spmd, %region_9.12_spmd} | conditional | flops 10807738368 | bytes 236381472 | solution.py:34
  269.0 4.3 fusion.3
  280.0 3.8 fusion.7
  288.9 7.4 %collective-permute-done.36 = bf16[192,2048]{1,0:T(8,128)(2,1)S(1)} collective-permute-done((bf16[192,2048]{1,0:T(8,128)(2,1)S(1)}, bf16[192,2048]{1,0:T(8,128)(2,1)S(1)}, u32[]{:S(2)}, u32[]{:S(2)}) %collective-permute-start.36) | collective-permute-done | bytes 786464 | tf_op jit(solution)/shard_map/cond/branch_1_fun/ppermute | solution.py:43
  300.1 7.1 %collective-permute-done.39 = bf16[96,2048]{1,0:T(8,128)(2,1)S(1)} collective-permute-done((bf16[96,2048]{1,0:T(8,128)(2,1)S(1)}, bf16[96,2048]{1,0:T(8,128)(2,1)S(1)}, u32[]{:S(2)}, u32[]{:S(2)}) %collective-permute-start.39) | collective-permute-done | bytes 393248 | tf_op jit(solution)/shard_map/cond/branch_1_fun/ppermute | solution.py:43
  309.9 3.5 multiply_convert_fusion.1
  317.6 8.0 %collective-permute-done.40.refs_1_ = bf16[96,2048]{1,0:T(8,128)(2,1)S(1)} collective-permute-done((bf16[96,2048]{1,0:T(8,128)(2,1)S(1)}, bf16[96,2048]{1,0:T(8,128)(2,1)S(1)}, u32[]{:S(2)}, u32[]{:S(2)}) %collective-permute-start.40) | collective-permute-done | bytes 393248 | tf_op jit(solution)/shard_map/cond/branch_1_fun/ppermute | solution.py:43
  335.3 4.5 collective-permute-done.42.refs_3_
  340.7 3.6 join.7
  344.5 3.7 convolution_convert_fusion.2
  350.9 86.7 %conditional.9 = (f32[192,2048]{1,0:T(8,128)}, bf16[656,2048]{1,0:T(8,128)(2,1)}, bf16[192,2048]{1,0:T(8,128)(2,1)}, bf16[192,2048]{1,0:T(8,128)(2,1)}, bf16[1056,512]{1,0:T(8,128)(2,1)}) conditional(s32[]{:T(128)} %bitcast.69, () %tuple.86, (bf16[656,2048]{1,0:T(8,128)(2,1)S(1)}, bf16[768,2048]{1,0:T(8,128)(2,1)}, s32[17]{0:T(128)S(1)}, ...), branch_computations={%region_13.0_spmd, %region_14.19_spmd} | conditional | flops 21800714240 | bytes 174490656 | solution.py:34
  353.8 3.7 convolution_convert_fusion.5.doo
  357.5 13.7 %attn_backward.1 = (bf16[768,256]{1,0:T(8,128)(2,1)}, bf16[768,256]{1,0:T(8,128)(2,1)}, f32[768,128]{1,0:T(8,128)}, f32[768,128]{1,0:T(8,128)}, bf16[768,128]{1,0:T(8,128)(2,1)}, /*index=5*/bf16[768,128]{1,0:T(8,128)(2,1)}) custom-call(s32[17]{0:T(128)S(1)} %get-tuple-element.267.starts_ref, bf16[768,256]{1,0:T(8,128)(2,1)} %get-tuple-element.268.qm, ...), custom_call_target="tpu_custom_call" | custom-call | flops 14495514624 | bytes 6291456 | tf_op jit(solution)/shard_map/cond/branch_1_fun/attn_backward/pallas_call | solution.py:415
  374.4 2.9 convolution_convert_fusion.3
  391.8 4.2 fusion.21
  396.0 3.0 fusion.23
  399.0 3.0 fusion.26
  402.8 3.3 fusion.60
  406.1 3.4 add_convert_fusion.12
  411.4 10.5 %collective-permute-done.53 = bf16[192,2048]{1,0:T(8,128)(2,1)S(1)} collective-permute-done((bf16[192,2048]{1,0:T(8,128)(2,1)S(1)}, bf16[192,2048]{1,0:T(8,128)(2,1)S(1)}, u32[]{:S(2)}, u32[]{:S(2)}) %collective-permute-start.53) | collective-permute-done | bytes 786464 | tf_op jit(solution)/shard_map/cond/branch_1_fun/ppermute | solution.py:43
  425.0 2.9 fusion.61
  427.9 2.9 fusion.27.rest_0_
  434.5 2.9 add_last.1
  437.6 52.6 %conditional.10 = (bf16[192,2048]{1,0:T(8,128)(2,1)}, f32[512,2816]{1,0:T(8,128)}, bf16[1584,512]{1,0:T(8,128)(2,1)}, bf16[1056,512]{1,0:T(8,128)(2,1)}, bf16[52...) conditional(s32[]{:T(128)} %bitcast.69, () %tuple.85, ...), branch_computations={%region_21.22_spmd, %region_22.25_spmd} | conditional | flops 16746689 | bytes 76061856 | solution.py:34
  451.0 3.0 pad_maximum_fusion.6
  460.0 3.4 collective-permute-done.5.refs_6_
  463.4 3.3 add_convert_fusion.20
  468.7 6.9 %finish.3.rest_0_ = f32[512,2816]{1,0:T(8,128)} custom-call(s32[1]{0:T(128)} %get-tuple-element.321.c_ref, bf16[1584,512]{1,0:T(8,128)(2,1)S(1)} %copy-done.8, bf16[1584,512]{1,0:T(8,128)(2,1)} %collective-permute-done.2.refs_1_, bf16[1056,512]{1,0:T(8,128)(2,1)} %get-tuple-element.323.refs_2_, bf16[1056,512]{1,0:T(8,128)(2,1)} %collective-permute-done.3.refs_3_, ...), custom_call_target="tpu_custom_call" | custom-call | tf_op jit(solution)/shard_map/cond/branch_1_fun/finish/pallas_call | solution.py:567
  475.5 6.7 %collective-permute-done.7.v_ref = bf16[880,512]{1,0:T(8,128)(2,1)} collective-permute-done((bf16[880,512]{1,0:T(8,128)(2,1)}, bf16[880,512]{1,0:T(8,128)(2,1)}, u32[]{:S(2)}, u32[]{:S(2)}) %collective-permute-start.7) | collective-permute-done | bytes 901152 | tf_op jit(solution)/shard_map/cond/branch_1_fun/ppermute | solution.py:43
  486.9 3.3 maximum_select_fusion
  490.2 31.9 %conditional.11 = (f32[512,2816]{1,0:T(8,128)}, f32[2816,512]{1,0:T(8,128)}, f32[512,1024]{1,0:T(8,128)}, f32[512,256]{1,0:T(8,128)}, f32[512,256]{1,0:T(8,128)}...) conditional(s32[]{:T(128)} %bitcast.69, () %tuple.78, ...), branch_computations={%region_25.26_spmd, %region_26.27_spmd} | conditional | flops 7077889 | bytes 32063892 | solution.py:34
  492.8 5.8 %finish.5.rest_1_ = f32[2816,512]{1,0:T(8,128)} custom-call(s32[1]{0:T(128)} %get-tuple-element.330.c_ref, bf16[1584,512]{1,0:T(8,128)(2,1)} %get-tuple-element.331.refs_0_, bf16[1584,512]{1,0:T(8,128)(2,1)} %get-tuple-element.332.refs_1_, bf16[880,512]{1,0:T(8,128)(2,1)} %get-tuple-element.337.refs_6_.refs_2_, ...), custom_call_target="tpu_custom_call" | custom-call | tf_op jit(solution)/shard_map/cond/branch_1_fun/finish/pallas_call | solution.py:567
  498.6 6.9 %finish.4.rest_0_ = f32[512,2816]{1,0:T(8,128)} custom-call(s32[1]{0:T(128)} %get-tuple-element.330.c_ref, bf16[1584,512]{1,0:T(8,128)(2,1)S(1)} %copy-done.9, bf16[1584,512]{1,0:T(8,128)(2,1)} %get-tuple-element.332.refs_1_, bf16[1056,512]{1,0:T(8,128)(2,1)} %get-tuple-element.333.refs_2_, bf16[1056,512]{1,0:T(8,128)(2,1)} %get-tuple-element.334.refs_3_, ...), custom_call_target="tpu_custom_call" | custom-call | tf_op jit(solution)/shard_map/cond/branch_1_fun/finish/pallas_call | solution.py:567
  514.8 4.5 finish_attn.1
  (387 shorter events, 182.8 us)
Async XLA Ops:
  7.2 62.3 %all-gather.6.cloned.1.call-start = ((), (), s32[]{:S(2)}) async-start(), calls=%async_computation.4 | async-start | bytes 3358720 | tf_op jit(solution)/shard_map/all_gather | solution.py:166
  10.7 186.2 %all-gather.4.cloned.1.call-start = ((), (), s32[]{:S(2)}) async-start(), calls=%async_computation.3 | async-start | bytes 8110080 | tf_op jit(solution)/shard_map/all_gather | solution.py:166
  14.1 28.7 %collective-permute-start.59 = (bf16[96,2048]{1,0:T(8,128)(2,1)}, bf16[96,2048]{1,0:T(8,128)(2,1)}, u32[]{:S(2)}, u32[]{:S(2)}) collective-permute-start(bf16[96,2048]{1,0:T(8,128)(2,1)} %get-tuple-element.202.refs_0_), channel_id=1, source_target_pairs={{0,4},{2,6},{4,0},{6,2},{1,5},{3,7},{5,1},{7,3},{8,12},{10,14},{12... | collective-permute-start | bytes 1179656 | tf_op jit(solution)/shard_map/cond/branch_1_fun/ppermute | solution.py:43
  17.0 25.8 %collective-permute-start.61 = (bf16[96,2048]{1,0:T(8,128)(2,1)}, bf16[96,2048]{1,0:T(8,128)(2,1)}, u32[]{:S(2)}, u32[]{:S(2)}) collective-permute-start(bf16[96,2048]{1,0:T(8,128)(2,1)} %get-tuple-element.202.refs_0_), channel_id=1, source_target_pairs={{0,1},{1,0},{2,3},{3,2},{4,5},{5,4},{6,7},{7,6},{8,9},{9,8},{10,11... | collective-permute-start | bytes 1179656 | tf_op jit(solution)/shard_map/cond/branch_1_fun/ppermute | solution.py:51
  18.5 24.3 %collective-permute-start.60 = (bf16[96,2048]{1,0:T(8,128)(2,1)}, bf16[96,2048]{1,0:T(8,128)(2,1)}, u32[]{:S(2)}, u32[]{:S(2)}) collective-permute-start(bf16[96,2048]{1,0:T(8,128)(2,1)} %get-tuple-element.206.refs_4_), channel_id=1, source_target_pairs={{0,1},{1,0},{2,3},{3,2},{4,5},{5,4},{6,7},{7,6},{8,9},{9,8},{10,11... | collective-permute-start | bytes 1179656 | tf_op jit(solution)/shard_map/cond/branch_1_fun/ppermute | solution.py:51
  19.0 23.8 %collective-permute-start.62 = (bf16[96,2048]{1,0:T(8,128)(2,1)}, bf16[96,2048]{1,0:T(8,128)(2,1)}, u32[]{:S(2)}, u32[]{:S(2)}) collective-permute-start(bf16[96,2048]{1,0:T(8,128)(2,1)} %get-tuple-element.206.refs_4_), channel_id=1, source_target_pairs={{0,4},{2,6},{4,0},{6,2},{1,5},{3,7},{5,1},{7,3},{8,12},{10,14},{12... | collective-permute-start | bytes 1179656 | tf_op jit(solution)/shard_map/cond/branch_1_fun/ppermute | solution.py:43
  42.8 10.3 %collective-permute-start.63 = (bf16[96,2048]{1,0:T(8,128)(2,1)}, bf16[96,2048]{1,0:T(8,128)(2,1)S(1)}, u32[]{:S(2)}, u32[]{:S(2)}) collective-permute-start(bf16[96,2048]{1,0:T(8,128)(2,1)} %collective-permute-done.59.refs_1_), channel_id=1, source_target_pairs={{0,1},{1,0},{2,3},{3,2},{4,5},{5,4},{6,7},{7,6},{8,9},{9,8},{10,11... | collective-permute-start | bytes 1179656 | tf_op jit(solution)/shard_map/cond/branch_1_fun/ppermute | solution.py:51
  44.9 9.7 %collective-permute-start.64 = (bf16[96,2048]{1,0:T(8,128)(2,1)}, bf16[96,2048]{1,0:T(8,128)(2,1)S(1)}, u32[]{:S(2)}, u32[]{:S(2)}) collective-permute-start(bf16[96,2048]{1,0:T(8,128)(2,1)} %collective-permute-done.60.refs_5_), channel_id=1, source_target_pairs={{0,4},{2,6},{4,0},{6,2},{1,5},{3,7},{5,1},{7,3},{8,12},{10,14},{12... | collective-permute-start | bytes 1179656 | tf_op jit(solution)/shard_map/cond/branch_1_fun/ppermute | solution.py:43
  67.3 168.7 %all-gather.8.cloned.1.call-start = ((), (), s32[]{:S(2)}) async-start(), calls=%async_computation.6 | async-start | bytes 2703360 | tf_op jit(solution)/shard_map/all_gather | solution.py:166
  69.4 281.4 %reduce-scatter.4.cloned.1.call-start = ((), (), s32[]{:S(2)}) async-start(), calls=%async_computation.5 | async-start | bytes 8110080 | tf_op jit(solution)/shard_map/reduce_scatter | solution.py:170
  72.2 18.2 %collective-permute-start.14 = (bf16[96,2048]{1,0:T(8,128)(2,1)S(1)}, bf16[96,2048]{1,0:T(8,128)(2,1)}, u32[]{:S(2)}, u32[]{:S(2)}) collective-permute-start(bf16[96,2048]{1,0:T(8,128)(2,1)S(1)} %get-tuple-element.233.refs_0_), channel_id=1, source_target_pairs={{0,4},{2,6},{4,0},{6,2},{1,5},{3,7},{5,1},{7,3},{8,12},{10,14},{12... | collective-permute-start | bytes 1179656 | tf_op jit(solution)/shard_map/cond/branch_1_fun/ppermute | solution.py:43
  73.7 19.4 %collective-permute-start.16 = (bf16[96,2048]{1,0:T(8,128)(2,1)S(1)}, bf16[96,2048]{1,0:T(8,128)(2,1)}, u32[]{:S(2)}, u32[]{:S(2)}) collective-permute-start(bf16[96,2048]{1,0:T(8,128)(2,1)S(1)} %get-tuple-element.233.refs_0_), channel_id=1, source_target_pairs={{0,1},{1,0},{2,3},{3,2},{4,5},{5,4},{6,7},{7,6},{8,9},{9,8},{10,11... | collective-permute-start | bytes 1179656 | tf_op jit(solution)/shard_map/cond/branch_1_fun/ppermute | solution.py:51
  75.1 18.0 %collective-permute-start.15 = (bf16[96,2048]{1,0:T(8,128)(2,1)S(1)}, bf16[96,2048]{1,0:T(8,128)(2,1)}, u32[]{:S(2)}, u32[]{:S(2)}) collective-permute-start(bf16[96,2048]{1,0:T(8,128)(2,1)S(1)} %get-tuple-element.237.refs_4_), channel_id=1, source_target_pairs={{0,1},{1,0},{2,3},{3,2},{4,5},{5,4},{6,7},{7,6},{8,9},{9,8},{10,11... | collective-permute-start | bytes 1179656 | tf_op jit(solution)/shard_map/cond/branch_1_fun/ppermute | solution.py:51
  75.7 17.4 %collective-permute-start.17 = (bf16[96,2048]{1,0:T(8,128)(2,1)S(1)}, bf16[96,2048]{1,0:T(8,128)(2,1)}, u32[]{:S(2)}, u32[]{:S(2)}) collective-permute-start(bf16[96,2048]{1,0:T(8,128)(2,1)S(1)} %get-tuple-element.237.refs_4_), channel_id=1, source_target_pairs={{0,4},{2,6},{4,0},{6,2},{1,5},{3,7},{5,1},{7,3},{8,12},{10,14},{12... | collective-permute-start | bytes 1179656 | tf_op jit(solution)/shard_map/cond/branch_1_fun/ppermute | solution.py:43
  84.8 9.9 %collective-permute-start.18 = (bf16[768,128]{1,0:T(8,128)(2,1)}, bf16[768,128]{1,0:T(8,128)(2,1)}, u32[]{:S(2)}, u32[]{:S(2)}) collective-permute-start(bf16[768,128]{1,0:T(8,128)(2,1)} %get-tuple-element.697.ko), channel_id=1, source_target_pairs={{0,2},{2,0},{4,6},{6,4},{1,3},{3,1},{5,7},{7,5},{8,10},{10,8},{12,... | collective-permute-start | bytes 589832 | tf_op jit(solution)/shard_map/cond/branch_1_fun/ppermute | solution.py:47
  93.1 15.5 %collective-permute-start.20 = (bf16[96,2048]{1,0:T(8,128)(2,1)}, bf16[96,2048]{1,0:T(8,128)(2,1)}, u32[]{:S(2)}, u32[]{:S(2)}) collective-permute-start(bf16[96,2048]{1,0:T(8,128)(2,1)} %collective-permute-done.14.refs_1_), channel_id=1, source_target_pairs={{0,1},{1,0},{2,3},{3,2},{4,5},{5,4},{6,7},{7,6},{8,9},{9,8},{10,11... | collective-permute-start | bytes 1179656 | tf_op jit(solution)/shard_map/cond/branch_1_fun/ppermute | solution.py:51
  94.2 14.4 %collective-permute-start.21 = (bf16[96,2048]{1,0:T(8,128)(2,1)}, bf16[96,2048]{1,0:T(8,128)(2,1)}, u32[]{:S(2)}, u32[]{:S(2)}) collective-permute-start(bf16[96,2048]{1,0:T(8,128)(2,1)} %collective-permute-done.15.refs_5_), channel_id=1, source_target_pairs={{0,4},{2,6},{4,0},{6,2},{1,5},{3,7},{5,1},{7,3},{8,12},{10,14},{12... | collective-permute-start | bytes 1179656 | tf_op jit(solution)/shard_map/cond/branch_1_fun/ppermute | solution.py:43
  119.6 19.9 %collective-permute-start.24 = (bf16[192,2048]{1,0:T(8,128)(2,1)}, bf16[192,2048]{1,0:T(8,128)(2,1)}, u32[]{:S(2)}, u32[]{:S(2)}) collective-permute-start(bf16[192,2048]{1,0:T(8,128)(2,1)} %bitcast.34), channel_id=1, source_target_pairs={{0,4},{2,6},{4,0},{6,2},{1,5},{3,7},{5,1},{7,3},{8,12},{10,14},{12... | collective-permute-start | bytes 2359304 | tf_op jit(solution)/shard_map/cond/branch_1_fun/ppermute | solution.py:43
  121.0 19.6 %collective-permute-start.25 = (bf16[192,2048]{1,0:T(8,128)(2,1)}, bf16[192,2048]{1,0:T(8,128)(2,1)}, u32[]{:S(2)}, u32[]{:S(2)}) collective-permute-start(bf16[192,2048]{1,0:T(8,128)(2,1)} %bitcast.35), channel_id=1, source_target_pairs={{0,1},{1,0},{2,3},{3,2},{4,5},{5,4},{6,7},{7,6},{8,9},{9,8},{10,11... | collective-permute-start | bytes 2359304 | tf_op jit(solution)/shard_map/cond/branch_1_fun/ppermute | solution.py:51
  142.1 10.1 %collective-permute-start.27 = (bf16[96,2048]{1,0:T(8,128)(2,1)S(1)}, bf16[96,2048]{1,0:T(8,128)(2,1)S(1)}, u32[]{:S(2)}, u32[]{:S(2)}) collective-permute-start(bf16[96,2048]{1,0:T(8,128)(2,1)S(1)} %slice.276), channel_id=1, source_target_pairs={{0,4},{2,6},{4,0},{6,2},{1,5},{3,7},{5,1},{7,3},{8,12},{10,14},{12... | collective-permute-start | bytes 1179656 | tf_op jit(solution)/shard_map/cond/branch_1_fun/ppermute | solution.py:43
  144.2 9.9 %collective-permute-start.26 = (bf16[96,2048]{1,0:T(8,128)(2,1)S(1)}, bf16[96,2048]{1,0:T(8,128)(2,1)S(1)}, u32[]{:S(2)}, u32[]{:S(2)}) collective-permute-start(bf16[96,2048]{1,0:T(8,128)(2,1)S(1)} %slice.274), channel_id=1, source_target_pairs={{0,1},{1,0},{2,3},{3,2},{4,5},{5,4},{6,7},{7,6},{8,9},{9,8},{10,11... | collective-permute-start | bytes 1179656 | tf_op jit(solution)/shard_map/cond/branch_1_fun/ppermute | solution.py:51
  158.5 12.1 %collective-permute-start.28 = (bf16[96,2048]{1,0:T(8,128)(2,1)S(1)}, bf16[96,2048]{1,0:T(8,128)(2,1)S(1)}, u32[]{:S(2)}, u32[]{:S(2)}) collective-permute-start(bf16[96,2048]{1,0:T(8,128)(2,1)S(1)} %get-tuple-element.614.refs_0_), channel_id=1, source_target_pairs={{0,4},{2,6},{4,0},{6,2},{1,5},{3,7},{5,1},{7,3},{8,12},{10,14},{12... | collective-permute-start | bytes 1179656 | tf_op jit(solution)/shard_map/cond/branch_1_fun/ppermute | solution.py:43
  160.0 12.1 %collective-permute-start.31 = (bf16[96,2048]{1,0:T(8,128)(2,1)S(1)}, bf16[96,2048]{1,0:T(8,128)(2,1)S(1)}, u32[]{:S(2)}, u32[]{:S(2)}) collective-permute-start(bf16[96,2048]{1,0:T(8,128)(2,1)S(1)} %get-tuple-element.613.refs_4_), channel_id=1, source_target_pairs={{0,1},{1,0},{2,3},{3,2},{4,5},{5,4},{6,7},{7,6},{8,9},{9,8},{10,11... | collective-permute-start | bytes 1179656 | tf_op jit(solution)/shard_map/cond/branch_1_fun/ppermute | solution.py:51
  160.9 19.5 %collective-permute-start.29 = (bf16[96,2048]{1,0:T(8,128)(2,1)S(1)}, bf16[96,2048]{1,0:T(8,128)(2,1)S(1)}, u32[]{:S(2)}, u32[]{:S(2)}) collective-permute-start(bf16[96,2048]{1,0:T(8,128)(2,1)S(1)} %get-tuple-element.614.refs_0_), channel_id=1, source_target_pairs={{0,1},{1,0},{2,3},{3,2},{4,5},{5,4},{6,7},{7,6},{8,9},{9,8},{10,11... | collective-permute-start | bytes 1179656 | tf_op jit(solution)/shard_map/cond/branch_1_fun/ppermute | solution.py:51
  162.0 18.5 %collective-permute-start.32 = (bf16[96,2048]{1,0:T(8,128)(2,1)S(1)}, bf16[96,2048]{1,0:T(8,128)(2,1)S(1)}, u32[]{:S(2)}, u32[]{:S(2)}) collective-permute-start(bf16[96,2048]{1,0:T(8,128)(2,1)S(1)} %get-tuple-element.613.refs_4_), channel_id=1, source_target_pairs={{0,4},{2,6},{4,0},{6,2},{1,5},{3,7},{5,1},{7,3},{8,12},{10,14},{12... | collective-permute-start | bytes 1179656 | tf_op jit(solution)/shard_map/cond/branch_1_fun/ppermute | solution.py:43
  170.6 14.8 %collective-permute-start.30 = (bf16[96,2048]{1,0:T(8,128)(2,1)S(1)}, bf16[96,2048]{1,0:T(8,128)(2,1)S(1)}, u32[]{:S(2)}, u32[]{:S(2)}) collective-permute-start(bf16[96,2048]{1,0:T(8,128)(2,1)S(1)} %collective-permute-done.28.refs_1_), channel_id=1, source_target_pairs={{0,1},{1,0},{2,3},{3,2},{4,5},{5,4},{6,7},{7,6},{8,9},{9,8},{10,11... | collective-permute-start | bytes 1179656 | tf_op jit(solution)/shard_map/cond/branch_1_fun/ppermute | solution.py:51
  172.0 13.4 %collective-permute-start.33 = (bf16[96,2048]{1,0:T(8,128)(2,1)S(1)}, bf16[96,2048]{1,0:T(8,128)(2,1)S(1)}, u32[]{:S(2)}, u32[]{:S(2)}) collective-permute-start(bf16[96,2048]{1,0:T(8,128)(2,1)S(1)} %collective-permute-done.31.refs_5_), channel_id=1, source_target_pairs={{0,4},{2,6},{4,0},{6,2},{1,5},{3,7},{5,1},{7,3},{8,12},{10,14},{12... | collective-permute-start | bytes 1179656 | tf_op jit(solution)/shard_map/cond/branch_1_fun/ppermute | solution.py:43
  173.0 17.6 %collective-permute-start.23 = (bf16[768,2048]{1,0:T(8,128)(2,1)}, bf16[768,2048]{1,0:T(8,128)(2,1)}, u32[]{:S(2)}, u32[]{:S(2)}) collective-permute-start(bf16[768,2048]{1,0:T(8,128)(2,1)} %join.5), channel_id=1, source_target_pairs={{0,2},{2,0},{4,6},{6,4},{1,3},{3,1},{5,7},{7,5},{8,10},{10,8},{12,... | collective-permute-start | bytes 9437192 | tf_op jit(solution)/shard_map/cond/branch_1_fun/ppermute | solution.py:47
  190.5 6.1 %collective-permute-start.34 = (bf16[768,2048]{1,0:T(8,128)(2,1)}, bf16[768,2048]{1,0:T(8,128)(2,1)}, u32[]{:S(2)}, u32[]{:S(2)}) collective-permute-start(bf16[768,2048]{1,0:T(8,128)(2,1)} %join.6), channel_id=1, source_target_pairs={{0,2},{2,0},{4,6},{6,4},{1,3},{3,1},{5,7},{7,5},{8,10},{10,8},{12,... | collective-permute-start | bytes 9437192 | tf_op jit(solution)/shard_map/cond/branch_1_fun/ppermute | solution.py:47
  233.6 204.0 %reduce-scatter.6.cloned.1.call-start = ((), (), s32[]{:S(2)}) async-start(), calls=%async_computation.7 | async-start | bytes 2703360 | tf_op jit(solution)/shard_map/reduce_scatter | solution.py:170
  258.7 231.5 %reduce-scatter.8.cloned.1.call-start = ((), (), s32[]{:S(2)}) async-start(), calls=%async_computation.8 | async-start | bytes 3358720 | tf_op jit(solution)/shard_map/reduce_scatter | solution.py:170
  268.0 7.3 %collective-permute-start.35 = (bf16[768,2048]{1,0:T(8,128)(2,1)S(1)}, bf16[768,2048]{1,0:T(8,128)(2,1)S(1)}, u32[]{:S(2)}, u32[]{:S(2)}) collective-permute-start(bf16[768,2048]{1,0:T(8,128)(2,1)S(1)} %add_convert_fusion.7), channel_id=1, source_target_pairs={{0,2},{2,0},{4,6},{6,4},{1,3},{3,1},{5,7},{7,5},{8,10},{10,8},{12,... | collective-permute-start | bytes 9437192 | tf_op jit(solution)/shard_map/cond/branch_1_fun/ppermute | solution.py:47
  277.1 19.1 %collective-permute-start.36 = (bf16[192,2048]{1,0:T(8,128)(2,1)S(1)}, bf16[192,2048]{1,0:T(8,128)(2,1)S(1)}, u32[]{:S(2)}, u32[]{:S(2)}) collective-permute-start(bf16[192,2048]{1,0:T(8,128)(2,1)S(1)} %bitcast.144), channel_id=1, source_target_pairs={{0,4},{2,6},{4,0},{6,2},{1,5},{3,7},{5,1},{7,3},{8,12},{10,14},{12... | collective-permute-start | bytes 2359304 | tf_op jit(solution)/shard_map/cond/branch_1_fun/ppermute | solution.py:43
  278.5 18.8 %collective-permute-start.37 = (bf16[192,2048]{1,0:T(8,128)(2,1)S(1)}, bf16[192,2048]{1,0:T(8,128)(2,1)S(1)}, u32[]{:S(2)}, u32[]{:S(2)}) collective-permute-start(bf16[192,2048]{1,0:T(8,128)(2,1)S(1)} %bitcast.145), channel_id=1, source_target_pairs={{0,1},{1,0},{2,3},{3,2},{4,5},{5,4},{6,7},{7,6},{8,9},{9,8},{10,11... | collective-permute-start | bytes 2359304 | tf_op jit(solution)/shard_map/cond/branch_1_fun/ppermute | solution.py:51
  285.1 43.3 %collective-permute-start.46 = (bf16[768,2048]{1,0:T(8,128)(2,1)S(1)}, bf16[768,2048]{1,0:T(8,128)(2,1)S(1)}, u32[]{:S(2)}, u32[]{:S(2)}) collective-permute-start(bf16[768,2048]{1,0:T(8,128)(2,1)S(1)} %add_convert_fusion.5), channel_id=1, source_target_pairs={{0,2},{2,0},{4,6},{6,4},{1,3},{3,1},{5,7},{7,5},{8,10},{10,8},{12,... | collective-permute-start | bytes 9437192 | tf_op jit(solution)/shard_map/cond/branch_1_fun/ppermute | solution.py:47
  297.6 9.6 %collective-permute-start.39 = (bf16[96,2048]{1,0:T(8,128)(2,1)S(1)}, bf16[96,2048]{1,0:T(8,128)(2,1)S(1)}, u32[]{:S(2)}, u32[]{:S(2)}) collective-permute-start(bf16[96,2048]{1,0:T(8,128)(2,1)S(1)} %slice.288), channel_id=1, source_target_pairs={{0,4},{2,6},{4,0},{6,2},{1,5},{3,7},{5,1},{7,3},{8,12},{10,14},{12... | collective-permute-start | bytes 1179656 | tf_op jit(solution)/shard_map/cond/branch_1_fun/ppermute | solution.py:43
  298.7 9.3 %collective-permute-start.38 = (bf16[96,2048]{1,0:T(8,128)(2,1)S(1)}, bf16[96,2048]{1,0:T(8,128)(2,1)S(1)}, u32[]{:S(2)}, u32[]{:S(2)}) collective-permute-start(bf16[96,2048]{1,0:T(8,128)(2,1)S(1)} %slice.286), channel_id=1, source_target_pairs={{0,1},{1,0},{2,3},{3,2},{4,5},{5,4},{6,7},{7,6},{8,9},{9,8},{10,11... | collective-permute-start | bytes 1179656 | tf_op jit(solution)/shard_map/cond/branch_1_fun/ppermute | solution.py:51
  313.5 12.1 %collective-permute-start.40 = (bf16[96,2048]{1,0:T(8,128)(2,1)S(1)}, bf16[96,2048]{1,0:T(8,128)(2,1)S(1)}, u32[]{:S(2)}, u32[]{:S(2)}) collective-permute-start(bf16[96,2048]{1,0:T(8,128)(2,1)S(1)} %get-tuple-element.636.refs_0_), channel_id=1, source_target_pairs={{0,4},{2,6},{4,0},{6,2},{1,5},{3,7},{5,1},{7,3},{8,12},{10,14},{12... | collective-permute-start | bytes 1179656 | tf_op jit(solution)/shard_map/cond/branch_1_fun/ppermute | solution.py:43
  314.8 12.1 %collective-permute-start.43 = (bf16[96,2048]{1,0:T(8,128)(2,1)S(1)}, bf16[96,2048]{1,0:T(8,128)(2,1)S(1)}, u32[]{:S(2)}, u32[]{:S(2)}) collective-permute-start(bf16[96,2048]{1,0:T(8,128)(2,1)S(1)} %get-tuple-element.635.refs_4_), channel_id=1, source_target_pairs={{0,1},{1,0},{2,3},{3,2},{4,5},{5,4},{6,7},{7,6},{8,9},{9,8},{10,11... | collective-permute-start | bytes 1179656 | tf_op jit(solution)/shard_map/cond/branch_1_fun/ppermute | solution.py:51
  316.3 19.0 %collective-permute-start.41 = (bf16[96,2048]{1,0:T(8,128)(2,1)S(1)}, bf16[96,2048]{1,0:T(8,128)(2,1)S(1)}, u32[]{:S(2)}, u32[]{:S(2)}) collective-permute-start(bf16[96,2048]{1,0:T(8,128)(2,1)S(1)} %get-tuple-element.636.refs_0_), channel_id=1, source_target_pairs={{0,1},{1,0},{2,3},{3,2},{4,5},{5,4},{6,7},{7,6},{8,9},{9,8},{10,11... | collective-permute-start | bytes 1179656 | tf_op jit(solution)/shard_map/cond/branch_1_fun/ppermute | solution.py:51
  316.9 18.5 %collective-permute-start.44 = (bf16[96,2048]{1,0:T(8,128)(2,1)S(1)}, bf16[96,2048]{1,0:T(8,128)(2,1)S(1)}, u32[]{:S(2)}, u32[]{:S(2)}) collective-permute-start(bf16[96,2048]{1,0:T(8,128)(2,1)S(1)} %get-tuple-element.635.refs_4_), channel_id=1, source_target_pairs={{0,4},{2,6},{4,0},{6,2},{1,5},{3,7},{5,1},{7,3},{8,12},{10,14},{12... | collective-permute-start | bytes 1179656 | tf_op jit(solution)/shard_map/cond/branch_1_fun/ppermute | solution.py:43
  325.6 14.2 %collective-permute-start.42 = (bf16[96,2048]{1,0:T(8,128)(2,1)S(1)}, bf16[96,2048]{1,0:T(8,128)(2,1)S(1)}, u32[]{:S(2)}, u32[]{:S(2)}) collective-permute-start(bf16[96,2048]{1,0:T(8,128)(2,1)S(1)} %collective-permute-done.40.refs_1_), channel_id=1, source_target_pairs={{0,1},{1,0},{2,3},{3,2},{4,5},{5,4},{6,7},{7,6},{8,9},{9,8},{10,11... | collective-permute-start | bytes 1179656 | tf_op jit(solution)/shard_map/cond/branch_1_fun/ppermute | solution.py:51
  326.9 12.9 %collective-permute-start.45 = (bf16[96,2048]{1,0:T(8,128)(2,1)S(1)}, bf16[96,2048]{1,0:T(8,128)(2,1)S(1)}, u32[]{:S(2)}, u32[]{:S(2)}) collective-permute-start(bf16[96,2048]{1,0:T(8,128)(2,1)S(1)} %collective-permute-done.43.refs_5_), channel_id=1, source_target_pairs={{0,4},{2,6},{4,0},{6,2},{1,5},{3,7},{5,1},{7,3},{8,12},{10,14},{12... | collective-permute-start | bytes 1179656 | tf_op jit(solution)/shard_map/cond/branch_1_fun/ppermute | solution.py:43
  344.4 6.1 %collective-permute-start.47 = (bf16[768,2048]{1,0:T(8,128)(2,1)}, bf16[768,2048]{1,0:T(8,128)(2,1)}, u32[]{:S(2)}, u32[]{:S(2)}) collective-permute-start(bf16[768,2048]{1,0:T(8,128)(2,1)} %join.7), channel_id=1, source_target_pairs={{0,2},{2,0},{4,6},{6,4},{1,3},{3,1},{5,7},{7,5},{8,10},{10,8},{12,... | collective-permute-start | bytes 9437192 | tf_op jit(solution)/shard_map/cond/branch_1_fun/ppermute | solution.py:47
  350.9 20.4 %collective-permute-start.48 = (bf16[192,2048]{1,0:T(8,128)(2,1)}, bf16[192,2048]{1,0:T(8,128)(2,1)}, u32[]{:S(2)}, u32[]{:S(2)}) collective-permute-start(bf16[192,2048]{1,0:T(8,128)(2,1)} %get-tuple-element.290), channel_id=1, source_target_pairs={{0,4},{2,6},{4,0},{6,2},{1,5},{3,7},{5,1},{7,3},{8,12},{10,14},{12... | collective-permute-start | bytes 2359304 | tf_op jit(solution)/shard_map/cond/branch_1_fun/ppermute | solution.py:43
  352.3 19.4 %collective-permute-start.49 = (bf16[192,2048]{1,0:T(8,128)(2,1)}, bf16[192,2048]{1,0:T(8,128)(2,1)}, u32[]{:S(2)}, u32[]{:S(2)}) collective-permute-start(bf16[192,2048]{1,0:T(8,128)(2,1)} %get-tuple-element.291), channel_id=1, source_target_pairs={{0,1},{1,0},{2,3},{3,2},{4,5},{5,4},{6,7},{7,6},{8,9},{9,8},{10,11... | collective-permute-start | bytes 2359304 | tf_op jit(solution)/shard_map/cond/branch_1_fun/ppermute | solution.py:51
  377.4 9.7 %collective-permute-start.52 = (bf16[768,2048]{1,0:T(8,128)(2,1)S(1)}, bf16[768,2048]{1,0:T(8,128)(2,1)S(1)}, u32[]{:S(2)}, u32[]{:S(2)}) collective-permute-start(bf16[768,2048]{1,0:T(8,128)(2,1)S(1)} %convolution_convert_fusion.3), channel_id=1, source_target_pairs={{0,2},{2,0},{4,6},{6,4},{1,3},{3,1},{5,7},{7,5},{8,10},{10,8},{12,... | collective-permute-start | bytes 9437192 | tf_op jit(solution)/shard_map/cond/branch_1_fun/ppermute | solution.py:47
  378.6 58.7 %collective-permute-start.58 = (bf16[1056,512]{1,0:T(8,128)(2,1)}, bf16[1056,512]{1,0:T(8,128)(2,1)}, u32[]{:S(2)}, u32[]{:S(2)}) collective-permute-start(bf16[1056,512]{1,0:T(8,128)(2,1)} %slice.249), channel_id=1, source_target_pairs={{0,4},{2,6},{4,0},{6,2},{1,5},{3,7},{5,1},{7,3},{8,12},{10,14},{12... | collective-permute-start | bytes 3244040 | tf_op jit(solution)/shard_map/cond/branch_1_fun/ppermute | solution.py:43
  389.1 32.7 %collective-permute-start.53 = (bf16[192,2048]{1,0:T(8,128)(2,1)S(1)}, bf16[192,2048]{1,0:T(8,128)(2,1)S(1)}, u32[]{:S(2)}, u32[]{:S(2)}) collective-permute-start(bf16[192,2048]{1,0:T(8,128)(2,1)S(1)} %bitcast.142), channel_id=1, source_target_pairs={{0,4},{2,6},{4,0},{6,2},{1,5},{3,7},{5,1},{7,3},{8,12},{10,14},{12... | collective-permute-start | bytes 2359304 | tf_op jit(solution)/shard_map/cond/branch_1_fun/ppermute | solution.py:43
  390.3 31.5 %collective-permute-start.54 = (bf16[192,2048]{1,0:T(8,128)(2,1)S(1)}, bf16[192,2048]{1,0:T(8,128)(2,1)S(1)}, u32[]{:S(2)}, u32[]{:S(2)}) collective-permute-start(bf16[192,2048]{1,0:T(8,128)(2,1)S(1)} %bitcast.143), channel_id=1, source_target_pairs={{0,1},{1,0},{2,3},{3,2},{4,5},{5,4},{6,7},{7,6},{8,9},{9,8},{10,11... | collective-permute-start | bytes 2359304 | tf_op jit(solution)/shard_map/cond/branch_1_fun/ppermute | solution.py:51
  402.1 9.1 %collective-permute-start.57 = (bf16[16,2048]{1,0:T(8,128)(2,1)S(1)}, bf16[16,2048]{1,0:T(8,128)(2,1)S(1)}, u32[]{:S(2)}, u32[]{:S(2)}) collective-permute-start(bf16[16,2048]{1,0:T(8,128)(2,1)S(1)} %fusion.31), channel_id=1, source_target_pairs={{0,1},{1,0},{2,3},{3,2},{4,5},{5,4},{6,7},{7,6},{8,9},{9,8},{10,11... | collective-permute-start | bytes 196616 | tf_op jit(solution)/shard_map/cond/branch_1_fun/ppermute | solution.py:51
  422.1 10.6 %collective-permute-start.55 = (bf16[96,2048]{1,0:T(8,128)(2,1)S(1)}, bf16[96,2048]{1,0:T(8,128)(2,1)S(1)}, u32[]{:S(2)}, u32[]{:S(2)}) collective-permute-start(bf16[96,2048]{1,0:T(8,128)(2,1)S(1)} %slice.303), channel_id=1, source_target_pairs={{0,1},{1,0},{2,3},{3,2},{4,5},{5,4},{6,7},{7,6},{8,9},{9,8},{10,11... | collective-permute-start | bytes 1179656 | tf_op jit(solution)/shard_map/cond/branch_1_fun/ppermute | solution.py:51
  424.0 10.5 %collective-permute-start.56 = (bf16[96,2048]{1,0:T(8,128)(2,1)S(1)}, bf16[96,2048]{1,0:T(8,128)(2,1)}, u32[]{:S(2)}, u32[]{:S(2)}) collective-permute-start(bf16[96,2048]{1,0:T(8,128)(2,1)S(1)} %slice.304), channel_id=1, source_target_pairs={{0,4},{2,6},{4,0},{6,2},{1,5},{3,7},{5,1},{7,3},{8,12},{10,14},{12... | collective-permute-start | bytes 1179656 | tf_op jit(solution)/shard_map/cond/branch_1_fun/ppermute | solution.py:43
  438.8 9.9 %collective-permute-start.1 = (bf16[96,2048]{1,0:T(8,128)(2,1)S(1)}, bf16[96,2048]{1,0:T(8,128)(2,1)S(1)}, u32[]{:S(2)}, u32[]{:S(2)}) collective-permute-start(bf16[96,2048]{1,0:T(8,128)(2,1)S(1)} %slice.253), channel_id=1, source_target_pairs={{0,4},{2,6},{4,0},{6,2},{1,5},{3,7},{5,1},{7,3},{8,12},{10,14},{12... | collective-permute-start | bytes 1179656 | tf_op jit(solution)/shard_map/cond/branch_1_fun/ppermute | solution.py:43
  440.8 9.2 %collective-permute-start = (bf16[96,2048]{1,0:T(8,128)(2,1)S(1)}, bf16[96,2048]{1,0:T(8,128)(2,1)S(1)}, u32[]{:S(2)}, u32[]{:S(2)}) collective-permute-start(bf16[96,2048]{1,0:T(8,128)(2,1)S(1)} %slice.251), channel_id=1, source_target_pairs={{0,1},{1,0},{2,3},{3,2},{4,5},{5,4},{6,7},{7,6},{8,9},{9,8},{10,11... | collective-permute-start | bytes 1179656 | tf_op jit(solution)/shard_map/cond/branch_1_fun/ppermute | solution.py:51
  441.4 26.6 %collective-permute-start.2 = (bf16[1584,512]{1,0:T(8,128)(2,1)}, bf16[1584,512]{1,0:T(8,128)(2,1)}, u32[]{:S(2)}, u32[]{:S(2)}) collective-permute-start(bf16[1584,512]{1,0:T(8,128)(2,1)} %get-tuple-element.322.refs_0_), channel_id=1, source_target_pairs={{0,2},{2,0},{4,6},{6,4},{1,3},{3,1},{5,7},{7,5},{8,10},{10,8},{12,... | collective-permute-start | bytes 4866056 | tf_op jit(solution)/shard_map/cond/branch_1_fun/ppermute | solution.py:47
  441.4 26.6 %collective-permute-start.3 = (bf16[1056,512]{1,0:T(8,128)(2,1)}, bf16[1056,512]{1,0:T(8,128)(2,1)}, u32[]{:S(2)}, u32[]{:S(2)}) collective-permute-start(bf16[1056,512]{1,0:T(8,128)(2,1)} %get-tuple-element.323.refs_2_), channel_id=1, source_target_pairs={{0,2},{2,0},{4,6},{6,4},{1,3},{3,1},{5,7},{7,5},{8,10},{10,8},{12,... | collective-permute-start | bytes 3244040 | tf_op jit(solution)/shard_map/cond/branch_1_fun/ppermute | solution.py:47
  441.9 24.8 %collective-permute-start.4 = (bf16[528,512]{1,0:T(8,128)(2,1)}, bf16[528,512]{1,0:T(8,128)(2,1)}, u32[]{:S(2)}, u32[]{:S(2)}) collective-permute-start(bf16[528,512]{1,0:T(8,128)(2,1)} %get-tuple-element.324.refs_4_), channel_id=1, source_target_pairs={{0,2},{2,0},{4,6},{6,4},{1,3},{3,1},{5,7},{7,5},{8,10},{10,8},{12,... | collective-permute-start | bytes 1622024 | tf_op jit(solution)/shard_map/cond/branch_1_fun/ppermute | solution.py:47
  455.8 7.6 %collective-permute-start.5 = (bf16[176,512]{1,0:T(8,128)(2,1)}, bf16[176,512]{1,0:T(8,128)(2,1)S(1)}, u32[]{:S(2)}, u32[]{:S(2)}) collective-permute-start(bf16[176,512]{1,0:T(8,128)(2,1)} %hold.4), channel_id=1, source_target_pairs={{0,4},{2,6},{4,0},{6,2},{1,5},{3,7},{5,1},{7,3},{8,12},{10,14},{12... | collective-permute-start | bytes 540680 | tf_op jit(solution)/shard_map/cond/branch_1_fun/ppermute | solution.py:43
  459.1 23.2 %collective-permute-start.7 = (bf16[880,512]{1,0:T(8,128)(2,1)}, bf16[880,512]{1,0:T(8,128)(2,1)}, u32[]{:S(2)}, u32[]{:S(2)}) collective-permute-start(bf16[880,512]{1,0:T(8,128)(2,1)} %hold.5), channel_id=1, source_target_pairs={{0,4},{2,6},{4,0},{6,2},{1,5},{3,7},{5,1},{7,3},{8,12},{10,14},{12... | collective-permute-start | bytes 2703368 | tf_op jit(solution)/shard_map/cond/branch_1_fun/ppermute | solution.py:43
  466.7 20.2 %collective-permute-start.9 = (bf16[192,2048]{1,0:T(8,128)(2,1)}, bf16[192,2048]{1,0:T(8,128)(2,1)S(1)}, u32[]{:S(2)}, u32[]{:S(2)}) collective-permute-start(bf16[192,2048]{1,0:T(8,128)(2,1)} %add_convert_fusion.20), channel_id=1, source_target_pairs={{0,1},{1,0},{2,3},{3,2},{4,5},{5,4},{6,7},{7,6},{8,9},{9,8},{10,11... | collective-permute-start | bytes 2359304 | tf_op jit(solution)/shard_map/cond/branch_1_fun/ppermute | solution.py:51
  490.2 16.9 %collective-permute-start.11 = (bf16[656,512]{1,0:T(8,128)(2,1)}, bf16[656,512]{1,0:T(8,128)(2,1)S(1)}, u32[]{:S(2)}, u32[]{:S(2)}) collective-permute-start(bf16[656,512]{1,0:T(8,128)(2,1)} %get-tuple-element.339.r0), channel_id=1, source_target_pairs={{0,4},{2,6},{4,0},{6,2},{1,5},{3,7},{5,1},{7,3},{8,12},{10,14},{12... | collective-permute-start | bytes 2015240 | tf_op jit(solution)/shard_map/cond/branch_1_fun/ppermute | solution.py:43
  491.3 19.2 %collective-permute-start.13 = (bf16[192,2048]{1,0:T(8,128)(2,1)}, bf16[192,2048]{1,0:T(8,128)(2,1)S(1)}, u32[]{:S(2)}, u32[]{:S(2)}) collective-permute-start(bf16[192,2048]{1,0:T(8,128)(2,1)} %get-tuple-element.346), channel_id=1, source_target_pairs={{0,1},{1,0},{2,3},{3,2},{4,5},{5,4},{6,7},{7,6},{8,9},{9,8},{10,11... | collective-permute-start | bytes 2359304 | tf_op jit(solution)/shard_map/cond/branch_1_fun/ppermute | solution.py:51
  492.8 21.2 %collective-permute-start.10 = (bf16[656,512]{1,0:T(8,128)(2,1)}, bf16[656,512]{1,0:T(8,128)(2,1)}, u32[]{:S(2)}, u32[]{:S(2)}) collective-permute-start(bf16[656,512]{1,0:T(8,128)(2,1)} %get-tuple-element.339.r0), channel_id=1, source_target_pairs={{0,2},{2,0},{4,6},{6,4},{1,3},{3,1},{5,7},{7,5},{8,10},{10,8},{12,... | collective-permute-start | bytes 2015240 | tf_op jit(solution)/shard_map/cond/branch_1_fun/ppermute | solution.py:47
  (77 other events, 461.0 us)
Sparse Core Ops, SparseCore 0:
  10.8 58.5 all-gather.5
  71.5 117.3 all-gather.3
  190.5 45.4 all-gather.7
  238.2 112.6 reduce-scatter.3
  353.1 45.4 reduce-scatter.5
  437.7 52.0 reduce-scatter.7

commit v4 on v3

--- a/solution.py
+++ b/solution.py
@@ -435,7 +435,8 @@
     )(starts, *q, *own, *got, *d_out, *out, lse, lo, hi, cosine, sine)
 
 
-def hidden_kernel(ff, w_ref, n2_ref, df_ref, out_ref):
+def hidden_kernel(ff, w_ref, n2_ref, df_ref, *rest):
+    out_ref = rest[-1]
     dh = dot(w_ref[2 * ff :, :], df_ref[...], 1, 1)
     gu = dot(w_ref[: 2 * ff, :], n2_ref[...], 1, 1)
     gate, up = gu[:ff], gu[ff:]
@@ -446,7 +447,7 @@
     out_ref[2 * ff :, :] = (silu * up).astype(BF16)
 
 
-def hidden_half(w, n2, df):
+def hidden_half(w, n2, df, *others):
     rows, width = n2.shape
     ff = w.shape[0] // 3
     tile = rows // 3
@@ -458,13 +459,14 @@
             pl.BlockSpec((3 * ff, width), lambda r: (0, 0), pipeline_mode=pl.Buffered(1)),
             pl.BlockSpec((tile, width), lambda r: (r, 0)),
             pl.BlockSpec((tile, width), lambda r: (r, 0)),
-        ],
+        ]
+        + [pl.BlockSpec(memory_space=pl.ANY)] * len(others),
         out_specs=pl.BlockSpec((3 * ff, tile), lambda r: (0, r)),
         cost_estimate=pl.CostEstimate(
             flops=6 * rows * width * ff, bytes_accessed=6 * ff * width, transcendentals=ff * rows
         ),
         name="hidden",
-    )(w, n2, df)
+    )(w, n2, df, *others)
 
 
 def grads_kernel(ff, lm_ref, lo_ref, nm_ref, no_ref, dm_ref, do_ref, out_ref):
@@ -718,7 +720,7 @@
     grad_a = feed_grads((am, ao), (n2m, n2o), (dfm, dfo))
     shard_a = scatter_whole(grad_a)
     pao = dot(ao[: 2 * part_a], wa[: 2 * part_a], 0, 0).astype(BF16)
-    bm, bo = hidden_half(wb, n2m, dfm), hidden_half(wb, n2o, dfo)
+    bm, bo = hidden_half(wb, n2m, dfm, pao), hidden_half(wb, n2o, dfo, pao)
     grad_b = feed_grads((bm, bo), (n2m, n2o), (dfm, dfo))
     shard_b = scatter_whole(grad_b)
 

time: 540 us -> 549 us (1.017)
  loops' own time: 2.65 us -> 12.9 us
    another operation x6, loops' own time: 2.65 us -> 12.9 us  [fenced(): return lax.cond(flag, stage, empty, *values)]
  transfers between devices with their start and end apart: 72 -> 72, of which waited for: 35 -> 33; matrix products, arithmetic and copies ran while one was open for 30% -> 30% of each run, Pallas kernels for 27% -> 26%
where the time goes in v4:
time: 549 us; the launch traced here: 544 us
  Pallas kernels  149 us (27%)
  waiting for transfers between devices  135 us (25%)
  other arithmetic  71.1 us (13%)
  matrix products  55.5 us (10%)
  starting transfers between devices  53.8 us (10%)
  local copies, waits for them, and re-layouts  51.3 us (9%)
  between operations  15.2 us (3%)
  loops' own time  12.9 us (2%)
    ppermute x24, waiting for transfers between devices, far(): return lax.ppermute(v, 'ctx', [(i, i ^ 2) for i in range(4)])  77.9 us
    dot_general x18, matrix products, dot(): lax.dot_general(a, b, (((ca,), (cb,)), ((), ())), preferred_element_type=...  55.5 us
    ppermute x23, waiting for transfers between devices, side(): return lax.ppermute(v, 'tp', [(0, 1), (1, 0)])  37.4 us
    pallas_call x4, Pallas kernels, hidden_half(): pl.pallas_call(functools.partial(hidden_kernel, ff), out_shape=jax.ShapeD...  32.5 us
    ppermute x23, starting transfers between devices, side(): return lax.ppermute(v, 'tp', [(0, 1), (1, 0)])  27.4 us
    pallas_call x2, Pallas kernels, feed_grads(): pl.pallas_call(functools.partial(grads_kernel, rows // 3), out_shape=jax....  26.2 us
    ppermute x24, starting transfers between devices, far(): return lax.ppermute(v, 'ctx', [(i, i ^ 2) for i in range(4)])  24.2 us
    pallas_call x3, Pallas kernels, finish(): pl.pallas_call(functools.partial(finish_kernel, (turned, firsts), sizes),...  19.6 us
  transfers between devices with their start and end apart: 72, of which 33 were waited for; matrix products, arithmetic and copies ran while one was open for 30% of the time, Pallas kernels for 26%

profile of v4, /device:TPU:0, one launch (start us, length us, event | category | flops | bytes accessed | tf_op | source)
XLA Modules:
  0.0 543.6 jit_solution(6807241689018684052)
XLA Ops:
  12.0 53.0 %conditional.6 = (f32[192,2048]{1,0:T(8,128)S(1)}, f32[192,1]{0,1:T(1,128)S(1)}, f32[192,2048]{1,0:T(8,128)}, bf16[192,2048]{1,0:T(8,128)(2,1)}, bf16[768,2048]{...) conditional(s32[]{:T(128)} %bitcast.69, () %tuple.79, ...), branch_computations={%region_0.0_spmd, %region_1.5_spmd} | conditional | flops 17967146 | bytes 63024752 | solution.py:34
  14.1 2.9 collective-permute-start.59
  19.1 3.2 copy.84
  28.9 4.4 fusion.32
  36.5 3.0 concatenate.57
  39.7 3.1 pad_maximum_fusion.8
  47.9 5.2 collective-permute-done.63.refs_3_
  55.3 3.6 join.4
  60.3 4.6 collective-permute-done.65
  69.5 137.4 %conditional.7 = (bf16[768,2048]{1,0:T(8,128)(2,1)}, bf16[768,2048]{1,0:T(8,128)(2,1)}, bf16[768,256]{1,0:T(8,128)(2,1)}, bf16[768,256]{1,0:T(8,128)(2,1)}, bf16...) conditional(s32[]{:T(128)} %bitcast.69, () %tuple.83, ...), branch_computations={%region_5.6_spmd, %region_6.8_spmd} | conditional | flops 11291199488 | bytes 187464880 | solution.py:34
  89.4 5.5 %qkv.3 = (bf16[768,2048]{1,0:T(8,128)(2,1)}, bf16[768,256]{1,0:T(8,128)(2,1)}, bf16[768,128]{1,0:T(8,128)(2,1)}) custom-call(s32[1]{0:T(128)} %get-tuple-element.210.core_ref, bf16[768,2048]{1,0:T(8,128)(2,1)} %get-tuple-element.216.x_ref, bf16[656,2048]{1,0:T(8,128)(2,1)S(1)} %copy-done.1, bf16[656,2048]{1,0:T(8,128)(2,1)S(1)} %copy-done.1, ...), custom_call_target="tpu_custom_call" | custom-call | flops 1207959552 | bytes 7864320 | tf_op jit(solution)/shard_map/cond/branch_1_fun/qkv/pallas_call | solution.py:237
  95.0 5.5 %qkv.2 = (bf16[768,2048]{1,0:T(8,128)(2,1)}, bf16[768,256]{1,0:T(8,128)(2,1)}, bf16[768,128]{1,0:T(8,128)(2,1)}) custom-call(s32[1]{0:T(128)} %get-tuple-element.210.core_ref, bf16[768,2048]{1,0:T(8,128)(2,1)} %get-tuple-element.211.x_ref, bf16[656,2048]{1,0:T(8,128)(2,1)S(1)} %copy-done.1, bf16[656,2048]{1,0:T(8,128)(2,1)S(1)} %copy-done.1, ...), custom_call_target="tpu_custom_call" | custom-call | flops 1207959552 | bytes 7864320 | tf_op jit(solution)/shard_map/cond/branch_1_fun/qkv/pallas_call | solution.py:237
  105.0 13.8 %attn_forward.1 = (bf16[768,256]{1,0:T(8,128)(2,1)S(1)}, bf16[768,256]{1,0:T(8,128)(2,1)S(1)}, f32[2,1,1536]{2,1,0:T(1,128)S(1)}) custom-call(s32[17]{0:T(128)S(1)} %get-tuple-element.225.starts_ref, bf16[768,256]{1,0:T(8,128)(2,1)} %get-tuple-element.694.qm, bf16[768,256]{1,0:T(8,128)(2,1)} %get-tuple-element.695.qo, ...), custom_call_target="tpu_custom_call" | custom-call | flops 7247757312 | bytes 3145728 | tf_op jit(solution)/shard_map/cond/branch_1_fun/attn_forward/pallas_call | solution.py:338
  120.9 4.6 collective-permute-done.22
  132.5 3.6 join.5
  136.0 13.6 %collective-permute-done.24 = bf16[192,2048]{1,0:T(8,128)(2,1)} collective-permute-done((bf16[192,2048]{1,0:T(8,128)(2,1)}, bf16[192,2048]{1,0:T(8,128)(2,1)}, u32[]{:S(2)}, u32[]{:S(2)}) %collective-permute-start.24) | collective-permute-done | bytes 786464 | tf_op jit(solution)/shard_map/cond/branch_1_fun/ppermute | solution.py:43
  155.7 6.6 %collective-permute-done.27 = bf16[96,2048]{1,0:T(8,128)(2,1)S(1)} collective-permute-done((bf16[96,2048]{1,0:T(8,128)(2,1)S(1)}, bf16[96,2048]{1,0:T(8,128)(2,1)S(1)}, u32[]{:S(2)}, u32[]{:S(2)}) %collective-permute-start.27) | collective-permute-done | bytes 393248 | tf_op jit(solution)/shard_map/cond/branch_1_fun/ppermute | solution.py:43
  172.8 8.0 %collective-permute-done.28.refs_1_ = bf16[96,2048]{1,0:T(8,128)(2,1)S(1)} collective-permute-done((bf16[96,2048]{1,0:T(8,128)(2,1)S(1)}, bf16[96,2048]{1,0:T(8,128)(2,1)S(1)}, u32[]{:S(2)}, u32[]{:S(2)}) %collective-permute-start.28) | collective-permute-done | bytes 393248 | tf_op jit(solution)/shard_map/cond/branch_1_fun/ppermute | solution.py:43
  183.4 7.2 %collective-permute-done.29.refs_2_ = bf16[96,2048]{1,0:T(8,128)(2,1)S(1)} collective-permute-done((bf16[96,2048]{1,0:T(8,128)(2,1)S(1)}, bf16[96,2048]{1,0:T(8,128)(2,1)S(1)}, u32[]{:S(2)}, u32[]{:S(2)}) %collective-permute-start.29) | collective-permute-done | bytes 393248 | tf_op jit(solution)/shard_map/cond/branch_1_fun/ppermute | solution.py:51
  190.6 5.0 collective-permute-done.30.refs_3_
  197.1 3.6 join.6
  200.8 6.0 %collective-permute-done.34 = bf16[768,2048]{1,0:T(8,128)(2,1)} collective-permute-done((bf16[768,2048]{1,0:T(8,128)(2,1)}, bf16[768,2048]{1,0:T(8,128)(2,1)}, u32[]{:S(2)}, u32[]{:S(2)}) %collective-permute-start.34) | collective-permute-done | bytes 3145760 | tf_op jit(solution)/shard_map/cond/branch_1_fun/ppermute | solution.py:47
  207.0 9.6 %hidden.4.lm_ref = bf16[1584,768]{1,0:T(8,128)(2,1)S(1)} custom-call(bf16[1584,2048]{1,0:T(8,128)(2,1)} %all-gather.4.cloned.1.call-done.w_ref, bf16[768,2048]{1,0:T(8,128)(2,1)} %get-tuple-element.456.n2_ref.nm_ref, bf16[768,2048]{1,0:T(8,128)(2,1)} %get-tuple-element.457.df_ref.dm_ref), custom_call_target="tpu_custom_call" | custom-call | flops 4982833152 | bytes 6488064 | tf_op jit(solution)/shard_map/hidden/pallas_call | solution.py:454
  216.6 11.3 %hidden.5.lo_ref = bf16[1584,768]{1,0:T(8,128)(2,1)} custom-call(bf16[1584,2048]{1,0:T(8,128)(2,1)} %all-gather.4.cloned.1.call-done.w_ref, bf16[768,2048]{1,0:T(8,128)(2,1)} %get-tuple-element.458.n2_ref.no_ref, bf16[768,2048]{1,0:T(8,128)(2,1)} %get-tuple-element.459.df_ref.do_ref), custom_call_target="tpu_custom_call" | custom-call | flops 4982833152 | bytes 6488064 | tf_op jit(solution)/shard_map/hidden/pallas_call | solution.py:454
  227.9 15.6 %feed_grads.2 = bf16[1584,2048]{1,0:T(8,128)(2,1)} custom-call(bf16[1584,768]{1,0:T(8,128)(2,1)S(1)} %hidden.4.lm_ref, bf16[1584,768]{1,0:T(8,128)(2,1)} %hidden.5.lo_ref, bf16[768,2048]{1,0:T(8,128)(2,1)} %get-tuple-element.456.n2_ref.nm_ref, bf16[768,2048]{1,0:T(8,128)(2,1)} %get-tuple-element.458.n2_ref.no_ref, ...), custom_call_target="tpu_custom_call" | custom-call | flops 9965666304 | bytes 6488064 | tf_op jit(solution)/shard_map/feed_grads/pallas_call | solution.py:487
  245.2 7.9 %fusion.37.rest_0_ = bf16[768,2048]{1,0:T(8,128)(2,1)} fusion(bf16[1584,2048]{1,0:T(8,128)(2,1)} %all-gather.4.cloned.1.call-done.w_ref, bf16[1584,768]{1,0:T(8,128)(2,1)S(1)} %copy-done.68), kind=kOutput, calls=%fused_computation.130 | convolution fusion | flops 3323461632 | bytes 9093120 | tf_op jit(solution)/shard_map/dot_general | solution.py:21
  253.2 5.8 %hidden.6.lm_ref = bf16[528,768]{1,0:T(8,128)(2,1)S(1)} custom-call(bf16[528,2048]{1,0:T(8,128)(2,1)} %all-gather.8.cloned.1.call-done.w_ref, bf16[768,2048]{1,0:T(8,128)(2,1)} %get-tuple-element.456.n2_ref.nm_ref, bf16[768,2048]{1,0:T(8,128)(2,1)} %get-tuple-element.457.df_ref.dm_ref, bf16[768,2048]{1,0:T(8,128)(2,1)} %fusion.37.rest_0_), custom_call_target="tpu_custom_call" | custom-call | flops 1660944384 | bytes 2162688 | tf_op jit(solution)/shard_map/hidden/pallas_call | solution.py:454
  259.0 5.8 %hidden.7.lo_ref = bf16[528,768]{1,0:T(8,128)(2,1)} custom-call(bf16[528,2048]{1,0:T(8,128)(2,1)S(1)} %copy-done.10, bf16[768,2048]{1,0:T(8,128)(2,1)} %get-tuple-element.458.n2_ref.no_ref, bf16[768,2048]{1,0:T(8,128)(2,1)} %get-tuple-element.459.df_ref.do_ref, bf16[768,2048]{1,0:T(8,128)(2,1)} %fusion.37.rest_0_), custom_call_target="tpu_custom_call" | custom-call | flops 1660944384 | bytes 2162688 | tf_op jit(solution)/shard_map/hidden/pallas_call | solution.py:454
  264.7 10.6 %feed_grads.3 = bf16[528,2048]{1,0:T(8,128)(2,1)} custom-call(bf16[528,768]{1,0:T(8,128)(2,1)S(1)} %hidden.6.lm_ref, bf16[528,768]{1,0:T(8,128)(2,1)} %hidden.7.lo_ref, bf16[768,2048]{1,0:T(8,128)(2,1)} %get-tuple-element.456.n2_ref.nm_ref, bf16[768,2048]{1,0:T(8,128)(2,1)} %get-tuple-element.458.n2_ref.no_ref, ...), custom_call_target="tpu_custom_call" | custom-call | flops 3321888768 | bytes 2162688 | tf_op jit(solution)/shard_map/feed_grads/pallas_call | solution.py:487
  275.4 89.3 %conditional.8 = (f32[192,2048]{1,0:T(8,128)}, f32[1,2048]{1,0:T(1,128)S(1)}, bf16[768,2048]{1,0:T(8,128)(2,1)}, bf16[768,2048]{1,0:T(8,128)(2,1)}, bf16[192,204...) conditional(s32[]{:T(128)} %bitcast.69, () %tuple.87, ...), branch_computations={%region_8.9_spmd, %region_9.12_spmd} | conditional | flops 10807738368 | bytes 254764384 | solution.py:34
  275.8 4.5 add_convert_fusion.7
  281.1 4.4 fusion.3
  291.1 3.8 fusion.7
  300.9 8.2 %collective-permute-done.36 = bf16[192,2048]{1,0:T(8,128)(2,1)S(1)} collective-permute-done((bf16[192,2048]{1,0:T(8,128)(2,1)S(1)}, bf16[192,2048]{1,0:T(8,128)(2,1)S(1)}, u32[]{:S(2)}, u32[]{:S(2)}) %collective-permute-start.36) | collective-permute-done | bytes 786464 | tf_op jit(solution)/shard_map/cond/branch_1_fun/ppermute | solution.py:43
  312.9 7.5 %collective-permute-done.39 = bf16[96,2048]{1,0:T(8,128)(2,1)S(1)} collective-permute-done((bf16[96,2048]{1,0:T(8,128)(2,1)S(1)}, bf16[96,2048]{1,0:T(8,128)(2,1)S(1)}, u32[]{:S(2)}, u32[]{:S(2)}) %collective-permute-start.39) | collective-permute-done | bytes 393248 | tf_op jit(solution)/shard_map/cond/branch_1_fun/ppermute | solution.py:43
  323.2 3.5 multiply_convert_fusion.1
  330.9 8.0 %collective-permute-done.40.refs_1_ = bf16[96,2048]{1,0:T(8,128)(2,1)S(1)} collective-permute-done((bf16[96,2048]{1,0:T(8,128)(2,1)S(1)}, bf16[96,2048]{1,0:T(8,128)(2,1)S(1)}, u32[]{:S(2)}, u32[]{:S(2)}) %collective-permute-start.40) | collective-permute-done | bytes 393248 | tf_op jit(solution)/shard_map/cond/branch_1_fun/ppermute | solution.py:43
  345.6 3.0 collective-permute-done.41.refs_2_
  348.6 5.5 %collective-permute-done.42.refs_3_ = bf16[96,2048]{1,0:T(8,128)(2,1)S(1)} collective-permute-done((bf16[96,2048]{1,0:T(8,128)(2,1)S(1)}, bf16[96,2048]{1,0:T(8,128)(2,1)S(1)}, u32[]{:S(2)}, u32[]{:S(2)}) %collective-permute-start.42) | collective-permute-done | bytes 393248 | tf_op jit(solution)/shard_map/cond/branch_1_fun/ppermute | solution.py:51
  355.0 3.5 join.7
  358.6 3.7 convolution_convert_fusion.2
  364.8 85.8 %conditional.9 = (f32[192,2048]{1,0:T(8,128)}, bf16[656,2048]{1,0:T(8,128)(2,1)}, bf16[192,2048]{1,0:T(8,128)(2,1)}, bf16[192,2048]{1,0:T(8,128)(2,1)}, bf16[1056,512]{1,0:T(8,128)(2,1)}) conditional(s32[]{:T(128)} %bitcast.69, () %tuple.86, (bf16[656,2048]{1,0:T(8,128)(2,1)S(1)}, bf16[768,2048]{1,0:T(8,128)(2,1)}, s32[17]{0:T(128)S(1)}, ...), branch_computations={%region_13.0_spmd, %region_14.19_spmd} | conditional | flops 21800714240 | bytes 174490656 | solution.py:34
  366.6 3.8 convolution_convert_fusion.5.doo
  370.4 13.6 %attn_backward.1 = (bf16[768,256]{1,0:T(8,128)(2,1)}, bf16[768,256]{1,0:T(8,128)(2,1)}, f32[768,128]{1,0:T(8,128)}, f32[768,128]{1,0:T(8,128)}, bf16[768,128]{1,0:T(8,128)(2,1)}, /*index=5*/bf16[768,128]{1,0:T(8,128)(2,1)}) custom-call(s32[17]{0:T(128)S(1)} %get-tuple-element.267.starts_ref, bf16[768,256]{1,0:T(8,128)(2,1)} %get-tuple-element.268.qm, ...), custom_call_target="tpu_custom_call" | custom-call | flops 14495514624 | bytes 6291456 | tf_op jit(solution)/shard_map/cond/branch_1_fun/attn_backward/pallas_call | solution.py:415
  387.6 2.9 convolution_convert_fusion.3
  405.2 4.1 fusion.21
  409.3 3.0 fusion.23
  412.4 3.0 fusion.26
  416.2 3.3 fusion.60
  419.6 3.4 add_convert_fusion.12
  424.9 10.1 %collective-permute-done.53 = bf16[192,2048]{1,0:T(8,128)(2,1)S(1)} collective-permute-done((bf16[192,2048]{1,0:T(8,128)(2,1)S(1)}, bf16[192,2048]{1,0:T(8,128)(2,1)S(1)}, u32[]{:S(2)}, u32[]{:S(2)}) %collective-permute-start.53) | collective-permute-done | bytes 786464 | tf_op jit(solution)/shard_map/cond/branch_1_fun/ppermute | solution.py:43
  438.0 2.9 fusion.61
  440.8 2.9 fusion.27.rest_0_
  450.6 53.3 %conditional.10 = (bf16[192,2048]{1,0:T(8,128)(2,1)}, f32[512,2816]{1,0:T(8,128)}, bf16[1584,512]{1,0:T(8,128)(2,1)}, bf16[1056,512]{1,0:T(8,128)(2,1)}, bf16[52...) conditional(s32[]{:T(128)} %bitcast.69, () %tuple.85, ...), branch_computations={%region_21.22_spmd, %region_22.25_spmd} | conditional | flops 16746689 | bytes 76061856 | solution.py:34
  464.7 3.1 pad_maximum_fusion.6
  473.7 3.4 collective-permute-done.5.refs_6_
  477.1 3.3 add_convert_fusion.20
  481.8 6.9 %finish.3.rest_0_ = f32[512,2816]{1,0:T(8,128)} custom-call(s32[1]{0:T(128)} %get-tuple-element.321.c_ref, bf16[1584,512]{1,0:T(8,128)(2,1)S(1)} %copy-done.8, bf16[1584,512]{1,0:T(8,128)(2,1)} %collective-permute-done.2.refs_1_, bf16[1056,512]{1,0:T(8,128)(2,1)} %get-tuple-element.323.refs_2_, bf16[1056,512]{1,0:T(8,128)(2,1)} %collective-permute-done.3.refs_3_, ...), custom_call_target="tpu_custom_call" | custom-call | tf_op jit(solution)/shard_map/cond/branch_1_fun/finish/pallas_call | solution.py:569
  488.7 7.4 %collective-permute-done.7.v_ref = bf16[880,512]{1,0:T(8,128)(2,1)} collective-permute-done((bf16[880,512]{1,0:T(8,128)(2,1)}, bf16[880,512]{1,0:T(8,128)(2,1)}, u32[]{:S(2)}, u32[]{:S(2)}) %collective-permute-start.7) | collective-permute-done | bytes 901152 | tf_op jit(solution)/shard_map/cond/branch_1_fun/ppermute | solution.py:43
  500.6 3.3 maximum_select_fusion
  503.9 31.5 %conditional.11 = (f32[512,2816]{1,0:T(8,128)}, f32[2816,512]{1,0:T(8,128)}, f32[512,1024]{1,0:T(8,128)}, f32[512,256]{1,0:T(8,128)}, f32[512,256]{1,0:T(8,128)}...) conditional(s32[]{:T(128)} %bitcast.69, () %tuple.78, ...), branch_computations={%region_25.26_spmd, %region_26.27_spmd} | conditional | flops 7077889 | bytes 32063892 | solution.py:34
  506.1 5.8 %finish.5.rest_1_ = f32[2816,512]{1,0:T(8,128)} custom-call(s32[1]{0:T(128)} %get-tuple-element.330.c_ref, bf16[1584,512]{1,0:T(8,128)(2,1)} %get-tuple-element.331.refs_0_, bf16[1584,512]{1,0:T(8,128)(2,1)} %get-tuple-element.332.refs_1_, bf16[880,512]{1,0:T(8,128)(2,1)} %get-tuple-element.337.refs_6_.refs_2_, ...), custom_call_target="tpu_custom_call" | custom-call | tf_op jit(solution)/shard_map/cond/branch_1_fun/finish/pallas_call | solution.py:569
  511.9 6.9 %finish.4.rest_0_ = f32[512,2816]{1,0:T(8,128)} custom-call(s32[1]{0:T(128)} %get-tuple-element.330.c_ref, bf16[1584,512]{1,0:T(8,128)(2,1)S(1)} %copy-done.9, bf16[1584,512]{1,0:T(8,128)(2,1)} %get-tuple-element.332.refs_1_, bf16[1056,512]{1,0:T(8,128)(2,1)} %get-tuple-element.333.refs_2_, bf16[1056,512]{1,0:T(8,128)(2,1)} %get-tuple-element.334.refs_3_, ...), custom_call_target="tpu_custom_call" | custom-call | tf_op jit(solution)/shard_map/cond/branch_1_fun/finish/pallas_call | solution.py:569
  528.1 4.5 finish_attn.1
  (387 shorter events, 182.8 us)
Async XLA Ops:
  7.2 62.3 %all-gather.6.cloned.1.call-start = ((), (), s32[]{:S(2)}) async-start(), calls=%async_computation.4 | async-start | bytes 3358720 | tf_op jit(solution)/shard_map/all_gather | solution.py:166
  10.7 196.3 %all-gather.4.cloned.1.call-start = ((), (), s32[]{:S(2)}) async-start(), calls=%async_computation.3 | async-start | bytes 8110080 | tf_op jit(solution)/shard_map/all_gather | solution.py:166
  14.1 28.7 %collective-permute-start.59 = (bf16[96,2048]{1,0:T(8,128)(2,1)}, bf16[96,2048]{1,0:T(8,128)(2,1)}, u32[]{:S(2)}, u32[]{:S(2)}) collective-permute-start(bf16[96,2048]{1,0:T(8,128)(2,1)} %get-tuple-element.202.refs_0_), channel_id=1, source_target_pairs={{0,4},{2,6},{4,0},{6,2},{1,5},{3,7},{5,1},{7,3},{8,12},{10,14},{12... | collective-permute-start | bytes 1179656 | tf_op jit(solution)/shard_map/cond/branch_1_fun/ppermute | solution.py:43
  17.0 25.8 %collective-permute-start.61 = (bf16[96,2048]{1,0:T(8,128)(2,1)}, bf16[96,2048]{1,0:T(8,128)(2,1)}, u32[]{:S(2)}, u32[]{:S(2)}) collective-permute-start(bf16[96,2048]{1,0:T(8,128)(2,1)} %get-tuple-element.202.refs_0_), channel_id=1, source_target_pairs={{0,1},{1,0},{2,3},{3,2},{4,5},{5,4},{6,7},{7,6},{8,9},{9,8},{10,11... | collective-permute-start | bytes 1179656 | tf_op jit(solution)/shard_map/cond/branch_1_fun/ppermute | solution.py:51
  18.5 24.3 %collective-permute-start.60 = (bf16[96,2048]{1,0:T(8,128)(2,1)}, bf16[96,2048]{1,0:T(8,128)(2,1)}, u32[]{:S(2)}, u32[]{:S(2)}) collective-permute-start(bf16[96,2048]{1,0:T(8,128)(2,1)} %get-tuple-element.206.refs_4_), channel_id=1, source_target_pairs={{0,1},{1,0},{2,3},{3,2},{4,5},{5,4},{6,7},{7,6},{8,9},{9,8},{10,11... | collective-permute-start | bytes 1179656 | tf_op jit(solution)/shard_map/cond/branch_1_fun/ppermute | solution.py:51
  19.0 23.8 %collective-permute-start.62 = (bf16[96,2048]{1,0:T(8,128)(2,1)}, bf16[96,2048]{1,0:T(8,128)(2,1)}, u32[]{:S(2)}, u32[]{:S(2)}) collective-permute-start(bf16[96,2048]{1,0:T(8,128)(2,1)} %get-tuple-element.206.refs_4_), channel_id=1, source_target_pairs={{0,4},{2,6},{4,0},{6,2},{1,5},{3,7},{5,1},{7,3},{8,12},{10,14},{12... | collective-permute-start | bytes 1179656 | tf_op jit(solution)/shard_map/cond/branch_1_fun/ppermute | solution.py:43
  42.8 10.3 %collective-permute-start.63 = (bf16[96,2048]{1,0:T(8,128)(2,1)}, bf16[96,2048]{1,0:T(8,128)(2,1)S(1)}, u32[]{:S(2)}, u32[]{:S(2)}) collective-permute-start(bf16[96,2048]{1,0:T(8,128)(2,1)} %collective-permute-done.59.refs_1_), channel_id=1, source_target_pairs={{0,1},{1,0},{2,3},{3,2},{4,5},{5,4},{6,7},{7,6},{8,9},{9,8},{10,11... | collective-permute-start | bytes 1179656 | tf_op jit(solution)/shard_map/cond/branch_1_fun/ppermute | solution.py:51
  44.9 9.7 %collective-permute-start.64 = (bf16[96,2048]{1,0:T(8,128)(2,1)}, bf16[96,2048]{1,0:T(8,128)(2,1)S(1)}, u32[]{:S(2)}, u32[]{:S(2)}) collective-permute-start(bf16[96,2048]{1,0:T(8,128)(2,1)} %collective-permute-done.60.refs_5_), channel_id=1, source_target_pairs={{0,4},{2,6},{4,0},{6,2},{1,5},{3,7},{5,1},{7,3},{8,12},{10,14},{12... | collective-permute-start | bytes 1179656 | tf_op jit(solution)/shard_map/cond/branch_1_fun/ppermute | solution.py:43
  58.9 6.1 %collective-permute-start.65 = (bf16[768,2048]{1,0:T(8,128)(2,1)}, bf16[768,2048]{1,0:T(8,128)(2,1)}, u32[]{:S(2)}, u32[]{:S(2)}) collective-permute-start(bf16[768,2048]{1,0:T(8,128)(2,1)} %join.4), channel_id=1, source_target_pairs={{0,2},{2,0},{4,6},{6,4},{1,3},{3,1},{5,7},{7,5},{8,10},{10,8},{12,... | collective-permute-start | bytes 9437192 | tf_op jit(solution)/shard_map/cond/branch_1_fun/ppermute | solution.py:47
  67.3 185.9 %all-gather.8.cloned.1.call-start = ((), (), s32[]{:S(2)}) async-start(), calls=%async_computation.6 | async-start | bytes 2703360 | tf_op jit(solution)/shard_map/all_gather | solution.py:166
  69.5 295.3 %reduce-scatter.4.cloned.1.call-start = ((), (), s32[]{:S(2)}) async-start(), calls=%async_computation.5 | async-start | bytes 8110080 | tf_op jit(solution)/shard_map/reduce_scatter | solution.py:170
  82.7 17.8 %collective-permute-start.14 = (bf16[96,2048]{1,0:T(8,128)(2,1)S(1)}, bf16[96,2048]{1,0:T(8,128)(2,1)}, u32[]{:S(2)}, u32[]{:S(2)}) collective-permute-start(bf16[96,2048]{1,0:T(8,128)(2,1)S(1)} %get-tuple-element.233.refs_0_), channel_id=1, source_target_pairs={{0,4},{2,6},{4,0},{6,2},{1,5},{3,7},{5,1},{7,3},{8,12},{10,14},{12... | collective-permute-start | bytes 1179656 | tf_op jit(solution)/shard_map/cond/branch_1_fun/ppermute | solution.py:43
  84.2 19.4 %collective-permute-start.16 = (bf16[96,2048]{1,0:T(8,128)(2,1)S(1)}, bf16[96,2048]{1,0:T(8,128)(2,1)}, u32[]{:S(2)}, u32[]{:S(2)}) collective-permute-start(bf16[96,2048]{1,0:T(8,128)(2,1)S(1)} %get-tuple-element.233.refs_0_), channel_id=1, source_target_pairs={{0,1},{1,0},{2,3},{3,2},{4,5},{5,4},{6,7},{7,6},{8,9},{9,8},{10,11... | collective-permute-start | bytes 1179656 | tf_op jit(solution)/shard_map/cond/branch_1_fun/ppermute | solution.py:51
  85.3 18.3 %collective-permute-start.15 = (bf16[96,2048]{1,0:T(8,128)(2,1)S(1)}, bf16[96,2048]{1,0:T(8,128)(2,1)}, u32[]{:S(2)}, u32[]{:S(2)}) collective-permute-start(bf16[96,2048]{1,0:T(8,128)(2,1)S(1)} %get-tuple-element.237.refs_4_), channel_id=1, source_target_pairs={{0,1},{1,0},{2,3},{3,2},{4,5},{5,4},{6,7},{7,6},{8,9},{9,8},{10,11... | collective-permute-start | bytes 1179656 | tf_op jit(solution)/shard_map/cond/branch_1_fun/ppermute | solution.py:51
  86.2 17.4 %collective-permute-start.17 = (bf16[96,2048]{1,0:T(8,128)(2,1)S(1)}, bf16[96,2048]{1,0:T(8,128)(2,1)}, u32[]{:S(2)}, u32[]{:S(2)}) collective-permute-start(bf16[96,2048]{1,0:T(8,128)(2,1)S(1)} %get-tuple-element.237.refs_4_), channel_id=1, source_target_pairs={{0,4},{2,6},{4,0},{6,2},{1,5},{3,7},{5,1},{7,3},{8,12},{10,14},{12... | collective-permute-start | bytes 1179656 | tf_op jit(solution)/shard_map/cond/branch_1_fun/ppermute | solution.py:43
  94.9 10.1 %collective-permute-start.18 = (bf16[768,128]{1,0:T(8,128)(2,1)}, bf16[768,128]{1,0:T(8,128)(2,1)}, u32[]{:S(2)}, u32[]{:S(2)}) collective-permute-start(bf16[768,128]{1,0:T(8,128)(2,1)} %get-tuple-element.697.ko), channel_id=1, source_target_pairs={{0,2},{2,0},{4,6},{6,4},{1,3},{3,1},{5,7},{7,5},{8,10},{10,8},{12,... | collective-permute-start | bytes 589832 | tf_op jit(solution)/shard_map/cond/branch_1_fun/ppermute | solution.py:47
  103.6 15.2 %collective-permute-start.20 = (bf16[96,2048]{1,0:T(8,128)(2,1)}, bf16[96,2048]{1,0:T(8,128)(2,1)}, u32[]{:S(2)}, u32[]{:S(2)}) collective-permute-start(bf16[96,2048]{1,0:T(8,128)(2,1)} %collective-permute-done.14.refs_1_), channel_id=1, source_target_pairs={{0,1},{1,0},{2,3},{3,2},{4,5},{5,4},{6,7},{7,6},{8,9},{9,8},{10,11... | collective-permute-start | bytes 1179656 | tf_op jit(solution)/shard_map/cond/branch_1_fun/ppermute | solution.py:51
  104.4 14.4 %collective-permute-start.21 = (bf16[96,2048]{1,0:T(8,128)(2,1)}, bf16[96,2048]{1,0:T(8,128)(2,1)}, u32[]{:S(2)}, u32[]{:S(2)}) collective-permute-start(bf16[96,2048]{1,0:T(8,128)(2,1)} %collective-permute-done.15.refs_5_), channel_id=1, source_target_pairs={{0,4},{2,6},{4,0},{6,2},{1,5},{3,7},{5,1},{7,3},{8,12},{10,14},{12... | collective-permute-start | bytes 1179656 | tf_op jit(solution)/shard_map/cond/branch_1_fun/ppermute | solution.py:43
  129.7 19.9 %collective-permute-start.24 = (bf16[192,2048]{1,0:T(8,128)(2,1)}, bf16[192,2048]{1,0:T(8,128)(2,1)}, u32[]{:S(2)}, u32[]{:S(2)}) collective-permute-start(bf16[192,2048]{1,0:T(8,128)(2,1)} %bitcast.34), channel_id=1, source_target_pairs={{0,4},{2,6},{4,0},{6,2},{1,5},{3,7},{5,1},{7,3},{8,12},{10,14},{12... | collective-permute-start | bytes 2359304 | tf_op jit(solution)/shard_map/cond/branch_1_fun/ppermute | solution.py:43
  131.2 19.6 %collective-permute-start.25 = (bf16[192,2048]{1,0:T(8,128)(2,1)}, bf16[192,2048]{1,0:T(8,128)(2,1)}, u32[]{:S(2)}, u32[]{:S(2)}) collective-permute-start(bf16[192,2048]{1,0:T(8,128)(2,1)} %bitcast.35), channel_id=1, source_target_pairs={{0,1},{1,0},{2,3},{3,2},{4,5},{5,4},{6,7},{7,6},{8,9},{9,8},{10,11... | collective-permute-start | bytes 2359304 | tf_op jit(solution)/shard_map/cond/branch_1_fun/ppermute | solution.py:51
  152.3 10.1 %collective-permute-start.27 = (bf16[96,2048]{1,0:T(8,128)(2,1)S(1)}, bf16[96,2048]{1,0:T(8,128)(2,1)S(1)}, u32[]{:S(2)}, u32[]{:S(2)}) collective-permute-start(bf16[96,2048]{1,0:T(8,128)(2,1)S(1)} %slice.276), channel_id=1, source_target_pairs={{0,4},{2,6},{4,0},{6,2},{1,5},{3,7},{5,1},{7,3},{8,12},{10,14},{12... | collective-permute-start | bytes 1179656 | tf_op jit(solution)/shard_map/cond/branch_1_fun/ppermute | solution.py:43
  154.3 9.8 %collective-permute-start.26 = (bf16[96,2048]{1,0:T(8,128)(2,1)S(1)}, bf16[96,2048]{1,0:T(8,128)(2,1)S(1)}, u32[]{:S(2)}, u32[]{:S(2)}) collective-permute-start(bf16[96,2048]{1,0:T(8,128)(2,1)S(1)} %slice.274), channel_id=1, source_target_pairs={{0,1},{1,0},{2,3},{3,2},{4,5},{5,4},{6,7},{7,6},{8,9},{9,8},{10,11... | collective-permute-start | bytes 1179656 | tf_op jit(solution)/shard_map/cond/branch_1_fun/ppermute | solution.py:51
  168.6 12.1 %collective-permute-start.28 = (bf16[96,2048]{1,0:T(8,128)(2,1)S(1)}, bf16[96,2048]{1,0:T(8,128)(2,1)S(1)}, u32[]{:S(2)}, u32[]{:S(2)}) collective-permute-start(bf16[96,2048]{1,0:T(8,128)(2,1)S(1)} %get-tuple-element.614.refs_0_), channel_id=1, source_target_pairs={{0,4},{2,6},{4,0},{6,2},{1,5},{3,7},{5,1},{7,3},{8,12},{10,14},{12... | collective-permute-start | bytes 1179656 | tf_op jit(solution)/shard_map/cond/branch_1_fun/ppermute | solution.py:43
  170.1 12.1 %collective-permute-start.31 = (bf16[96,2048]{1,0:T(8,128)(2,1)S(1)}, bf16[96,2048]{1,0:T(8,128)(2,1)S(1)}, u32[]{:S(2)}, u32[]{:S(2)}) collective-permute-start(bf16[96,2048]{1,0:T(8,128)(2,1)S(1)} %get-tuple-element.613.refs_4_), channel_id=1, source_target_pairs={{0,1},{1,0},{2,3},{3,2},{4,5},{5,4},{6,7},{7,6},{8,9},{9,8},{10,11... | collective-permute-start | bytes 1179656 | tf_op jit(solution)/shard_map/cond/branch_1_fun/ppermute | solution.py:51
  171.3 19.2 %collective-permute-start.29 = (bf16[96,2048]{1,0:T(8,128)(2,1)S(1)}, bf16[96,2048]{1,0:T(8,128)(2,1)S(1)}, u32[]{:S(2)}, u32[]{:S(2)}) collective-permute-start(bf16[96,2048]{1,0:T(8,128)(2,1)S(1)} %get-tuple-element.614.refs_0_), channel_id=1, source_target_pairs={{0,1},{1,0},{2,3},{3,2},{4,5},{5,4},{6,7},{7,6},{8,9},{9,8},{10,11... | collective-permute-start | bytes 1179656 | tf_op jit(solution)/shard_map/cond/branch_1_fun/ppermute | solution.py:51
  172.1 18.5 %collective-permute-start.32 = (bf16[96,2048]{1,0:T(8,128)(2,1)S(1)}, bf16[96,2048]{1,0:T(8,128)(2,1)S(1)}, u32[]{:S(2)}, u32[]{:S(2)}) collective-permute-start(bf16[96,2048]{1,0:T(8,128)(2,1)S(1)} %get-tuple-element.613.refs_4_), channel_id=1, source_target_pairs={{0,4},{2,6},{4,0},{6,2},{1,5},{3,7},{5,1},{7,3},{8,12},{10,14},{12... | collective-permute-start | bytes 1179656 | tf_op jit(solution)/shard_map/cond/branch_1_fun/ppermute | solution.py:43
  180.8 14.8 %collective-permute-start.30 = (bf16[96,2048]{1,0:T(8,128)(2,1)S(1)}, bf16[96,2048]{1,0:T(8,128)(2,1)S(1)}, u32[]{:S(2)}, u32[]{:S(2)}) collective-permute-start(bf16[96,2048]{1,0:T(8,128)(2,1)S(1)} %collective-permute-done.28.refs_1_), channel_id=1, source_target_pairs={{0,1},{1,0},{2,3},{3,2},{4,5},{5,4},{6,7},{7,6},{8,9},{9,8},{10,11... | collective-permute-start | bytes 1179656 | tf_op jit(solution)/shard_map/cond/branch_1_fun/ppermute | solution.py:51
  182.2 13.4 %collective-permute-start.33 = (bf16[96,2048]{1,0:T(8,128)(2,1)S(1)}, bf16[96,2048]{1,0:T(8,128)(2,1)S(1)}, u32[]{:S(2)}, u32[]{:S(2)}) collective-permute-start(bf16[96,2048]{1,0:T(8,128)(2,1)S(1)} %collective-permute-done.31.refs_5_), channel_id=1, source_target_pairs={{0,4},{2,6},{4,0},{6,2},{1,5},{3,7},{5,1},{7,3},{8,12},{10,14},{12... | collective-permute-start | bytes 1179656 | tf_op jit(solution)/shard_map/cond/branch_1_fun/ppermute | solution.py:43
  183.4 17.4 %collective-permute-start.23 = (bf16[768,2048]{1,0:T(8,128)(2,1)}, bf16[768,2048]{1,0:T(8,128)(2,1)}, u32[]{:S(2)}, u32[]{:S(2)}) collective-permute-start(bf16[768,2048]{1,0:T(8,128)(2,1)} %join.5), channel_id=1, source_target_pairs={{0,2},{2,0},{4,6},{6,4},{1,3},{3,1},{5,7},{7,5},{8,10},{10,8},{12,... | collective-permute-start | bytes 9437192 | tf_op jit(solution)/shard_map/cond/branch_1_fun/ppermute | solution.py:47
  243.6 207.0 %reduce-scatter.6.cloned.1.call-start = ((), (), s32[]{:S(2)}) async-start(), calls=%async_computation.7 | async-start | bytes 2703360 | tf_op jit(solution)/shard_map/reduce_scatter | solution.py:170
  275.3 228.6 %reduce-scatter.8.cloned.1.call-start = ((), (), s32[]{:S(2)}) async-start(), calls=%async_computation.8 | async-start | bytes 3358720 | tf_op jit(solution)/shard_map/reduce_scatter | solution.py:170
  280.3 7.1 %collective-permute-start.35 = (bf16[768,2048]{1,0:T(8,128)(2,1)S(1)}, bf16[768,2048]{1,0:T(8,128)(2,1)S(1)}, u32[]{:S(2)}, u32[]{:S(2)}) collective-permute-start(bf16[768,2048]{1,0:T(8,128)(2,1)S(1)} %add_convert_fusion.7), channel_id=1, source_target_pairs={{0,2},{2,0},{4,6},{6,4},{1,3},{3,1},{5,7},{7,5},{8,10},{10,8},{12,... | collective-permute-start | bytes 9437192 | tf_op jit(solution)/shard_map/cond/branch_1_fun/ppermute | solution.py:47
  289.5 19.6 %collective-permute-start.36 = (bf16[192,2048]{1,0:T(8,128)(2,1)S(1)}, bf16[192,2048]{1,0:T(8,128)(2,1)S(1)}, u32[]{:S(2)}, u32[]{:S(2)}) collective-permute-start(bf16[192,2048]{1,0:T(8,128)(2,1)S(1)} %bitcast.144), channel_id=1, source_target_pairs={{0,4},{2,6},{4,0},{6,2},{1,5},{3,7},{5,1},{7,3},{8,12},{10,14},{12... | collective-permute-start | bytes 2359304 | tf_op jit(solution)/shard_map/cond/branch_1_fun/ppermute | solution.py:43
  290.0 19.6 %collective-permute-start.37 = (bf16[192,2048]{1,0:T(8,128)(2,1)S(1)}, bf16[192,2048]{1,0:T(8,128)(2,1)S(1)}, u32[]{:S(2)}, u32[]{:S(2)}) collective-permute-start(bf16[192,2048]{1,0:T(8,128)(2,1)S(1)} %bitcast.145), channel_id=1, source_target_pairs={{0,1},{1,0},{2,3},{3,2},{4,5},{5,4},{6,7},{7,6},{8,9},{9,8},{10,11... | collective-permute-start | bytes 2359304 | tf_op jit(solution)/shard_map/cond/branch_1_fun/ppermute | solution.py:51
  297.1 43.9 %collective-permute-start.46 = (bf16[768,2048]{1,0:T(8,128)(2,1)S(1)}, bf16[768,2048]{1,0:T(8,128)(2,1)S(1)}, u32[]{:S(2)}, u32[]{:S(2)}) collective-permute-start(bf16[768,2048]{1,0:T(8,128)(2,1)S(1)} %add_convert_fusion.5), channel_id=1, source_target_pairs={{0,2},{2,0},{4,6},{6,4},{1,3},{3,1},{5,7},{7,5},{8,10},{10,8},{12,... | collective-permute-start | bytes 9437192 | tf_op jit(solution)/shard_map/cond/branch_1_fun/ppermute | solution.py:47
  309.9 10.5 %collective-permute-start.39 = (bf16[96,2048]{1,0:T(8,128)(2,1)S(1)}, bf16[96,2048]{1,0:T(8,128)(2,1)S(1)}, u32[]{:S(2)}, u32[]{:S(2)}) collective-permute-start(bf16[96,2048]{1,0:T(8,128)(2,1)S(1)} %slice.288), channel_id=1, source_target_pairs={{0,4},{2,6},{4,0},{6,2},{1,5},{3,7},{5,1},{7,3},{8,12},{10,14},{12... | collective-permute-start | bytes 1179656 | tf_op jit(solution)/shard_map/cond/branch_1_fun/ppermute | solution.py:43
  311.5 9.8 %collective-permute-start.38 = (bf16[96,2048]{1,0:T(8,128)(2,1)S(1)}, bf16[96,2048]{1,0:T(8,128)(2,1)S(1)}, u32[]{:S(2)}, u32[]{:S(2)}) collective-permute-start(bf16[96,2048]{1,0:T(8,128)(2,1)S(1)} %slice.286), channel_id=1, source_target_pairs={{0,1},{1,0},{2,3},{3,2},{4,5},{5,4},{6,7},{7,6},{8,9},{9,8},{10,11... | collective-permute-start | bytes 1179656 | tf_op jit(solution)/shard_map/cond/branch_1_fun/ppermute | solution.py:51
  326.8 12.1 %collective-permute-start.40 = (bf16[96,2048]{1,0:T(8,128)(2,1)S(1)}, bf16[96,2048]{1,0:T(8,128)(2,1)S(1)}, u32[]{:S(2)}, u32[]{:S(2)}) collective-permute-start(bf16[96,2048]{1,0:T(8,128)(2,1)S(1)} %get-tuple-element.636.refs_0_), channel_id=1, source_target_pairs={{0,4},{2,6},{4,0},{6,2},{1,5},{3,7},{5,1},{7,3},{8,12},{10,14},{12... | collective-permute-start | bytes 1179656 | tf_op jit(solution)/shard_map/cond/branch_1_fun/ppermute | solution.py:43
  328.1 12.2 %collective-permute-start.43 = (bf16[96,2048]{1,0:T(8,128)(2,1)S(1)}, bf16[96,2048]{1,0:T(8,128)(2,1)S(1)}, u32[]{:S(2)}, u32[]{:S(2)}) collective-permute-start(bf16[96,2048]{1,0:T(8,128)(2,1)S(1)} %get-tuple-element.635.refs_4_), channel_id=1, source_target_pairs={{0,1},{1,0},{2,3},{3,2},{4,5},{5,4},{6,7},{7,6},{8,9},{9,8},{10,11... | collective-permute-start | bytes 1179656 | tf_op jit(solution)/shard_map/cond/branch_1_fun/ppermute | solution.py:51
  329.0 19.6 %collective-permute-start.41 = (bf16[96,2048]{1,0:T(8,128)(2,1)S(1)}, bf16[96,2048]{1,0:T(8,128)(2,1)S(1)}, u32[]{:S(2)}, u32[]{:S(2)}) collective-permute-start(bf16[96,2048]{1,0:T(8,128)(2,1)S(1)} %get-tuple-element.636.refs_0_), channel_id=1, source_target_pairs={{0,1},{1,0},{2,3},{3,2},{4,5},{5,4},{6,7},{7,6},{8,9},{9,8},{10,11... | collective-permute-start | bytes 1179656 | tf_op jit(solution)/shard_map/cond/branch_1_fun/ppermute | solution.py:51
  330.1 18.5 %collective-permute-start.44 = (bf16[96,2048]{1,0:T(8,128)(2,1)S(1)}, bf16[96,2048]{1,0:T(8,128)(2,1)S(1)}, u32[]{:S(2)}, u32[]{:S(2)}) collective-permute-start(bf16[96,2048]{1,0:T(8,128)(2,1)S(1)} %get-tuple-element.635.refs_4_), channel_id=1, source_target_pairs={{0,4},{2,6},{4,0},{6,2},{1,5},{3,7},{5,1},{7,3},{8,12},{10,14},{12... | collective-permute-start | bytes 1179656 | tf_op jit(solution)/shard_map/cond/branch_1_fun/ppermute | solution.py:43
  338.9 15.2 %collective-permute-start.42 = (bf16[96,2048]{1,0:T(8,128)(2,1)S(1)}, bf16[96,2048]{1,0:T(8,128)(2,1)S(1)}, u32[]{:S(2)}, u32[]{:S(2)}) collective-permute-start(bf16[96,2048]{1,0:T(8,128)(2,1)S(1)} %collective-permute-done.40.refs_1_), channel_id=1, source_target_pairs={{0,1},{1,0},{2,3},{3,2},{4,5},{5,4},{6,7},{7,6},{8,9},{9,8},{10,11... | collective-permute-start | bytes 1179656 | tf_op jit(solution)/shard_map/cond/branch_1_fun/ppermute | solution.py:51
  340.3 13.8 %collective-permute-start.45 = (bf16[96,2048]{1,0:T(8,128)(2,1)S(1)}, bf16[96,2048]{1,0:T(8,128)(2,1)S(1)}, u32[]{:S(2)}, u32[]{:S(2)}) collective-permute-start(bf16[96,2048]{1,0:T(8,128)(2,1)S(1)} %collective-permute-done.43.refs_5_), channel_id=1, source_target_pairs={{0,4},{2,6},{4,0},{6,2},{1,5},{3,7},{5,1},{7,3},{8,12},{10,14},{12... | collective-permute-start | bytes 1179656 | tf_op jit(solution)/shard_map/cond/branch_1_fun/ppermute | solution.py:43
  358.5 6.1 %collective-permute-start.47 = (bf16[768,2048]{1,0:T(8,128)(2,1)}, bf16[768,2048]{1,0:T(8,128)(2,1)}, u32[]{:S(2)}, u32[]{:S(2)}) collective-permute-start(bf16[768,2048]{1,0:T(8,128)(2,1)} %join.7), channel_id=1, source_target_pairs={{0,2},{2,0},{4,6},{6,4},{1,3},{3,1},{5,7},{7,5},{8,10},{10,8},{12,... | collective-permute-start | bytes 9437192 | tf_op jit(solution)/shard_map/cond/branch_1_fun/ppermute | solution.py:47
  364.8 20.0 %collective-permute-start.48 = (bf16[192,2048]{1,0:T(8,128)(2,1)}, bf16[192,2048]{1,0:T(8,128)(2,1)}, u32[]{:S(2)}, u32[]{:S(2)}) collective-permute-start(bf16[192,2048]{1,0:T(8,128)(2,1)} %get-tuple-element.290), channel_id=1, source_target_pairs={{0,4},{2,6},{4,0},{6,2},{1,5},{3,7},{5,1},{7,3},{8,12},{10,14},{12... | collective-permute-start | bytes 2359304 | tf_op jit(solution)/shard_map/cond/branch_1_fun/ppermute | solution.py:43
  365.2 19.6 %collective-permute-start.49 = (bf16[192,2048]{1,0:T(8,128)(2,1)}, bf16[192,2048]{1,0:T(8,128)(2,1)}, u32[]{:S(2)}, u32[]{:S(2)}) collective-permute-start(bf16[192,2048]{1,0:T(8,128)(2,1)} %get-tuple-element.291), channel_id=1, source_target_pairs={{0,1},{1,0},{2,3},{3,2},{4,5},{5,4},{6,7},{7,6},{8,9},{9,8},{10,11... | collective-permute-start | bytes 2359304 | tf_op jit(solution)/shard_map/cond/branch_1_fun/ppermute | solution.py:51
  390.5 10.8 %collective-permute-start.52 = (bf16[768,2048]{1,0:T(8,128)(2,1)S(1)}, bf16[768,2048]{1,0:T(8,128)(2,1)S(1)}, u32[]{:S(2)}, u32[]{:S(2)}) collective-permute-start(bf16[768,2048]{1,0:T(8,128)(2,1)S(1)} %convolution_convert_fusion.3), channel_id=1, source_target_pairs={{0,2},{2,0},{4,6},{6,4},{1,3},{3,1},{5,7},{7,5},{8,10},{10,8},{12,... | collective-permute-start | bytes 9437192 | tf_op jit(solution)/shard_map/cond/branch_1_fun/ppermute | solution.py:47
  391.7 58.6 %collective-permute-start.58 = (bf16[1056,512]{1,0:T(8,128)(2,1)}, bf16[1056,512]{1,0:T(8,128)(2,1)}, u32[]{:S(2)}, u32[]{:S(2)}) collective-permute-start(bf16[1056,512]{1,0:T(8,128)(2,1)} %slice.249), channel_id=1, source_target_pairs={{0,4},{2,6},{4,0},{6,2},{1,5},{3,7},{5,1},{7,3},{8,12},{10,14},{12... | collective-permute-start | bytes 3244040 | tf_op jit(solution)/shard_map/cond/branch_1_fun/ppermute | solution.py:43
  403.4 31.5 %collective-permute-start.53 = (bf16[192,2048]{1,0:T(8,128)(2,1)S(1)}, bf16[192,2048]{1,0:T(8,128)(2,1)S(1)}, u32[]{:S(2)}, u32[]{:S(2)}) collective-permute-start(bf16[192,2048]{1,0:T(8,128)(2,1)S(1)} %bitcast.142), channel_id=1, source_target_pairs={{0,4},{2,6},{4,0},{6,2},{1,5},{3,7},{5,1},{7,3},{8,12},{10,14},{12... | collective-permute-start | bytes 2359304 | tf_op jit(solution)/shard_map/cond/branch_1_fun/ppermute | solution.py:43
  403.8 31.1 %collective-permute-start.54 = (bf16[192,2048]{1,0:T(8,128)(2,1)S(1)}, bf16[192,2048]{1,0:T(8,128)(2,1)S(1)}, u32[]{:S(2)}, u32[]{:S(2)}) collective-permute-start(bf16[192,2048]{1,0:T(8,128)(2,1)S(1)} %bitcast.143), channel_id=1, source_target_pairs={{0,1},{1,0},{2,3},{3,2},{4,5},{5,4},{6,7},{7,6},{8,9},{9,8},{10,11... | collective-permute-start | bytes 2359304 | tf_op jit(solution)/shard_map/cond/branch_1_fun/ppermute | solution.py:51
  415.5 9.3 %collective-permute-start.57 = (bf16[16,2048]{1,0:T(8,128)(2,1)S(1)}, bf16[16,2048]{1,0:T(8,128)(2,1)S(1)}, u32[]{:S(2)}, u32[]{:S(2)}) collective-permute-start(bf16[16,2048]{1,0:T(8,128)(2,1)S(1)} %fusion.31), channel_id=1, source_target_pairs={{0,1},{1,0},{2,3},{3,2},{4,5},{5,4},{6,7},{7,6},{8,9},{9,8},{10,11... | collective-permute-start | bytes 196616 | tf_op jit(solution)/shard_map/cond/branch_1_fun/ppermute | solution.py:51
  435.3 10.6 %collective-permute-start.55 = (bf16[96,2048]{1,0:T(8,128)(2,1)S(1)}, bf16[96,2048]{1,0:T(8,128)(2,1)S(1)}, u32[]{:S(2)}, u32[]{:S(2)}) collective-permute-start(bf16[96,2048]{1,0:T(8,128)(2,1)S(1)} %slice.303), channel_id=1, source_target_pairs={{0,1},{1,0},{2,3},{3,2},{4,5},{5,4},{6,7},{7,6},{8,9},{9,8},{10,11... | collective-permute-start | bytes 1179656 | tf_op jit(solution)/shard_map/cond/branch_1_fun/ppermute | solution.py:51
  437.0 10.5 %collective-permute-start.56 = (bf16[96,2048]{1,0:T(8,128)(2,1)S(1)}, bf16[96,2048]{1,0:T(8,128)(2,1)}, u32[]{:S(2)}, u32[]{:S(2)}) collective-permute-start(bf16[96,2048]{1,0:T(8,128)(2,1)S(1)} %slice.304), channel_id=1, source_target_pairs={{0,4},{2,6},{4,0},{6,2},{1,5},{3,7},{5,1},{7,3},{8,12},{10,14},{12... | collective-permute-start | bytes 1179656 | tf_op jit(solution)/shard_map/cond/branch_1_fun/ppermute | solution.py:43
  451.8 10.7 %collective-permute-start.1 = (bf16[96,2048]{1,0:T(8,128)(2,1)S(1)}, bf16[96,2048]{1,0:T(8,128)(2,1)S(1)}, u32[]{:S(2)}, u32[]{:S(2)}) collective-permute-start(bf16[96,2048]{1,0:T(8,128)(2,1)S(1)} %slice.253), channel_id=1, source_target_pairs={{0,4},{2,6},{4,0},{6,2},{1,5},{3,7},{5,1},{7,3},{8,12},{10,14},{12... | collective-permute-start | bytes 1179656 | tf_op jit(solution)/shard_map/cond/branch_1_fun/ppermute | solution.py:43
  453.7 9.9 %collective-permute-start = (bf16[96,2048]{1,0:T(8,128)(2,1)S(1)}, bf16[96,2048]{1,0:T(8,128)(2,1)S(1)}, u32[]{:S(2)}, u32[]{:S(2)}) collective-permute-start(bf16[96,2048]{1,0:T(8,128)(2,1)S(1)} %slice.251), channel_id=1, source_target_pairs={{0,1},{1,0},{2,3},{3,2},{4,5},{5,4},{6,7},{7,6},{8,9},{9,8},{10,11... | collective-permute-start | bytes 1179656 | tf_op jit(solution)/shard_map/cond/branch_1_fun/ppermute | solution.py:51
  455.3 25.9 %collective-permute-start.2 = (bf16[1584,512]{1,0:T(8,128)(2,1)}, bf16[1584,512]{1,0:T(8,128)(2,1)}, u32[]{:S(2)}, u32[]{:S(2)}) collective-permute-start(bf16[1584,512]{1,0:T(8,128)(2,1)} %get-tuple-element.322.refs_0_), channel_id=1, source_target_pairs={{0,2},{2,0},{4,6},{6,4},{1,3},{3,1},{5,7},{7,5},{8,10},{10,8},{12,... | collective-permute-start | bytes 4866056 | tf_op jit(solution)/shard_map/cond/branch_1_fun/ppermute | solution.py:47
  455.3 25.9 %collective-permute-start.3 = (bf16[1056,512]{1,0:T(8,128)(2,1)}, bf16[1056,512]{1,0:T(8,128)(2,1)}, u32[]{:S(2)}, u32[]{:S(2)}) collective-permute-start(bf16[1056,512]{1,0:T(8,128)(2,1)} %get-tuple-element.323.refs_2_), channel_id=1, source_target_pairs={{0,2},{2,0},{4,6},{6,4},{1,3},{3,1},{5,7},{7,5},{8,10},{10,8},{12,... | collective-permute-start | bytes 3244040 | tf_op jit(solution)/shard_map/cond/branch_1_fun/ppermute | solution.py:47
  455.8 24.6 %collective-permute-start.4 = (bf16[528,512]{1,0:T(8,128)(2,1)}, bf16[528,512]{1,0:T(8,128)(2,1)}, u32[]{:S(2)}, u32[]{:S(2)}) collective-permute-start(bf16[528,512]{1,0:T(8,128)(2,1)} %get-tuple-element.324.refs_4_), channel_id=1, source_target_pairs={{0,2},{2,0},{4,6},{6,4},{1,3},{3,1},{5,7},{7,5},{8,10},{10,8},{12,... | collective-permute-start | bytes 1622024 | tf_op jit(solution)/shard_map/cond/branch_1_fun/ppermute | solution.py:47
  469.5 7.6 %collective-permute-start.5 = (bf16[176,512]{1,0:T(8,128)(2,1)}, bf16[176,512]{1,0:T(8,128)(2,1)S(1)}, u32[]{:S(2)}, u32[]{:S(2)}) collective-permute-start(bf16[176,512]{1,0:T(8,128)(2,1)} %hold.4), channel_id=1, source_target_pairs={{0,4},{2,6},{4,0},{6,2},{1,5},{3,7},{5,1},{7,3},{8,12},{10,14},{12... | collective-permute-start | bytes 540680 | tf_op jit(solution)/shard_map/cond/branch_1_fun/ppermute | solution.py:43
  472.1 24.0 %collective-permute-start.7 = (bf16[880,512]{1,0:T(8,128)(2,1)}, bf16[880,512]{1,0:T(8,128)(2,1)}, u32[]{:S(2)}, u32[]{:S(2)}) collective-permute-start(bf16[880,512]{1,0:T(8,128)(2,1)} %hold.5), channel_id=1, source_target_pairs={{0,4},{2,6},{4,0},{6,2},{1,5},{3,7},{5,1},{7,3},{8,12},{10,14},{12... | collective-permute-start | bytes 2703368 | tf_op jit(solution)/shard_map/cond/branch_1_fun/ppermute | solution.py:43
  480.4 20.2 %collective-permute-start.9 = (bf16[192,2048]{1,0:T(8,128)(2,1)}, bf16[192,2048]{1,0:T(8,128)(2,1)S(1)}, u32[]{:S(2)}, u32[]{:S(2)}) collective-permute-start(bf16[192,2048]{1,0:T(8,128)(2,1)} %add_convert_fusion.20), channel_id=1, source_target_pairs={{0,1},{1,0},{2,3},{3,2},{4,5},{5,4},{6,7},{7,6},{8,9},{9,8},{10,11... | collective-permute-start | bytes 2359304 | tf_op jit(solution)/shard_map/cond/branch_1_fun/ppermute | solution.py:51
  503.9 17.0 %collective-permute-start.11 = (bf16[656,512]{1,0:T(8,128)(2,1)}, bf16[656,512]{1,0:T(8,128)(2,1)S(1)}, u32[]{:S(2)}, u32[]{:S(2)}) collective-permute-start(bf16[656,512]{1,0:T(8,128)(2,1)} %get-tuple-element.339.r0), channel_id=1, source_target_pairs={{0,4},{2,6},{4,0},{6,2},{1,5},{3,7},{5,1},{7,3},{8,12},{10,14},{12... | collective-permute-start | bytes 2015240 | tf_op jit(solution)/shard_map/cond/branch_1_fun/ppermute | solution.py:43
  504.6 19.2 %collective-permute-start.13 = (bf16[192,2048]{1,0:T(8,128)(2,1)}, bf16[192,2048]{1,0:T(8,128)(2,1)S(1)}, u32[]{:S(2)}, u32[]{:S(2)}) collective-permute-start(bf16[192,2048]{1,0:T(8,128)(2,1)} %get-tuple-element.346), channel_id=1, source_target_pairs={{0,1},{1,0},{2,3},{3,2},{4,5},{5,4},{6,7},{7,6},{8,9},{9,8},{10,11... | collective-permute-start | bytes 2359304 | tf_op jit(solution)/shard_map/cond/branch_1_fun/ppermute | solution.py:51
  506.1 21.2 %collective-permute-start.10 = (bf16[656,512]{1,0:T(8,128)(2,1)}, bf16[656,512]{1,0:T(8,128)(2,1)}, u32[]{:S(2)}, u32[]{:S(2)}) collective-permute-start(bf16[656,512]{1,0:T(8,128)(2,1)} %get-tuple-element.339.r0), channel_id=1, source_target_pairs={{0,2},{2,0},{4,6},{6,4},{1,3},{3,1},{5,7},{7,5},{8,10},{10,8},{12,... | collective-permute-start | bytes 2015240 | tf_op jit(solution)/shard_map/cond/branch_1_fun/ppermute | solution.py:47
  (77 other events, 453.5 us)
Sparse Core Ops, SparseCore 0:
  10.8 58.5 all-gather.5
  71.5 117.3 all-gather.3
  190.5 45.4 all-gather.7
  243.7 113.9 reduce-scatter.3
  360.0 45.4 reduce-scatter.5
  450.7 52.3 reduce-scatter.7
